TPU v7x, 256 devices: a whole 4x4x8 slice. The times are simulated.
256 devices in a mesh: group: 4 (over x), leaf: 64 (over z, y, core).
Axes of the slice: x: 4, y: 4, z: 8, core: 2. Of those that a mesh axis runs over, the one named last changes fastest.
Arguments:
- right_sides: float32 [16, 1048576], P(None, ('group', 'leaf')), may hold values from -6 to 6
- near_blocks: float32 [16384, 8, 4096], P(('group', 'leaf')), may hold values from -0.375 to 0.375
- near_source: int32 [16384, 8], P(('group', 'leaf')), may hold values from 0 to 16383, as said below
- near_count: int32 [16384], P(('group', 'leaf')), may hold values from 1 to 8
- basis: float32 [16384, 2048], P(('group', 'leaf')), may hold values from -0.75 to 0.75
- leaf_source: int32 [16384, 8], P(('group', 'leaf')), may hold values from 0 to 16383
- leaf_coupling: float32 [16384, 8, 1024], P(('group', 'leaf')), may hold values from -0.375 to 0.375
- leaf_transfer: float32 [16384, 1024], P(('group', 'leaf')), may hold values from -1 to 1
- cluster_source: int32 [1024, 8], P(('group', 'leaf')), may hold values from 0 to 255
- cluster_coupling: float32 [1024, 8, 1024], P(('group', 'leaf')), may hold values from -0.09375 to 0.09375
- cluster_transfer: float32 [1024, 1024], P(('group', 'leaf')), may hold values from -1 to 1
- group_coupling: float32 [4, 4, 1024], P('group'), may hold values from -0.0078125 to 0.0078125
Outputs:
- applied: float32 [16, 1048576], P(None, ('group', 'leaf'))
Inputs may be any that keep to these rules, and one draw needn't show every extreme that they name: near_source[t, j] and leaf_source[t, j] name a leaf held by the same device as t or by the device just before or after it in the order of devices.
All inputs are finite; a program needn't handle non-finite values.
Results may differ from a plain program's by a relative error of at most 0.0001.
Values sent between devices are 32-bit elements; how exact they have to be, the bound alone decides.
No kernel may reach another device: no remote copies, remote signals or barrier semaphores. Data moves between devices by JAX's collectives and lax.ppermute only.
A program may use at most 128 MiB of HBM per device.

v0:
```python
import jax
import jax.numpy as jnp
from jax import lax
from jax.sharding import PartitionSpec as P

LEAF = 64
K = 32
RHS = 16
FAR0 = 8
FAR1 = 8


highest_precision = lax.Precision.HIGHEST


def extended(value, sides, width):
    for axis, dim in sides:
        size, length = (lax.axis_size(axis), value.shape[dim])
        up = [(i, (i + 1) % size) for i in range(size - 1)]
        down = [(j, i) for i, j in up]
        last = lax.slice_in_dim(value, length - width, length, axis=dim)
        leading = lax.slice_in_dim(value, 0, width, axis=dim)
        before = lax.ppermute(last, axis, up)
        after = lax.ppermute(leading, axis, down)
        value = jnp.concatenate([before, value, after], axis=dim)
    return value


def per_device(
    right_sides,
    near_blocks,
    near_source,
    near_count,
    basis,
    leaf_source,
    leaf_coupling,
    leaf_transfer,
    cluster_source,
    cluster_coupling,
    cluster_transfer,
    group_coupling,
):
    leaves_here = near_blocks.shape[0]
    clusters_here = cluster_coupling.shape[0]
    ngroups = lax.axis_size("group")
    device = lax.axis_index(("group", "leaf"))
    blocks = right_sides.reshape(RHS, leaves_here, LEAF).transpose(1, 0, 2)
    bases = basis.reshape(leaves_here, K, LEAF)
    leaf_coef = jnp.einsum("tka,tra->tkr", bases, blocks, precision=highest_precision)
    coef_rows = leaf_coef.transpose(2, 0, 1).reshape(RHS, leaves_here * K)
    point_ext = extended(right_sides, ((("group", "leaf"), 1),), leaves_here * LEAF)
    coef_ext = extended(coef_rows, ((("group", "leaf"), 1),), leaves_here * K)
    window_start = (device - 1) * leaves_here
    near_local = near_source - window_start
    point_blocks = point_ext.reshape(RHS, 3 * leaves_here, LEAF).transpose(1, 0, 2)
    busiest = jnp.max(near_count)

    def near_step(slot_index, running):
        picked = jnp.take(point_blocks, near_local[:, slot_index], axis=0)
        slab = lax.dynamic_index_in_dim(near_blocks, slot_index, axis=1, keepdims=False).reshape(
            leaves_here, LEAF, LEAF
        )
        live = (near_count > slot_index).astype(jnp.float32)
        term = jnp.einsum("tab,trb->tra", slab, picked, precision=highest_precision)
        return running + term * live[:, None, None]

    near_total = lax.fori_loop(
        0, busiest, near_step, jnp.zeros((leaves_here, RHS, LEAF), jnp.float32)
    )
    coef_blocks = coef_ext.reshape(RHS, 3 * leaves_here, K)
    picked_coef = jnp.take(coef_blocks, leaf_source - window_start, axis=1)
    leaf_far = jnp.einsum(
        "tjkl,rtjl->tkr",
        leaf_coupling.reshape(leaves_here, FAR0, K, K),
        picked_coef,
        precision=highest_precision,
    )
    transfers = leaf_transfer.reshape(leaves_here, K, K)
    lifted = jnp.einsum("tkl,tlr->tkr", transfers, leaf_coef, precision=highest_precision)
    cluster_coef = lifted.reshape(clusters_here, leaves_here // clusters_here, K, RHS).sum(axis=1)
    cluster_rows = cluster_coef.reshape(clusters_here, K * RHS)
    couplings = cluster_coupling.reshape(clusters_here, FAR1, K, K)
    shard_rows = lax.all_gather(cluster_rows, "leaf", axis=0, tiled=True)
    onehot = (cluster_source[:, :, None] == jnp.arange(shard_rows.shape[0])[None, None, :]).astype(
        jnp.float32
    )
    selected = jnp.einsum("ujn,nm->ujm", onehot, shard_rows, precision=highest_precision)
    selected = selected.reshape(clusters_here, FAR1, K, RHS)
    cluster_far = jnp.einsum("ujkl,ujlr->ukr", couplings, selected, precision=highest_precision)
    upper = cluster_transfer.reshape(clusters_here, K, K)
    projected = jnp.einsum("ukl,ulr->ukr", upper, cluster_coef, precision=highest_precision)
    projected_sum = projected.sum(axis=0).reshape(1, K * RHS)
    group_sum = lax.psum(projected_sum, "leaf")
    all_groups = lax.all_gather(group_sum, "group", axis=0, tiled=True)
    group_field = jnp.einsum(
        "hkl,hlr->kr",
        group_coupling.reshape(ngroups, K, K),
        all_groups.reshape(ngroups, K, RHS),
        precision=highest_precision,
    )
    cluster_field = cluster_far + jnp.einsum(
        "ulk,lr->ukr", upper, group_field, precision=highest_precision
    )
    spread_cluster = jnp.repeat(cluster_field, leaves_here // clusters_here, axis=0)
    leaf_field = leaf_far + jnp.einsum(
        "tlk,tlr->tkr", transfers, spread_cluster, precision=highest_precision
    )
    total = near_total + jnp.einsum("tka,tkr->tra", bases, leaf_field, precision=highest_precision)
    return total.transpose(1, 0, 2).reshape(RHS, leaves_here * LEAF)


def solution(mesh):
    in_specs = (
        P(None, ("group", "leaf")),
        P(("group", "leaf"), None, None),
        P(("group", "leaf"), None),
        P(("group", "leaf")),
        P(("group", "leaf"), None),
        P(("group", "leaf"), None),
        P(("group", "leaf"), None, None),
        P(("group", "leaf"), None),
        P(("group", "leaf"), None),
        P(("group", "leaf"), None, None),
        P(("group", "leaf"), None),
        P("group", None, None),
    )
    out_specs = P(None, ("group", "leaf"))
    return jax.shard_map(
        per_device, mesh=mesh, in_specs=in_specs, out_specs=out_specs, check_vma=False
    )
```

profile of v0, /device:TPU:0, one launch (start us, length us, event | category | flops | bytes accessed | tf_op | source)
XLA Modules:
  0.0 376.4 jit_solution(737260132806493097)
XLA Ops:
  1.4 3.7 collective-permute-start
  18.9 60.3 %all-gather = f32[64,4,512]{2,1,0:T(4,128)S(1)} all-gather(f32[1,4,512]{2,1,0:T(4,128)S(1)} %reshape.105), channel_id=1, replica_groups=mesh['group'=4,'leaf'=64] {'leaf'}, dimensions={0}, use_global_device_ids=true | all-gather | bytes 532480 | tf_op jit(solution)/shard_map/all_gather | solution.py:83
  83.3 126.7 %psum.7 = f32[1,512]{1,0:T(1,128)S(1)} all-reduce(f32[1,512]{1,0:T(1,128)S(1)} %reshape.82), channel_id=1, replica_groups=mesh['group'=4,'leaf'=64] {'leaf'}, use_global_device_ids=true, to_apply=%region_4.5 | all-reduce | flops 512 | bytes 4096 | tf_op jit(solution)/shard_map/psum | solution.py:93
  209.9 11.2 %all-gather.1 = f32[4,1,512]{2,1,0:T(1,128)S(1)} all-gather(f32[1,1,512]{2,1,0:T(1,128)S(1)} %bitcast.75), channel_id=1, replica_groups=mesh['group'=4,'leaf'=64] {'group'}, dimensions={0}, use_global_device_ids=true | all-gather | bytes 10240 | tf_op jit(solution)/shard_map/all_gather | solution.py:94
  222.9 3.8 %copy.82 = f32[64,8,1024]{0,2,1:T(8,128)} copy(f32[64,8,1024]{2,1,0:T(8,128)} %param.20) | data formatting | bytes 4194304 | tf_op args[6]
  226.7 9.1 %copy.83 = f32[64,8,32,32]{3,2,1,0:T(8,128)} copy(f32[64,8,32,32]{0,3,2,1:T(8,128)} %bitcast.67) | data formatting | bytes 4194304 | tf_op jit(solution)/shard_map/reshape | solution.py:74
  244.6 10.6 %fusion.10 = f32[64,16,32]{2,1,0:T(8,128)S(1)} fusion(f32[64,8,32,32]{3,2,1,0:T(8,128)} %copy.83, f32[64,8,16,32]{3,2,1,0:T(8,128)} %bitcast.68, pred[64,8]{1,0:T(8,128)(4,1)S(1)} %copy.76), kind=kOutput, calls=%fused_computation.19 | convolution fusion | flops 100925440 | bytes 3277312 | tf_op jit(solution)/shard_map/tjkl,rtjl->tkr/dot_general | solution.py:72
  261.6 111.1 %while.10 = (s32[]{:T(128)}, f32[64,16,64]{2,1,0:T(8,128)}, s32[]{:T(128)}, s32[64,8]{0,1:T(8,128)S(1)}, f32[192,16,64]{2,1,0:T(8,128)}, /*index=5*/f32[64,8,409...) while((s32[]{:T(128)}, f32[64,16,64]{2,1,0:T(8,128)}, s32[]{:T(128)}, ...), condition=%wide.region_2.0_spmd, body=%wide.region_1.2_spmd.sunk | while | flops 50529796 | bytes 8656923 | solution.py:67
  262.4 4.4 %constant_dynamic-slice_fusion.2 = f32[64,1,4096]{2,1,0:T(1,128)S(1)} fusion(f32[64,8,4096]{2,1,0:T(8,128)} %get-tuple-element.170, s32[]{:T(128)S(6)} %select_n.43), kind=kLoop, calls=%fused_computation.11.clone.1 | loop fusion | bytes 2097156 | tf_op jit(solution)/shard_map/while/body/jit(dynamic_index_in_dim)/dynamic_slice | solution.py:60
  270.4 5.3 %fusion.45 = f32[64,16,64]{2,1,0:T(8,128)} fusion(f32[64,16,64]{2,1,0:T(8,128)} %get-tuple-element.156, f32[64,64,64]{2,1,0:T(8,128)S(1)} %reshape.124, f32[64,16,64]{2,1,0:T(8,128)S(1)} %gather_fusion, f32[64]{0:T(128)S(1)} %compare_convert_fusion.2, pred[64]{0:T(512)(128)(4,1)S(1)} %get-tuple-element.144), kind=kOutput, calls=%fused_computation.3.clone.1 | convolution fusion | flops 50528256 | bytes 1835328 | tf_op jit(solution)/shard_map/while/body/tab,trb->tra/dot_general | solution.py:64
  276.2 4.4 %constant_dynamic-slice_fusion.2 = f32[64,1,4096]{2,1,0:T(1,128)S(1)} fusion(f32[64,8,4096]{2,1,0:T(8,128)} %get-tuple-element.170, s32[]{:T(128)S(6)} %select_n.43), kind=kLoop, calls=%fused_computation.11.clone.1 | loop fusion | bytes 2097156 | tf_op jit(solution)/shard_map/while/body/jit(dynamic_index_in_dim)/dynamic_slice | solution.py:60
  284.2 5.3 %fusion.45 = f32[64,16,64]{2,1,0:T(8,128)} fusion(f32[64,16,64]{2,1,0:T(8,128)} %get-tuple-element.156, f32[64,64,64]{2,1,0:T(8,128)S(1)} %reshape.124, f32[64,16,64]{2,1,0:T(8,128)S(1)} %gather_fusion, f32[64]{0:T(128)S(1)} %compare_convert_fusion.2, pred[64]{0:T(512)(128)(4,1)S(1)} %get-tuple-element.144), kind=kOutput, calls=%fused_computation.3.clone.1 | convolution fusion | flops 50528256 | bytes 1835328 | tf_op jit(solution)/shard_map/while/body/tab,trb->tra/dot_general | solution.py:64
  290.0 4.4 %constant_dynamic-slice_fusion.2 = f32[64,1,4096]{2,1,0:T(1,128)S(1)} fusion(f32[64,8,4096]{2,1,0:T(8,128)} %get-tuple-element.170, s32[]{:T(128)S(6)} %select_n.43), kind=kLoop, calls=%fused_computation.11.clone.1 | loop fusion | bytes 2097156 | tf_op jit(solution)/shard_map/while/body/jit(dynamic_index_in_dim)/dynamic_slice | solution.py:60
  298.0 5.3 %fusion.45 = f32[64,16,64]{2,1,0:T(8,128)} fusion(f32[64,16,64]{2,1,0:T(8,128)} %get-tuple-element.156, f32[64,64,64]{2,1,0:T(8,128)S(1)} %reshape.124, f32[64,16,64]{2,1,0:T(8,128)S(1)} %gather_fusion, f32[64]{0:T(128)S(1)} %compare_convert_fusion.2, pred[64]{0:T(512)(128)(4,1)S(1)} %get-tuple-element.144), kind=kOutput, calls=%fused_computation.3.clone.1 | convolution fusion | flops 50528256 | bytes 1835328 | tf_op jit(solution)/shard_map/while/body/tab,trb->tra/dot_general | solution.py:64
  303.8 4.4 %constant_dynamic-slice_fusion.2 = f32[64,1,4096]{2,1,0:T(1,128)S(1)} fusion(f32[64,8,4096]{2,1,0:T(8,128)} %get-tuple-element.170, s32[]{:T(128)S(6)} %select_n.43), kind=kLoop, calls=%fused_computation.11.clone.1 | loop fusion | bytes 2097156 | tf_op jit(solution)/shard_map/while/body/jit(dynamic_index_in_dim)/dynamic_slice | solution.py:60
  311.8 5.3 %fusion.45 = f32[64,16,64]{2,1,0:T(8,128)} fusion(f32[64,16,64]{2,1,0:T(8,128)} %get-tuple-element.156, f32[64,64,64]{2,1,0:T(8,128)S(1)} %reshape.124, f32[64,16,64]{2,1,0:T(8,128)S(1)} %gather_fusion, f32[64]{0:T(128)S(1)} %compare_convert_fusion.2, pred[64]{0:T(512)(128)(4,1)S(1)} %get-tuple-element.144), kind=kOutput, calls=%fused_computation.3.clone.1 | convolution fusion | flops 50528256 | bytes 1835328 | tf_op jit(solution)/shard_map/while/body/tab,trb->tra/dot_general | solution.py:64
  317.6 4.4 %constant_dynamic-slice_fusion.2 = f32[64,1,4096]{2,1,0:T(1,128)S(1)} fusion(f32[64,8,4096]{2,1,0:T(8,128)} %get-tuple-element.170, s32[]{:T(128)S(6)} %select_n.43), kind=kLoop, calls=%fused_computation.11.clone.1 | loop fusion | bytes 2097156 | tf_op jit(solution)/shard_map/while/body/jit(dynamic_index_in_dim)/dynamic_slice | solution.py:60
  325.5 5.3 %fusion.45 = f32[64,16,64]{2,1,0:T(8,128)} fusion(f32[64,16,64]{2,1,0:T(8,128)} %get-tuple-element.156, f32[64,64,64]{2,1,0:T(8,128)S(1)} %reshape.124, f32[64,16,64]{2,1,0:T(8,128)S(1)} %gather_fusion, f32[64]{0:T(128)S(1)} %compare_convert_fusion.2, pred[64]{0:T(512)(128)(4,1)S(1)} %get-tuple-element.144), kind=kOutput, calls=%fused_computation.3.clone.1 | convolution fusion | flops 50528256 | bytes 1835328 | tf_op jit(solution)/shard_map/while/body/tab,trb->tra/dot_general | solution.py:64
  331.4 4.4 %constant_dynamic-slice_fusion.2 = f32[64,1,4096]{2,1,0:T(1,128)S(1)} fusion(f32[64,8,4096]{2,1,0:T(8,128)} %get-tuple-element.170, s32[]{:T(128)S(6)} %select_n.43), kind=kLoop, calls=%fused_computation.11.clone.1 | loop fusion | bytes 2097156 | tf_op jit(solution)/shard_map/while/body/jit(dynamic_index_in_dim)/dynamic_slice | solution.py:60
  339.3 5.3 %fusion.45 = f32[64,16,64]{2,1,0:T(8,128)} fusion(f32[64,16,64]{2,1,0:T(8,128)} %get-tuple-element.156, f32[64,64,64]{2,1,0:T(8,128)S(1)} %reshape.124, f32[64,16,64]{2,1,0:T(8,128)S(1)} %gather_fusion, f32[64]{0:T(128)S(1)} %compare_convert_fusion.2, pred[64]{0:T(512)(128)(4,1)S(1)} %get-tuple-element.144), kind=kOutput, calls=%fused_computation.3.clone.1 | convolution fusion | flops 50528256 | bytes 1835328 | tf_op jit(solution)/shard_map/while/body/tab,trb->tra/dot_general | solution.py:64
  345.2 4.4 %constant_dynamic-slice_fusion.2 = f32[64,1,4096]{2,1,0:T(1,128)S(1)} fusion(f32[64,8,4096]{2,1,0:T(8,128)} %get-tuple-element.170, s32[]{:T(128)S(6)} %select_n.43), kind=kLoop, calls=%fused_computation.11.clone.1 | loop fusion | bytes 2097156 | tf_op jit(solution)/shard_map/while/body/jit(dynamic_index_in_dim)/dynamic_slice | solution.py:60
  353.1 5.3 %fusion.45 = f32[64,16,64]{2,1,0:T(8,128)} fusion(f32[64,16,64]{2,1,0:T(8,128)} %get-tuple-element.156, f32[64,64,64]{2,1,0:T(8,128)S(1)} %reshape.124, f32[64,16,64]{2,1,0:T(8,128)S(1)} %gather_fusion, f32[64]{0:T(128)S(1)} %compare_convert_fusion.2, pred[64]{0:T(512)(128)(4,1)S(1)} %get-tuple-element.144), kind=kOutput, calls=%fused_computation.3.clone.1 | convolution fusion | flops 50528256 | bytes 1835328 | tf_op jit(solution)/shard_map/while/body/tab,trb->tra/dot_general | solution.py:64
  359.0 4.4 %constant_dynamic-slice_fusion.2 = f32[64,1,4096]{2,1,0:T(1,128)S(1)} fusion(f32[64,8,4096]{2,1,0:T(8,128)} %get-tuple-element.170, s32[]{:T(128)S(6)} %select_n.43), kind=kLoop, calls=%fused_computation.11.clone.1 | loop fusion | bytes 2097156 | tf_op jit(solution)/shard_map/while/body/jit(dynamic_index_in_dim)/dynamic_slice | solution.py:60
  366.9 5.3 %fusion.45 = f32[64,16,64]{2,1,0:T(8,128)} fusion(f32[64,16,64]{2,1,0:T(8,128)} %get-tuple-element.156, f32[64,64,64]{2,1,0:T(8,128)S(1)} %reshape.124, f32[64,16,64]{2,1,0:T(8,128)S(1)} %gather_fusion, f32[64]{0:T(128)S(1)} %compare_convert_fusion.2, pred[64]{0:T(512)(128)(4,1)S(1)} %get-tuple-element.144), kind=kOutput, calls=%fused_computation.3.clone.1 | convolution fusion | flops 50528256 | bytes 1835328 | tf_op jit(solution)/shard_map/while/body/tab,trb->tra/dot_general | solution.py:64
  (119 shorter events, 67.3 us)
Async XLA Ops:
  0.0 15.8 %copy-start.2 = (f32[64,1024]{1,0:T(8,128)S(1)}, f32[64,1024]{1,0:T(8,128)}, u32[]{:S(2)}) copy-start(f32[64,1024]{1,0:T(8,128)} %param.21) | copy-start | bytes 786436
  0.0 257.1 %collective-permute-start.1 = (f32[16,4096]{1,0:T(8,128)}, f32[16,4096]{1,0:T(8,128)S(1)}, u32[]{:S(2)}, u32[]{:S(2)}) collective-permute-start(f32[16,4096]{1,0:T(8,128)} %param.14), channel_id=1, source_target_pairs={{1,0},{2,1},{3,2},{4,3},{5,4},{6,5},{7,6},{8,7},{9,8},{10,9},{11,1... | collective-permute-start | bytes 786440 | tf_op jit(solution)/shard_map/ppermute | solution.py:24
  1.4 255.7 %collective-permute-start = (f32[16,4096]{1,0:T(8,128)}, f32[16,4096]{1,0:T(8,128)}, u32[]{:S(2)}, u32[]{:S(2)}) collective-permute-start(f32[16,4096]{1,0:T(8,128)} %param.14), channel_id=1, source_target_pairs={{0,1},{1,2},{2,3},{3,4},{4,5},{5,6},{6,7},{7,8},{8,9},{9,10},{10,1... | collective-permute-start | bytes 786440 | tf_op jit(solution)/shard_map/ppermute | solution.py:23
  7.8 71.4 %copy-start = (f32[64,32,64]{2,1,0:T(8,128)}, f32[64,32,64]{2,1,0:T(8,128)S(1)}, u32[]{:S(2)}) copy-start(f32[64,32,64]{2,1,0:T(8,128)S(1)} %reshape.72) | copy-start | bytes 1572868
  9.7 70.4 %copy-start.7 = (s32[4,8]{1,0:T(4,128)S(1)}, s32[4,8]{1,0:T(4,128)}, u32[]{:S(2)}) copy-start(s32[4,8]{1,0:T(4,128)} %param.22) | copy-start | bytes 388
  9.9 72.9 %copy-start.3 = (f32[4,1024]{1,0:T(4,128)S(1)}, f32[4,1024]{1,0:T(4,128)}, u32[]{:S(2)}) copy-start(f32[4,1024]{1,0:T(4,128)} %param.24) | copy-start | bytes 49156
  9.9 211.4 %copy-start.4 = (f32[1,4,1024]{2,1,0:T(4,128)S(1)}, f32[1,4,1024]{2,1,0:T(4,128)}, u32[]{:S(2)}) copy-start(f32[1,4,1024]{2,1,0:T(4,128)} %param.25) | copy-start | bytes 49156
  10.0 211.4 %copy-start.5 = (s32[64,8]{0,1:T(8,128)S(1)}, s32[64,8]{0,1:T(8,128)}, u32[]{:S(2)}) copy-start(s32[64,8]{0,1:T(8,128)} %param.19) | copy-start | bytes 6148
  10.9 225.9 %collective-permute-start.3 = (f32[16,2048]{1,0:T(8,128)}, f32[16,2048]{1,0:T(8,128)}, u32[]{:S(2)}, u32[]{:S(2)}) collective-permute-start(f32[16,2048]{1,0:T(8,128)} %reshape.74), channel_id=1, source_target_pairs={{1,0},{2,1},{3,2},{4,3},{5,4},{6,5},{7,6},{8,7},{9,8},{10,9},{11,1... | collective-permute-start | bytes 393224 | tf_op jit(solution)/shard_map/ppermute | solution.py:24
  12.2 226.9 %collective-permute-start.2 = (f32[16,2048]{1,0:T(8,128)}, f32[16,2048]{1,0:T(8,128)}, u32[]{:S(2)}, u32[]{:S(2)}) collective-permute-start(f32[16,2048]{1,0:T(8,128)} %reshape.74), channel_id=1, source_target_pairs={{0,1},{1,2},{2,3},{3,4},{4,5},{5,6},{6,7},{7,8},{8,9},{9,10},{10,1... | collective-permute-start | bytes 393224 | tf_op jit(solution)/shard_map/ppermute | solution.py:23
  16.0 206.8 %copy-start.6 = (s32[64,8]{0,1:T(8,128)S(1)}, s32[64,8]{0,1:T(8,128)}, u32[]{:S(2)}) copy-start(s32[64,8]{0,1:T(8,128)} %param.16) | copy-start | bytes 6148
  226.7 9.4 %copy-start.8 = (s32[64]{0:T(128)S(1)}, s32[64]{0:T(128)}, u32[]{:S(2)}) copy-start(s32[64]{0:T(128)} %param.17) | copy-start | bytes 772
  244.6 12.5 %copy-start.1 = (f32[16,4096]{1,0:T(8,128)S(1)}, f32[16,4096]{1,0:T(8,128)}, u32[]{:S(2)}) copy-start(f32[16,4096]{1,0:T(8,128)} %param.14) | copy-start | bytes 786436
where the time goes:
time: 378 us; the launch traced here: 376 us
  blocking collectives  198 us (52%)
  local copies, waits for them, and re-layouts  95.3 us (25%)
  matrix products  63.6 us (17%)
  starting transfers between devices  10.1 us (3%)
  loops' own time  5.86 us (2%)
    psum x1, blocking collectives, per_device(): group_sum = lax.psum(projected_sum, 'leaf')  127 us
    all_gather x1, blocking collectives, per_device(): shard_rows = lax.all_gather(cluster_rows, 'leaf', axis=0, tiled=True)  60.3 us
    dot_general x8, matrix products, near_step(): term = jnp.einsum('tab,trb->tra', slab, picked, precision=highest_precision)  42 us
    dynamic_slice x16, local copies, waits for them, and re-layouts, near_step(): lax.dynamic_index_in_dim(near_blocks, slot_index, axis=1, keepdims=False)  40.3 us
    gather x8, local copies, waits for them, and re-layouts, near_step(): picked = jnp.take(point_blocks, near_local[:, slot_index], axis=0)  16 us
    all_gather x1, blocking collectives, per_device(): all_groups = lax.all_gather(group_sum, 'group', axis=0, tiled=True)  11.2 us
    dot_general x1, matrix products, per_device(): jnp.einsum('tjkl,rtjl->tkr', leaf_coupling.reshape(leaves_here, FAR0, K,...  10.6 us
    reshape x1, local copies, waits for them, and re-layouts, per_device(): leaf_coupling.reshape(leaves_here, FAR0, K, K)  9.12 us
  transfers between devices with their start and end apart: 4, of which 0 were waited for; matrix products, arithmetic and copies ran while one was open for 13% of the time, Pallas kernels for 0%

commit v1 on v0

v1 whole, which is shorter than its diff:
```python
import jax
import jax.numpy as jnp
from jax import lax
from jax.experimental import pallas as pl
from jax.experimental.pallas import tpu as pltpu
from jax.sharding import PartitionSpec as P

LEAF=64;K=32;RHS=16
f32=jnp.float32; bf16=jnp.bfloat16
NT=(((1,),(1,)),((),()))
def split(a):
    h=a.astype(bf16)
    return h,(a-h.astype(f32)).astype(bf16)
def dotnt(a,b): return lax.dot_general(a,b,NT,preferred_element_type=f32)
def dotnn(a,b): return lax.dot_general(a,b,(((1,),(0,)),((),())),preferred_element_type=f32)

def point_pairs(x_ref, first, pairs, hi, lo):
    lane=lax.broadcasted_iota(jnp.int32,(RHS,128),1)
    left=lane<LEAF
    zero=jnp.zeros((RHS,128),f32)
    def body(q,_):
        x=x_ref[:,pl.ds(pl.multiple_of(q*128,128),128)]
        y=pltpu.roll(x,LEAF,1)
        for n,(a,b) in enumerate(((x,y),(y,x))):
            blk=jnp.concatenate([jnp.where(left,a,zero),jnp.where(left,zero,b)],axis=0)
            h,l=split(blk)
            hi[first+2*q+n]=h
            lo[first+2*q+n]=l
        return 0
    lax.fori_loop(0,pairs,body,0,unroll=4)

def near_kernel(base, src, cnt, xb, xo, xa, nb, out, hi, lo, weave):
    g=pl.program_id(0)
    n=xo.shape[1]//LEAF
    @pl.when(g==0)
    def _():
        point_pairs(xb,0,n//2,hi,lo)
        point_pairs(xo,n,n//2,hi,lo)
        point_pairs(xa,2*n,n//2,hi,lo)
        hi[3*n]=jnp.zeros((2*RHS,128),bf16)
        lo[3*n]=jnp.zeros((2*RHS,128),bf16)
        row=lax.broadcasted_iota(jnp.int32,(256,256),0)
        col=lax.broadcasted_iota(jnp.int32,(256,256),1)
        a=lax.rem(col,64)
        want=lax.rem(a,2)*128+(col//64)*32+a//2
        weave[...]=(row==want).astype(f32).astype(bf16)
    per=nb.shape[0]//256
    for quad in range(per//4):
        parts=[]
        for m in range(4):
            i=quad*4+m
            a=jnp.concatenate([nb[pl.ds(i*256+j,32,stride=8),:] for j in range(8)],axis=1)
            ah,al=split(a)
            t=g*per+i
            live=cnt[t]
            at=[jnp.where(j<live,src[t,j]-base[0],3*n) for j in range(8)]
            xh=jnp.concatenate([hi[s] for s in at],axis=1)
            xl=jnp.concatenate([lo[s] for s in at],axis=1)
            d=dotnt(jnp.concatenate([xh,xl],axis=0),ah)
            parts.append(d[:2*RHS]+d[2*RHS:]+dotnt(xh,al))
        m4=jnp.concatenate(parts,axis=1)
        m4=jnp.concatenate([m4[:RHS],m4[RHS:]],axis=1)
        h,l=split(m4)
        out[:,pl.ds(pl.multiple_of((g*per+quad*4)*LEAF,256),256)]=dotnn(h,weave[...])+dotnn(l,weave[...])

def near(base,src,cnt,xb,xo,xa,nb,steps=8):
    leaves=nb.shape[0]
    view=nb.reshape(leaves,8,32,128).transpose(0,2,1,3).reshape(leaves*256,128)
    blk=leaves*256//steps
    full=lambda g,*_:(0,0)
    return pl.pallas_call(near_kernel,
        out_shape=jax.ShapeDtypeStruct(xo.shape,f32),
        grid_spec=pltpu.PrefetchScalarGridSpec(num_scalar_prefetch=3,grid=(steps,),
            in_specs=[pl.BlockSpec(xb.shape,full)]*3+[pl.BlockSpec((blk,128),lambda g,*_:(g,0))],
            out_specs=pl.BlockSpec(xo.shape,full),
            scratch_shapes=[pltpu.VMEM((3*leaves+1,32,128),bf16)]*2+[pltpu.VMEM((256,256),bf16)]),
        compiler_params=pltpu.CompilerParams(vmem_limit_bytes=40<<20),
        name="near")(base,src,cnt,xb,xo,xa,view)


def iota(shape,d): return lax.broadcasted_iota(jnp.int32,shape,d)
def onehot(cond): return cond.astype(f32).astype(bf16)
def exact(v,m):
    h,l=split(v)
    return dotnn(h,m)+dotnn(l,m)
def spread4(tile,m):
    block=jnp.where(iota(tile.shape,1)//K==m,tile,0.0)
    block=block+pltpu.roll(block,64,1)
    return block+pltpu.roll(block,32,1)
def masked4(rows):
    lane=lax.rem(iota(rows.shape,1),128)//K
    both=jnp.concatenate([jnp.where(lane==m,rows,0.0) for m in range(4)],axis=0)
    return split(both)
def mul3(v,w):
    h,l=split(v)
    d=dotnt(jnp.concatenate([h,l],axis=0),w[0])
    return d[:RHS]+d[RHS:]+dotnt(h,w[1])

def up_kernel(x,bas,tra,upt,coef,pay,fs):
    lane=iota((RHS,128),1)
    left=lane<LEAF
    n=x.shape[1]//LEAF
    row=iota((256,256),0); col=iota((256,256),1)
    k2=lax.rem(row,128)//8
    s2=onehot(col==lax.rem(row,8)*32+2*k2+row//128)
    same=(iota((256,128),0)//32==lax.rem(iota((256,128),1),8))
    v4=[]
    for g in range(n//8):
        blks=[]
        for q in range(4):
            t=x[:,pl.ds((g*4+q)*128,128)]
            y=pltpu.roll(t,LEAF,1)
            for a,b in ((t,y),(y,t)):
                blks+= [jnp.where(left,a,0.0),jnp.where(left,0.0,b)]
        xh,xl=split(jnp.concatenate(blks,axis=0))
        bh,bl=split(bas[pl.ds(g*128,128),:])
        d=dotnt(xh,bh)+dotnt(xl,bh)+dotnt(xh,bl)
        d=jnp.where(same,d,0.0).reshape(8,32,128).sum(axis=0)
        c=exact(jnp.concatenate([d[:RHS],d[RHS:]],axis=1),s2)
        coef[:,pl.ds(g*256,256)]=c
        for i in range(8):
            v4.append(spread4(c[:,(i//4)*128:(i//4)*128+128],i%4))
    nc=upt.shape[0]
    per=n//nc
    outs=[]
    for u in range(nc):
        e=jnp.concatenate([tra[pl.ds(((u*per+i)//8)*64+(u*per+i)%8,8,stride=8),:] for i in range(per)],axis=1)
        outs.append(mul3(jnp.concatenate(v4[u*per:(u+1)*per],axis=1),masked4(e)))
    row=iota((128,128),0); col=iota((128,128),1)
    s3=onehot(col==row//32*32+lax.rem(row,8)*4+lax.rem(row,32)//8)
    cc=exact(jnp.concatenate(outs,axis=1),s3)
    pay[0:RHS,:]=cc
    for q in range(8):
        fs[pl.ds(q*nc,nc),:]=upt[:,pl.ds(q*128,128)]
    f=jnp.concatenate([fs[pl.ds(u,8,stride=nc),:] for u in range(nc)],axis=1)
    pr=mul3(jnp.concatenate([spread4(cc,u) for u in range(nc)],axis=1),masked4(f))
    pay[RHS:,:]=jnp.concatenate([jnp.concatenate([pr[0:8],pr[8:16]],axis=1),jnp.zeros((8,64),f32)],axis=1)

def up(x,basis,transfer,upper):
    n=basis.shape[0]
    bas=basis.reshape(n//8,8,16,128).transpose(0,2,1,3).reshape(n*16,128)
    tra=transfer.reshape(n//8,8,8,128).transpose(0,2,1,3).reshape(n*8,128)
    return pl.pallas_call(up_kernel,
        out_shape=(jax.ShapeDtypeStruct((RHS,n*K),f32),jax.ShapeDtypeStruct((24,128),f32)),
        scratch_shapes=[pltpu.VMEM((8*upper.shape[0],128),f32)],
        compiler_params=pltpu.CompilerParams(vmem_limit_bytes=24<<20),name="up")(x,bas,tra,upper)

def far_kernel(base,src,cb,co,ca,cpl,out,hi,lo):
    g=pl.program_id(0)
    tiles=co.shape[1]//128
    @pl.when(g==0)
    def _():
        for w,ref in enumerate((cb,co,ca)):
            def body(q,_):
                t=ref[:,pl.ds(pl.multiple_of(q*128,128),128)]
                for m in range(4):
                    h,l=split(spread4(t,m))
                    hi[(w*tiles+q)*4+m]=h
                    lo[(w*tiles+q)*4+m]=l
                return 0
            lax.fori_loop(0,tiles,body,0,unroll=4)
    per=cpl.shape[0]//64
    for i in range(per):
        c=jnp.concatenate([cpl[pl.ds(i*64+j,8,stride=8),:] for j in range(8)],axis=1)
        wh,wl=masked4(c)
        at=[src[g*per+i,j]-base[0] for j in range(8)]
        vh=jnp.concatenate([hi[s] for s in at],axis=1)
        vl=jnp.concatenate([lo[s] for s in at],axis=1)
        d=dotnt(jnp.concatenate([vh,vl],axis=0),wh)
        out[pl.ds(i*RHS,RHS),:]=d[:RHS]+d[RHS:]+dotnt(vh,wl)

def far(base,src,cb,co,ca,coupling,steps=8):
    n=coupling.shape[0]
    view=coupling.reshape(n,8,8,128).transpose(0,2,1,3).reshape(n*64,128)
    full=lambda g,*_:(0,0)
    return pl.pallas_call(far_kernel,
        out_shape=jax.ShapeDtypeStruct((n*RHS,K),f32),
        grid_spec=pltpu.PrefetchScalarGridSpec(num_scalar_prefetch=2,grid=(steps,),
            in_specs=[pl.BlockSpec(co.shape,full)]*3+[pl.BlockSpec((n*64//steps,128),lambda g,*_:(g,0))],
            out_specs=pl.BlockSpec((n*RHS//steps,K),lambda g,*_:(g,0)),
            scratch_shapes=[pltpu.VMEM((3*n,RHS,128),bf16)]*2),
        compiler_params=pltpu.CompilerParams(vmem_limit_bytes=24<<20),name="far")(base,src,cb,co,ca,view)

def down_kernel(csrc,pays,sums,gcp,ccp,upt,tra,bas,lf,near_ref,out,gs,fs):
    nc=upt.shape[0]; ng=gcp.shape[0]
    n=lf.shape[0]//RHS
    devs=pays.shape[0]//24
    row=iota((K,128),0); col=lax.rem(iota((K,128),1),K)
    s4=onehot(col==lax.rem(row,8)*4+row//8)
    for q in range(8):
        fs[pl.ds(q*nc,nc),:]=upt[:,pl.ds(q*128,128)]
        gs[pl.ds(q*ng,ng),:]=gcp[:,pl.ds(q*128,128)]
    gv=[]
    for h in range(ng):
        t=sums[pl.ds(h*8,8),:]
        gv.append(exact(jnp.concatenate([t[:,0:K],t[:,K:2*K]],axis=0),s4))
    gw=jnp.concatenate([gs[pl.ds(h,8,stride=ng),:] for h in range(ng)],axis=1)
    gf=mul3(jnp.concatenate(gv,axis=1),masked4(gw))
    fw=jnp.concatenate([fs[pl.ds(u,8,stride=nc),:] for u in range(nc)],axis=1)
    wh,wl=masked4(fw)
    gh,gl=split(gf)
    down=dotnn(gh,wh)+dotnn(gl,wh)+dotnn(gh,wl)
    row=lax.rem(iota((128,K),0),K); col=iota((128,K),1)
    s5=onehot(row==lax.rem(col,8)*4+col//8)
    down=jnp.concatenate([down[:,u*128:(u+1)*128] for u in range(nc)],axis=0)
    down=exact(down,s5)
    row=lax.rem(iota((128,256),0),K); col=iota((128,256),1)
    p1=onehot(row==2*(lax.rem(col,128)//8)+col//128)
    row=iota((K,256),0); col=iota((K,256),1)
    nat=2*(lax.rem(col,128)//8)+col//128
    p2=onehot(row==lax.rem(nat,4)*8+nat//4)
    left=iota((RHS,128),1)<LEAF
    per=n//nc
    for u in range(nc):
        w=jnp.concatenate([ccp[pl.ds(u*64+j,8,stride=8),:] for j in range(8)],axis=1)
        vs=[]
        for j in range(8):
            s=csrc[u,j]
            place=lax.rem(s//nc,2)*(devs//2)+s//(2*nc)
            vs.append(spread4(pays[pl.ds(pl.multiple_of(place*24,8),RHS),:],lax.rem(s,nc)))
        cf=mul3(jnp.concatenate(vs,axis=1),masked4(w))+down[u*RHS:(u+1)*RHS]
        e=jnp.concatenate([tra[pl.ds(((u*per+i)//8)*64+(u*per+i)%8,8,stride=8),:] for i in range(per)],axis=1)
        eh,el=masked4(e)
        ch,cl=split(cf)
        d=dotnn(jnp.concatenate([ch,cl,ch],axis=1),jnp.concatenate([eh,eh,el],axis=0))
        d=jnp.concatenate([d[:,i*128:(i+1)*128] for i in range(per)],axis=0)
        q=exact(d,p1)+exact(lf[pl.ds(u*per*RHS,per*RHS),:],p2)
        for b in range(per//8):
            g=(u*per)//8+b
            z=q[b*128:(b+1)*128].reshape(8,RHS,256)
            z=jnp.stack([z[:,:,:128],z[:,:,128:]],axis=1).reshape(256,128)
            same=(iota((256,128),0)//32==lax.rem(iota((256,128),1),8))
            zh,zl=split(jnp.where(same,z,0.0))
            bh,bl=split(bas[pl.ds(g*128,128),:])
            o=(dotnn(zh,bh)+dotnn(zl,bh)+dotnn(zh,bl)).reshape(8,2,RHS,128)
            for m in range(4):
                a=jnp.where(left,o[2*m,0],o[2*m,1])
                c=jnp.where(left,o[2*m+1,0],o[2*m+1,1])
                r=jnp.where(left,a,c)+pltpu.roll(jnp.where(left,c,a),LEAF,1)
                at=pl.ds(g*512+m*128,128)
                out[:,at]=near_ref[:,at]+r

def down(csrc,pays,sums,gcp,ccp,upper,transfer,basis,lf,nearv):
    n=basis.shape[0]; nc=upper.shape[0]; ng=gcp.shape[0]
    bas=basis.reshape(n//8,8,16,128).transpose(0,2,1,3).reshape(n*16,128)
    tra=transfer.reshape(n//8,8,8,128).transpose(0,2,1,3).reshape(n*8,128)
    ccv=ccp.reshape(nc,8,8,128).transpose(0,2,1,3).reshape(nc*64,128)
    vm=pl.BlockSpec(memory_space=pltpu.VMEM)
    return pl.pallas_call(down_kernel,
        out_shape=jax.ShapeDtypeStruct((RHS,n*LEAF),f32),
        in_specs=[pl.BlockSpec(memory_space=pltpu.SMEM)]+[vm]*9,
        scratch_shapes=[pltpu.VMEM((8*ng,128),f32),pltpu.VMEM((8*nc,128),f32)],
        compiler_params=pltpu.CompilerParams(vmem_limit_bytes=24<<20),name="down")(csrc,pays,sums,gcp,ccv,upper,tra,bas,lf,nearv)

def across(sizes):
    z,y,c=sizes
    return [[(a*y+b)*c+k for a in range(z) for b in range(y)] for k in range(c)]

def per_device(right_sides,near_blocks,near_source,near_count,basis,leaf_source,leaf_coupling,leaf_transfer,cluster_source,cluster_coupling,cluster_transfer,group_coupling):
    both=("group","leaf")
    leaves=near_blocks.shape[0]
    devs=lax.axis_size("leaf")
    every=lax.axis_size(both)
    base=((lax.axis_index(both)-1)*leaves).reshape(1).astype(jnp.int32)
    up_pairs=[(i,i+1) for i in range(every-1)]
    down_pairs=[(i+1,i) for i in range(every-1)]
    xb=lax.ppermute(right_sides,both,up_pairs)
    xa=lax.ppermute(right_sides,both,down_pairs)
    coef,pay=up(right_sides,basis,leaf_transfer,cluster_transfer)
    cb=lax.ppermute(coef,both,up_pairs)
    ca=lax.ppermute(coef,both,down_pairs)
    groups=across((devs//8,4,2))
    some=lax.all_to_all(jnp.broadcast_to(pay[None],(devs//2,)+pay.shape),"leaf",0,0,tiled=True,axis_index_groups=groups)
    pays=lax.all_gather(some,"leaf",axis=0,tiled=True,axis_index_groups=[[2*i,2*i+1] for i in range(devs//2)])
    total=pays[:,RHS:,:].sum(axis=0)
    sums=lax.all_gather(total,"group",axis=0,tiled=True)
    nearv=near(base,near_source,near_count,xb,right_sides,xa,near_blocks)
    lf=far(base,leaf_source,cb,coef,ca,leaf_coupling)
    return down(cluster_source,pays.reshape(devs*24,128),sums,group_coupling.reshape(-1,1024),cluster_coupling,cluster_transfer,leaf_transfer,basis,lf,nearv)

def solution(mesh):
    both=("group","leaf")
    one=P(both)
    two=P(both,None)
    three=P(both,None,None)
    return jax.shard_map(per_device,mesh=mesh,
        in_specs=(P(None,both),three,two,one,two,two,three,two,two,three,two,P("group",None,None)),
        out_specs=P(None,both),check_vma=False)
```

time: 378 us -> 87.6 us (0.23)
  the two profiles are of different devices: /device:TPU:0 before, /device:TPU:2 now
where the time goes in v1:
time: 87.6 us; the launch traced here: 87 us
  Pallas kernels  27.6 us (32%)
  starting transfers between devices  25.6 us (29%)
  blocking collectives  14.4 us (16%)
  local copies, waits for them, and re-layouts  12.7 us (14%)
  waiting for transfers between devices  6.55 us (7%)
    all_gather x1, blocking collectives, per_device(): sums = lax.all_gather(total, 'group', axis=0, tiled=True)  12 us
    unnamed x30, local copies, waits for them, and re-layouts  11.8 us
    pallas_call x1, Pallas kernels, near(): pl.pallas_call(near_kernel, out_shape=jax.ShapeDtypeStruct(xo.shape, f32)...  11.5 us
    all_to_all x1, starting transfers between devices, per_device(): lax.all_to_all(jnp.broadcast_to(pay[None], (devs // 2,) + pay.shape), 'le...  11.5 us
    ppermute x1, starting transfers between devices, per_device(): xa = lax.ppermute(right_sides, both, down_pairs)  7.86 us
    pallas_call x1, Pallas kernels, far(): pl.pallas_call(far_kernel, out_shape=jax.ShapeDtypeStruct((n * RHS, K), f...  7.19 us
    ppermute x1, waiting for transfers between devices, per_device(): cb = lax.ppermute(coef, both, up_pairs)  6.54 us
    pallas_call x1, Pallas kernels, down(): pl.pallas_call(down_kernel, out_shape=jax.ShapeDtypeStruct((RHS, n * LEAF...  5.58 us
  transfers between devices with their start and end apart: 5, of which 1 were waited for; matrix products, arithmetic and copies ran while one was open for 2% of the time, Pallas kernels for 21%

profile of v1, /device:TPU:2, one launch (start us, length us, event | category | flops | bytes accessed | tf_op | source)
XLA Modules:
  0.0 87.0 jit_solution(14277973815515076140)
XLA Ops:
  0.0 1.1 %copy-done.1 = f32[64,2048]{1,0:T(8,128)S(1)} copy-done((f32[64,2048]{1,0:T(8,128)S(1)}, f32[64,2048]{1,0:T(8,128)}, u32[]{:S(2)}) %copy-start.1) | copy-done | bytes 524312
  1.1 0.9 %copy-done.4 = f32[16,4096]{1,0:T(8,128)S(1)} copy-done((f32[16,4096]{1,0:T(8,128)S(1)}, f32[16,4096]{1,0:T(8,128)}, u32[]{:S(2)}) %copy-start.4) | copy-done | bytes 262168
  2.0 0.9 %copy-done.6 = f32[64,1024]{1,0:T(8,128)S(1)} copy-done((f32[64,1024]{1,0:T(8,128)S(1)}, f32[64,1024]{1,0:T(8,128)}, u32[]{:S(2)}) %copy-start.6) | copy-done | bytes 262168
  3.0 0.7 copy-done.9
  3.7 3.4 %up.1 = (f32[16,2048]{1,0:T(8,128)S(1)}, f32[24,128]{1,0:T(8,128)S(1)}) custom-call(f32[16,4096]{1,0:T(8,128)S(1)} %copy-done.4, f32[1024,128]{1,0:T(8,128)S(1)} %bitcast.30, f32[512,128]{1,0:T(8,128)S(1)} %bitcast.33, f32[4,1024]{1,0:T(4,128)S(1)} %copy-done.9), custom_call_target="tpu_custom_call" | custom-call | tf_op jit(solution)/shard_map/up/pallas_call | solution.py:143
  7.1 0.9 %broadcast_in_dim.2 = f32[32,24,128]{2,1,0:T(8,128)} broadcast(f32[24,128]{1,0:T(8,128)S(1)} %get-tuple-element.7), dimensions={1,2} | broadcast | bytes 405504 | tf_op jit(solution)/shard_map/broadcast_in_dim | solution.py:273
  7.9 11.5 %all-to-all-start = ((f32[32,24,128]{2,1,0:T(8,128)}), f32[32,24,128]{2,1,0:T(8,128)S(1)}, u32[]{:S(2)}, u32[]{:S(2)}) async-start(f32[32,24,128]{2,1,0:T(8,128)} %broadcast_in_dim.2), calls=%async_computation | async-start | bytes 786432 | tf_op jit(solution)/shard_map/all_to_all | solution.py:273
  19.4 1.9 %collective-permute-start.2 = (f32[16,4096]{1,0:T(8,128)}, f32[16,4096]{1,0:T(8,128)S(1)}, u32[]{:S(2)}, u32[]{:S(2)}) collective-permute-start(f32[16,4096]{1,0:T(8,128)} %xo.1), channel_id=1, source_target_pairs={{0,1},{1,2},{2,3},{3,4},{4,5},{5,6},{6,7},{7,8},{8,9},{9,10},{10,1... | collective-permute-start | bytes 786440 | tf_op jit(solution)/shard_map/ppermute | solution.py:267
  21.4 7.9 %collective-permute-start.3 = (f32[16,4096]{1,0:T(8,128)}, f32[16,4096]{1,0:T(8,128)S(1)}, u32[]{:S(2)}, u32[]{:S(2)}) collective-permute-start(f32[16,4096]{1,0:T(8,128)} %xo.1), channel_id=1, source_target_pairs={{1,0},{2,1},{3,2},{4,3},{5,4},{6,5},{7,6},{8,7},{9,8},{10,9},{11,1... | collective-permute-start | bytes 786440 | tf_op jit(solution)/shard_map/ppermute | solution.py:268
  29.2 1.9 %collective-permute-start.1 = (f32[16,2048]{1,0:T(8,128)S(1)}, f32[16,2048]{1,0:T(8,128)S(1)}, u32[]{:S(2)}, u32[]{:S(2)}) collective-permute-start(f32[16,2048]{1,0:T(8,128)S(1)} %get-tuple-element.8.co), channel_id=1, source_target_pairs={{1,0},{2,1},{3,2},{4,3},{5,4},{6,5},{7,6},{8,7},{9,8},{10,9},{11,1... | collective-permute-start | bytes 393224 | tf_op jit(solution)/shard_map/ppermute | solution.py:271
  31.2 2.4 %collective-permute-start = (f32[16,2048]{1,0:T(8,128)S(1)}, f32[16,2048]{1,0:T(8,128)S(1)}, u32[]{:S(2)}, u32[]{:S(2)}) collective-permute-start(f32[16,2048]{1,0:T(8,128)S(1)} %get-tuple-element.8.co), channel_id=1, source_target_pairs={{0,1},{1,2},{2,3},{3,4},{4,5},{5,6},{6,7},{7,8},{8,9},{9,10},{10,1... | collective-permute-start | bytes 393224 | tf_op jit(solution)/shard_map/ppermute | solution.py:270
  33.6 0.8 copy.16.src
  34.4 0.8 copy.15.src
  35.1 6.5 %collective-permute-done.cb = f32[16,2048]{1,0:T(8,128)S(1)} collective-permute-done((f32[16,2048]{1,0:T(8,128)S(1)}, f32[16,2048]{1,0:T(8,128)S(1)}, u32[]{:S(2)}, u32[]{:S(2)}) %collective-permute-start) | collective-permute-done | bytes 131104 | tf_op jit(solution)/shard_map/ppermute | solution.py:270
  41.7 1.6 %copy-done.3 = f32[64,8,1024]{2,1,0:T(8,128)S(1)} copy-done((f32[64,8,1024]{2,1,0:T(8,128)S(1)}, f32[64,8,1024]{2,1,0:T(8,128)}, u32[]{:S(2)}) %copy-start.3) | copy-done | bytes 2097176
  43.3 7.2 %far.1.lf = f32[1024,32]{1,0:T(8,128)S(1)} custom-call(s32[1]{0:T(128)} %bitcast.11.base, s32[64,8]{1,0:T(8,128)S(1)} %copy.15.src, f32[16,2048]{1,0:T(8,128)S(1)} %collective-permute-done.cb, f32[16,2048]{1,0:T(8,128)S(1)} %get-tuple-element.8.co, f32[16,2048]{1,0:T(8,128)S(1)} %collective-permute-done.1.ca, f32[4096,128]{1,0:T(8,128)S(1)} %bitcast.32), custom_call_target="tpu_custom_call" | custom-call | tf_op jit(solution)/shard_map/far/pallas_call | solution.py:176
  50.5 3.4 %copy-done = f32[64,8,4096]{2,1,0:T(8,128)S(1)} copy-done((f32[64,8,4096]{2,1,0:T(8,128)S(1)}, f32[64,8,4096]{2,1,0:T(8,128)}, u32[]{:S(2)}) %copy-start) | copy-done | bytes 8388632
  53.9 0.9 %copy-done.5 = f32[16,4096]{1,0:T(8,128)S(1)} copy-done((f32[16,4096]{1,0:T(8,128)S(1)}, f32[16,4096]{1,0:T(8,128)}, u32[]{:S(2)}) %copy-start.5) | copy-done | bytes 262168
  54.8 0.7 copy-done.13
  55.5 11.5 %near.1.near_ref = f32[16,4096]{1,0:T(8,128)S(1)} custom-call(s32[1]{0:T(128)} %bitcast.11.base, s32[64,8]{1,0:T(8,128)S(1)} %copy.16.src, s32[64]{0:T(128)S(1)} %copy-done.13, f32[16,4096]{1,0:T(8,128)S(1)} %collective-permute-done.2.xb, f32[16,4096]{1,0:T(8,128)S(1)} %copy-done.5, f32[16,4096]{1,0:T(8,128)S(1)} %collective-permute-done.3.xa, ...), custom_call_target="tpu_custom_call" | custom-call | tf_op jit(solution)/shard_map/near/pallas_call | solution.py:71
  67.0 2.4 %all_gather.6 = f32[64,24,128]{2,1,0:T(8,128)S(1)} all-gather(f32[32,24,128]{2,1,0:T(8,128)S(1)} %all-to-all-done), channel_id=1, replica_groups={{0,1},{2,3},{4,5},{6,7},{8,9},{10,11},{12,13},{14,15},{16,17},{18,19},{..., dimensions={0}, use_global_device_ids=true | all-gather | bytes 1179648 | tf_op jit(solution)/shard_map/all_gather | solution.py:274
  69.3 0.1 slice_reduce_fusion
  69.4 12.0 %all_gather.7.sums = f32[32,128]{1,0:T(8,128)S(1)} all-gather(f32[8,128]{1,0:T(8,128)S(1)} %slice_reduce_fusion), channel_id=1, replica_groups=mesh['group'=4,'leaf'=64] {'group'}, dimensions={0}, use_global_device_ids=true | all-gather | bytes 20480 | tf_op jit(solution)/shard_map/all_gather | solution.py:276
  81.4 5.6 %down.1 = f32[16,4096]{1,0:T(8,128)} custom-call(s32[4,8]{1,0:T(4,128)S(1)} %copy-done.12, f32[1536,128]{1,0:T(8,128)S(1)} %bitcast.29, f32[32,128]{1,0:T(8,128)S(1)} %all_gather.7.sums, f32[4,1024]{1,0:T(4,128)S(1)} %bitcast.36, f32[256,128]{1,0:T(8,128)S(1)} %bitcast.35, f32[4,1024]{1,0:T(4,128)S(1)} %copy-done.10, f32[512,128]{1,0:T(8,128)S(1)} %bitcast.34, ...), custom_call_target="tpu_custom_call" | custom-call | tf_op jit(solution)/shard_map/down/pallas_call | solution.py:249
  (24 shorter events, 0.1 us)
Async XLA Ops:
  0.0 81.4 %copy-start.12 = (s32[4,8]{1,0:T(4,128)S(1)}, s32[4,8]{1,0:T(4,128)}, u32[]{:S(2)}) copy-start(s32[4,8]{1,0:T(4,128)} %csrc.1) | copy-start | bytes 388
  0.0 1.1 %copy-start.1 = (f32[64,2048]{1,0:T(8,128)S(1)}, f32[64,2048]{1,0:T(8,128)}, u32[]{:S(2)}) copy-start(f32[64,2048]{1,0:T(8,128)} %param.16) | copy-start | bytes 1572868
  1.1 0.9 %copy-start.4 = (f32[16,4096]{1,0:T(8,128)S(1)}, f32[16,4096]{1,0:T(8,128)}, u32[]{:S(2)}) copy-start(f32[16,4096]{1,0:T(8,128)} %xo.1) | copy-start | bytes 786436
  2.0 0.9 %copy-start.6 = (f32[64,1024]{1,0:T(8,128)S(1)}, f32[64,1024]{1,0:T(8,128)}, u32[]{:S(2)}) copy-start(f32[64,1024]{1,0:T(8,128)} %param.19) | copy-start | bytes 786436
  3.0 0.7 copy-start.9
  3.7 77.7 %copy-start.2 = (f32[64,2048]{1,0:T(8,128)S(1)}, f32[64,2048]{1,0:T(8,128)}, u32[]{:S(2)}) copy-start(f32[64,2048]{1,0:T(8,128)} %param.16) | copy-start | bytes 1572868
  3.7 77.7 %copy-start.7 = (f32[64,1024]{1,0:T(8,128)S(1)}, f32[64,1024]{1,0:T(8,128)}, u32[]{:S(2)}) copy-start(f32[64,1024]{1,0:T(8,128)} %param.19) | copy-start | bytes 786436
  3.7 77.7 %copy-start.8 = (f32[4,8,1024]{2,1,0:T(8,128)S(1)}, f32[4,8,1024]{2,1,0:T(8,128)}, u32[]{:S(2)}) copy-start(f32[4,8,1024]{2,1,0:T(8,128)} %param.21) | copy-start | bytes 393220
  3.7 77.7 %copy-start.10 = (f32[4,1024]{1,0:T(4,128)S(1)}, f32[4,1024]{1,0:T(4,128)}, u32[]{:S(2)}) copy-start(f32[4,1024]{1,0:T(4,128)} %upt.3) | copy-start | bytes 49156
  3.7 77.7 %copy-start.11 = (f32[1,4,1024]{2,1,0:T(4,128)S(1)}, f32[1,4,1024]{2,1,0:T(4,128)}, u32[]{:S(2)}) copy-start(f32[1,4,1024]{2,1,0:T(4,128)} %param.23) | copy-start | bytes 49156
  7.9 59.0 %all-to-all-start = ((f32[32,24,128]{2,1,0:T(8,128)}), f32[32,24,128]{2,1,0:T(8,128)S(1)}, u32[]{:S(2)}, u32[]{:S(2)}) async-start(f32[32,24,128]{2,1,0:T(8,128)} %broadcast_in_dim.2), calls=%async_computation | async-start | bytes 786432 | tf_op jit(solution)/shard_map/all_to_all | solution.py:273
  19.4 31.0 %collective-permute-start.2 = (f32[16,4096]{1,0:T(8,128)}, f32[16,4096]{1,0:T(8,128)S(1)}, u32[]{:S(2)}, u32[]{:S(2)}) collective-permute-start(f32[16,4096]{1,0:T(8,128)} %xo.1), channel_id=1, source_target_pairs={{0,1},{1,2},{2,3},{3,4},{4,5},{5,6},{6,7},{7,8},{8,9},{9,10},{10,1... | collective-permute-start | bytes 786440 | tf_op jit(solution)/shard_map/ppermute | solution.py:267
  21.4 29.1 %collective-permute-start.3 = (f32[16,4096]{1,0:T(8,128)}, f32[16,4096]{1,0:T(8,128)S(1)}, u32[]{:S(2)}, u32[]{:S(2)}) collective-permute-start(f32[16,4096]{1,0:T(8,128)} %xo.1), channel_id=1, source_target_pairs={{1,0},{2,1},{3,2},{4,3},{5,4},{6,5},{7,6},{8,7},{9,8},{10,9},{11,1... | collective-permute-start | bytes 786440 | tf_op jit(solution)/shard_map/ppermute | solution.py:268
  29.2 5.9 %collective-permute-start.1 = (f32[16,2048]{1,0:T(8,128)S(1)}, f32[16,2048]{1,0:T(8,128)S(1)}, u32[]{:S(2)}, u32[]{:S(2)}) collective-permute-start(f32[16,2048]{1,0:T(8,128)S(1)} %get-tuple-element.8.co), channel_id=1, source_target_pairs={{1,0},{2,1},{3,2},{4,3},{5,4},{6,5},{7,6},{8,7},{9,8},{10,9},{11,1... | collective-permute-start | bytes 393224 | tf_op jit(solution)/shard_map/ppermute | solution.py:271
  31.2 10.5 %collective-permute-start = (f32[16,2048]{1,0:T(8,128)S(1)}, f32[16,2048]{1,0:T(8,128)S(1)}, u32[]{:S(2)}, u32[]{:S(2)}) collective-permute-start(f32[16,2048]{1,0:T(8,128)S(1)} %get-tuple-element.8.co), channel_id=1, source_target_pairs={{0,1},{1,2},{2,3},{3,4},{4,5},{5,6},{6,7},{7,8},{8,9},{9,10},{10,1... | collective-permute-start | bytes 393224 | tf_op jit(solution)/shard_map/ppermute | solution.py:270
  41.7 1.6 %copy-start.3 = (f32[64,8,1024]{2,1,0:T(8,128)S(1)}, f32[64,8,1024]{2,1,0:T(8,128)}, u32[]{:S(2)}) copy-start(f32[64,8,1024]{2,1,0:T(8,128)} %param.18) | copy-start | bytes 6291460
  50.5 3.4 %copy-start = (f32[64,8,4096]{2,1,0:T(8,128)S(1)}, f32[64,8,4096]{2,1,0:T(8,128)}, u32[]{:S(2)}) copy-start(f32[64,8,4096]{2,1,0:T(8,128)} %param.13) | copy-start | bytes 25165828
  53.9 0.9 %copy-start.5 = (f32[16,4096]{1,0:T(8,128)S(1)}, f32[16,4096]{1,0:T(8,128)}, u32[]{:S(2)}) copy-start(f32[16,4096]{1,0:T(8,128)} %xo.1) | copy-start | bytes 786436
  54.8 0.7 copy-start.13

commit v2 on v1

v2 whole, which is shorter than its diff:
```python
import functools

import jax
import jax.numpy as jnp
from jax import lax
from jax.experimental import pallas as pl
from jax.experimental.pallas import tpu as pltpu
from jax.sharding import PartitionSpec as P

LEAF=64;K=32;RHS=16
f32=jnp.float32; bf16=jnp.bfloat16
NT=(((1,),(1,)),((),()))
def split(a):
    h=a.astype(bf16)
    return h,(a-h.astype(f32)).astype(bf16)
def dotnt(a,b): return lax.dot_general(a,b,NT,preferred_element_type=f32)
def dotnn(a,b): return lax.dot_general(a,b,(((1,),(0,)),((),())),preferred_element_type=f32)

HBM=pltpu.HBM
def in_hbm(v): return pltpu.with_memory_space_constraint(v,HBM)

def point_table(x_ref, first, leaves, hi, lo):
    left=lax.broadcasted_iota(jnp.int32,(RHS,128),1)<LEAF
    def body(q,_):
        x=x_ref[:,pl.ds(pl.multiple_of(q*128,128),128)]
        y=pltpu.roll(x,LEAF,1)
        for n,(a,b) in enumerate(((x,y),(y,x))):
            h,l=split(jnp.where(left,a,b))
            hi[first+2*q+n]=h
            lo[first+2*q+n]=l
        return 0
    lax.fori_loop(0,leaves//2,body,0,unroll=4)

def near_kernel(var, base, src_h, cnt_h, nb_h, xb, xo, xa, out, hi, lo, weave, nb, src, cnt, sem, sem2):
    n=out.shape[1]//LEAF
    chunks=sem.shape[0]
    size=nb.shape[0]//chunks
    def chunk(c): return pltpu.make_async_copy(nb_h.at[pl.ds(c*size,size),:],nb.at[pl.ds(c*size,size),:],sem.at[c])
    ca=pltpu.make_async_copy(src_h,src,sem2.at[0]); cb=pltpu.make_async_copy(cnt_h,cnt,sem2.at[1])
    ca.start(); cb.start()
    for c in range(chunks): chunk(c).start()
    point_table(xb,0,n,hi,lo)
    point_table(xo,n,n,hi,lo)
    point_table(xa,2*n,n,hi,lo)
    hi[3*n]=jnp.zeros((RHS,128),bf16)
    lo[3*n]=jnp.zeros((RHS,128),bf16)
    row=lax.broadcasted_iota(jnp.int32,(256,256),0)
    col=lax.broadcasted_iota(jnp.int32,(256,256),1)
    a=lax.rem(col,64)
    weave[...]=(row==col-a+lax.rem(a,2)*32+a//2).astype(f32).astype(bf16)
    ca.wait(); cb.wait()
    per=n//chunks
    first=base[0]
    left=lax.broadcasted_iota(jnp.int32,(RHS,128),1)<LEAF
    left32=lax.broadcasted_iota(jnp.int32,(32,128),1)<LEAF
    def join(table,at): return jnp.concatenate([jnp.where(left,table[at[2*p]],table[at[2*p+1]]) for p in range(4)],axis=1)
    def step(c,_):
        chunk(c).wait()
        for quad in range(per//4):
            parts=[]
            for m in range(4):
                t=c*per+quad*4+m
                off=pl.multiple_of(t*256,256)
                even=[];odd=[]
                for p in range(4):
                    a=nb[pl.ds(off+2*p,32,stride=8),:]
                    b=nb[pl.ds(off+2*p+1,32,stride=8),:]
                    if var=="f32":
                        even.append(jnp.where(left32,a,pltpu.roll(b,LEAF,1)))
                        odd.append(jnp.where(left32,pltpu.roll(a,LEAF,1),b))
                    else:
                        even.append((a,b))
                if var=="f32":
                    w=jnp.concatenate([jnp.concatenate(even,axis=1),jnp.concatenate(odd,axis=1)],axis=0)
                    ah,al=split(w)
                else:
                    res=[]
                    es=[(split(a),split(b)) for a,b in even]
                    for k in range(2):
                        e=jnp.concatenate([jnp.concatenate([a[k][:,:64],b[k][:,:64]],axis=1) for a,b in es],axis=1)
                        o=jnp.concatenate([jnp.concatenate([a[k][:,64:],b[k][:,64:]],axis=1) for a,b in es],axis=1)
                        res.append(jnp.concatenate([e,o],axis=0))
                    ah,al=res
                live=cnt[t]
                at=[jnp.where(j<live,src[j,t]-first,3*n) for j in range(8)]
                xh=join(hi,at); xl=join(lo,at)
                if var=="n128":
                    d=dotnt(jnp.concatenate([xh,xl],axis=0),jnp.concatenate([ah,al],axis=0))
                    parts.append(d[:RHS,:64]+d[RHS:,:64]+d[:RHS,64:])
                else:
                    d=dotnt(jnp.concatenate([xh,xl],axis=0),ah)
                    parts.append(d[:RHS]+d[RHS:]+dotnt(xh,al))
            h,l=split(jnp.concatenate(parts,axis=1))
            d=dotnn(jnp.concatenate([h,l],axis=0),weave[...])
            out[:,pl.ds(pl.multiple_of((c*per+quad*4)*LEAF,256),256)]=d[:RHS]+d[RHS:]
        return 0
    lax.fori_loop(0,chunks,step,0)

def near(base,src,cnt,xb,xo,xa,nb,chunks=4,var="f32"):
    leaves=nb.shape[0]
    view=nb.reshape(leaves,8,32,128).transpose(0,2,1,3).reshape(leaves*256,128)
    pts=leaves*LEAF
    blk=pl.BlockSpec((RHS,pts),lambda g:(0,0))
    hbm=pl.BlockSpec(memory_space=HBM)
    return pl.pallas_call(functools.partial(near_kernel,var),
        out_shape=jax.ShapeDtypeStruct((RHS,pts),f32),grid=(1,),
        in_specs=[pl.BlockSpec(memory_space=pltpu.SMEM),hbm,hbm,hbm,blk,blk,blk],
        out_specs=blk,
        scratch_shapes=[pltpu.VMEM((3*leaves+1,RHS,128),bf16)]*2+[pltpu.VMEM((256,256),bf16),pltpu.VMEM((leaves*256,128),f32),
            pltpu.SMEM((8,leaves),jnp.int32),pltpu.SMEM((leaves,),jnp.int32),pltpu.SemaphoreType.DMA((chunks,)),pltpu.SemaphoreType.DMA((2,))],
        compiler_params=pltpu.CompilerParams(vmem_limit_bytes=24<<20),
        name="near")(base,in_hbm(src.T),in_hbm(cnt),in_hbm(view),xb,xo,xa)

def iota(shape,d): return lax.broadcasted_iota(jnp.int32,shape,d)
def onehot(cond): return cond.astype(f32).astype(bf16)
def exact(v,m):
    h,l=split(v)
    return dotnn(h,m)+dotnn(l,m)
def spread4(tile,m):
    block=jnp.where(iota(tile.shape,1)//K==m,tile,0.0)
    block=block+pltpu.roll(block,64,1)
    return block+pltpu.roll(block,32,1)
def masked4(rows):
    lane=lax.rem(iota(rows.shape,1),128)//K
    both=jnp.concatenate([jnp.where(lane==m,rows,0.0) for m in range(4)],axis=0)
    return split(both)
def mul3(v,w):
    h,l=split(v)
    d=dotnt(jnp.concatenate([h,l],axis=0),w[0])
    return d[:RHS]+d[RHS:]+dotnt(h,w[1])

def up_kernel(x_h,bas_h,tra_h,upt_h,ext,rep,fs,x,bas,tra,upt,sem):
    moves=[pltpu.make_async_copy(s,d,sem.at[i]) for i,(s,d) in enumerate(((x_h,x),(bas_h,bas),(tra_h,tra),(upt_h,upt)))]
    for m in moves: m.start()
    pts=x.shape[1]
    lane=iota((RHS,128),1)
    left=lane<LEAF
    n=x.shape[1]//LEAF
    row=iota((256,256),0); col=iota((256,256),1)
    k2=lax.rem(row,128)//8
    s2=onehot(col==lax.rem(row,8)*32+2*k2+row//128)
    same=(iota((256,128),0)//32==lax.rem(iota((256,128),1),8))
    v4=[]
    moves[0].wait()
    moves[1].wait()
    ext[:,:pts]=x[...]
    for g in range(n//8):
        blks=[]
        for q in range(4):
            t=x[:,pl.ds((g*4+q)*128,128)]
            y=pltpu.roll(t,LEAF,1)
            for a,b in ((t,y),(y,t)):
                blks+= [jnp.where(left,a,0.0),jnp.where(left,0.0,b)]
        xh,xl=split(jnp.concatenate(blks,axis=0))
        bh,bl=split(bas[pl.ds(g*128,128),:])
        d=dotnt(xh,bh)+dotnt(xl,bh)+dotnt(xh,bl)
        d=jnp.where(same,d,0.0).reshape(8,32,128).sum(axis=0)
        c=exact(jnp.concatenate([d[:RHS],d[RHS:]],axis=1),s2)
        ext[:,pl.ds(pts+g*256,256)]=c
        for i in range(8):
            v4.append(spread4(c[:,(i//4)*128:(i//4)*128+128],i%4))
    nc=upt.shape[0]
    per=n//nc
    moves[2].wait()
    moves[3].wait()
    outs=[]
    for u in range(nc):
        e=jnp.concatenate([tra[pl.ds(((u*per+i)//8)*64+(u*per+i)%8,8,stride=8),:] for i in range(per)],axis=1)
        outs.append(mul3(jnp.concatenate(v4[u*per:(u+1)*per],axis=1),masked4(e)))
    row=iota((128,128),0); col=iota((128,128),1)
    s3=onehot(col==row//32*32+lax.rem(row,8)*4+lax.rem(row,32)//8)
    cc=exact(jnp.concatenate(outs,axis=1),s3)
    for q in range(8):
        fs[pl.ds(q*nc,nc),:]=upt[:,pl.ds(q*128,128)]
    f=jnp.concatenate([fs[pl.ds(u,8,stride=nc),:] for u in range(nc)],axis=1)
    pr=mul3(jnp.concatenate([spread4(cc,u) for u in range(nc)],axis=1),masked4(f))
    pay=jnp.concatenate([cc,jnp.concatenate([pr[0:8],pr[8:16],jnp.zeros((8,64),f32)],axis=1)],axis=0)
    for c in range(rep.shape[0]//24): rep[pl.ds(c*24,24),:]=pay

def up(x,basis,transfer,upper,copies):
    n=basis.shape[0]
    bas=basis.reshape(n//8,8,16,128).transpose(0,2,1,3).reshape(n*16,128)
    tra=transfer.reshape(n//8,8,8,128).transpose(0,2,1,3).reshape(n*8,128)
    args=(x,bas,tra,upper)
    return pl.pallas_call(up_kernel,
        out_shape=(jax.ShapeDtypeStruct((RHS,n*(LEAF+K)),f32),jax.ShapeDtypeStruct((copies*24,128),f32)),
        in_specs=[pl.BlockSpec(memory_space=HBM)]*4,
        scratch_shapes=[pltpu.VMEM((8*upper.shape[0],128),f32)]+[pltpu.VMEM(v.shape,f32) for v in args]+[pltpu.SemaphoreType.DMA((4,))],
        compiler_params=pltpu.CompilerParams(vmem_limit_bytes=24<<20),name="up")(*[in_hbm(v) for v in args])

def far_kernel(base,src_h,cpl_h,cb,co,ca,out,hi,lo,cpl,src,sem,sem2):
    tiles=co.shape[1]//128
    n=src.shape[1]
    chunks=sem.shape[0]
    size=cpl.shape[0]//chunks
    def chunk(c): return pltpu.make_async_copy(cpl_h.at[pl.ds(c*size,size),:],cpl.at[pl.ds(c*size,size),:],sem.at[c])
    idx=pltpu.make_async_copy(src_h,src,sem2.at[0])
    idx.start()
    for c in range(chunks): chunk(c).start()
    for w,ref in enumerate((cb,co,ca)):
        def body(q,_):
            t=ref[:,pl.ds(pl.multiple_of(q*128,128),128)]
            for m in range(4):
                h,l=split(spread4(t,m))
                hi[(w*tiles+q)*4+m]=h
                lo[(w*tiles+q)*4+m]=l
            return 0
        lax.fori_loop(0,tiles,body,0,unroll=4)
    idx.wait()
    per=n//chunks
    first=base[0]
    def step(c,_):
        chunk(c).wait()
        for i in range(per):
            t=c*per+i
            off=pl.multiple_of(t*64,64)
            w=jnp.concatenate([cpl[pl.ds(off+j,8,stride=8),:] for j in range(8)],axis=1)
            wh,wl=masked4(w)
            at=[src[j,t]-first for j in range(8)]
            vh=jnp.concatenate([hi[s] for s in at],axis=1)
            vl=jnp.concatenate([lo[s] for s in at],axis=1)
            d=dotnt(jnp.concatenate([vh,vl],axis=0),wh)
            out[pl.ds(pl.multiple_of(t*RHS,RHS),RHS),:]=d[:RHS]+d[RHS:]+dotnt(vh,wl)
        return 0
    lax.fori_loop(0,chunks,step,0)

def far(base,src,eb,eo,ea,coupling,chunks=4):
    n=coupling.shape[0]
    view=coupling.reshape(n,8,8,128).transpose(0,2,1,3).reshape(n*64,128)
    blk=pl.BlockSpec((RHS,n*K),lambda g:(0,LEAF//K))
    hbm=pl.BlockSpec(memory_space=HBM)
    return pl.pallas_call(far_kernel,
        out_shape=jax.ShapeDtypeStruct((n*RHS,K),f32),grid=(1,),
        in_specs=[pl.BlockSpec(memory_space=pltpu.SMEM),hbm,hbm,blk,blk,blk],
        out_specs=pl.BlockSpec((n*RHS,K),lambda g:(0,0)),
        scratch_shapes=[pltpu.VMEM((3*n,RHS,128),bf16)]*2+[pltpu.VMEM((n*64,128),f32),pltpu.SMEM((8,n),jnp.int32),
            pltpu.SemaphoreType.DMA((chunks,)),pltpu.SemaphoreType.DMA((1,))],
        compiler_params=pltpu.CompilerParams(vmem_limit_bytes=24<<20),name="far")(base,in_hbm(src.T),in_hbm(view),eb,eo,ea)

def down_kernel(base,csrc,pays,s0,s1,s2,s3,gcp,ccp,upt,tra,bas,lf,near_ref,out,gs,fs):
    nc=upt.shape[0]; ng=gcp.shape[0]
    n=lf.shape[0]//RHS
    devs=pays.shape[0]//24
    row=iota((K,128),0); col=lax.rem(iota((K,128),1),K)
    s4=onehot(col==lax.rem(row,8)*4+row//8)
    for q in range(8):
        fs[pl.ds(q*nc,nc),:]=upt[:,pl.ds(q*128,128)]
        gs[pl.ds(q*ng,ng),:]=gcp[:,pl.ds(q*128,128)]
    gv=[]
    for h in range(ng):
        t=(s0,s1,s2,s3)[h][...]
        gv.append(exact(jnp.concatenate([t[:,0:K],t[:,K:2*K]],axis=0),s4))
    gw=jnp.concatenate([gs[pl.ds(lax.rem(base[1]+ng-h,ng),8,stride=ng),:] for h in range(ng)],axis=1)
    gf=mul3(jnp.concatenate(gv,axis=1),masked4(gw))
    fw=jnp.concatenate([fs[pl.ds(u,8,stride=nc),:] for u in range(nc)],axis=1)
    wh,wl=masked4(fw)
    gh,gl=split(gf)
    down=dotnn(gh,wh)+dotnn(gl,wh)+dotnn(gh,wl)
    row=lax.rem(iota((128,K),0),K); col=iota((128,K),1)
    s5=onehot(row==lax.rem(col,8)*4+col//8)
    down=jnp.concatenate([down[:,u*128:(u+1)*128] for u in range(nc)],axis=0)
    down=exact(down,s5)
    row=lax.rem(iota((128,256),0),K); col=iota((128,256),1)
    p1=onehot(row==2*(lax.rem(col,128)//8)+col//128)
    row=iota((K,256),0); col=iota((K,256),1)
    nat=2*(lax.rem(col,128)//8)+col//128
    p2=onehot(row==lax.rem(nat,4)*8+nat//4)
    left=iota((RHS,128),1)<LEAF
    per=n//nc
    for u in range(nc):
        w=jnp.concatenate([ccp[pl.ds(u*64+j,8,stride=8),:] for j in range(8)],axis=1)
        vs=[]
        for j in range(8):
            s=csrc[u,j]
            place=lax.rem(s//nc,2)*(devs//2)+s//(2*nc)
            vs.append(spread4(pays[pl.ds(pl.multiple_of(place*24,8),RHS),:],lax.rem(s,nc)))
        cf=mul3(jnp.concatenate(vs,axis=1),masked4(w))+down[u*RHS:(u+1)*RHS]
        e=jnp.concatenate([tra[pl.ds(((u*per+i)//8)*64+(u*per+i)%8,8,stride=8),:] for i in range(per)],axis=1)
        eh,el=masked4(e)
        ch,cl=split(cf)
        d=dotnn(jnp.concatenate([ch,cl,ch],axis=1),jnp.concatenate([eh,eh,el],axis=0))
        d=jnp.concatenate([d[:,i*128:(i+1)*128] for i in range(per)],axis=0)
        q=exact(d,p1)+exact(lf[pl.ds(u*per*RHS,per*RHS),:],p2)
        for b in range(per//8):
            g=(u*per)//8+b
            z=q[b*128:(b+1)*128].reshape(8,RHS,256)
            z=jnp.stack([z[:,:,:128],z[:,:,128:]],axis=1).reshape(256,128)
            same=(iota((256,128),0)//32==lax.rem(iota((256,128),1),8))
            zh,zl=split(jnp.where(same,z,0.0))
            bh,bl=split(bas[pl.ds(g*128,128),:])
            o=(dotnn(zh,bh)+dotnn(zl,bh)+dotnn(zh,bl)).reshape(8,2,RHS,128)
            for m in range(4):
                a=jnp.where(left,o[2*m,0],o[2*m,1])
                c=jnp.where(left,o[2*m+1,0],o[2*m+1,1])
                r=jnp.where(left,a,c)+pltpu.roll(jnp.where(left,c,a),LEAF,1)
                at=pl.ds(g*512+m*128,128)
                out[:,at]=near_ref[:,at]+r

def down(base,csrc,pays,sums,gcp,ccp,upper,transfer,basis,lf,nearv):
    n=basis.shape[0]; nc=upper.shape[0]; ng=gcp.shape[0]
    bas=basis.reshape(n//8,8,16,128).transpose(0,2,1,3).reshape(n*16,128)
    tra=transfer.reshape(n//8,8,8,128).transpose(0,2,1,3).reshape(n*8,128)
    ccv=ccp.reshape(nc,8,8,128).transpose(0,2,1,3).reshape(nc*64,128)
    vm=pl.BlockSpec(memory_space=pltpu.VMEM)
    return pl.pallas_call(down_kernel,
        out_shape=jax.ShapeDtypeStruct((RHS,n*LEAF),f32),
        in_specs=[pl.BlockSpec(memory_space=pltpu.SMEM)]*2+[vm]*12,
        scratch_shapes=[pltpu.VMEM((8*ng,128),f32),pltpu.VMEM((8*nc,128),f32)],
        compiler_params=pltpu.CompilerParams(vmem_limit_bytes=24<<20),name="down")(base,csrc,pays,*sums,gcp,ccv,upper,tra,bas,lf,nearv)

def across(devs):
    return [[2*i+c for i in range(devs//2)] for c in range(2)]

def per_device(right_sides,near_blocks,near_source,near_count,basis,leaf_source,leaf_coupling,leaf_transfer,cluster_source,cluster_coupling,cluster_transfer,group_coupling):
    both=("group","leaf")
    leaves=near_blocks.shape[0]
    devs=lax.axis_size("leaf")
    every=lax.axis_size(both)
    ng=lax.axis_size("group")
    base=jnp.stack([(lax.axis_index(both)-1)*leaves,lax.axis_index("group")]).astype(jnp.int32)
    ext,rep=up(right_sides,basis,leaf_transfer,cluster_transfer,devs//2)
    some=lax.all_to_all(rep.reshape(devs//2,24,128),"leaf",0,0,tiled=True,axis_index_groups=across(devs))
    eb=lax.ppermute(ext,both,[(i,i+1) for i in range(every-1)])
    ea=lax.ppermute(ext,both,[(i+1,i) for i in range(every-1)])
    nearv=near(base,near_source,near_count,eb,ext,ea,near_blocks)
    some,nearv=lax.optimization_barrier((some,nearv))
    pays=lax.all_gather(some,"leaf",axis=0,tiled=True,axis_index_groups=[[2*i,2*i+1] for i in range(devs//2)])
    total=pays[:,RHS:,:].sum(axis=0)
    sums=[total]+[lax.ppermute(total,"group",[(i,(i+k)%ng) for i in range(ng)]) for k in range(1,ng)]
    base2,_=lax.optimization_barrier((base,total))
    lf=far(base2,leaf_source,eb,ext,ea,leaf_coupling)
    return down(base,cluster_source,pays.reshape(devs*24,128),sums,group_coupling.reshape(-1,1024),cluster_coupling,cluster_transfer,leaf_transfer,basis,lf,nearv)

def solution(mesh):
    both=("group","leaf")
    one=P(both)
    two=P(both,None)
    three=P(both,None,None)
    return jax.shard_map(per_device,mesh=mesh,
        in_specs=(P(None,both),three,two,one,two,two,three,two,two,three,two,P("group",None,None)),
        out_specs=P(None,both),check_vma=False)
```

time: 87.6 us -> 65.2 us (0.74)
  the two profiles are of different devices: /device:TPU:2 before, /device:TPU:1 now
where the time goes in v2:
time: 65.2 us; the launch traced here: 64.6 us
  starting transfers between devices  29.1 us (45%)
  Pallas kernels  26.1 us (40%)
  waiting for transfers between devices  6.64 us (10%)
  blocking collectives  2.37 us (4%)
    all_to_all x1, starting transfers between devices, per_device(): lax.all_to_all(rep.reshape(devs // 2, 24, 128), 'leaf', 0, 0, tiled=True,...  12 us
    ppermute x3, starting transfers between devices, per_device(): lax.ppermute(total, 'group', [(i, (i + k) % ng) for i in range(ng)])  10.9 us
    pallas_call x1, Pallas kernels, near(): pl.pallas_call(functools.partial(near_kernel, var), out_shape=jax.ShapeDt...  8.62 us
    ppermute x1, waiting for transfers between devices, per_device(): ea = lax.ppermute(ext, both, [(i + 1, i) for i in range(every - 1)])  6.63 us
    pallas_call x1, Pallas kernels, far(): pl.pallas_call(far_kernel, out_shape=jax.ShapeDtypeStruct((n * RHS, K), f...  6.22 us
    pallas_call x1, Pallas kernels, up(): pl.pallas_call(up_kernel, out_shape=(jax.ShapeDtypeStruct((RHS, n * (LEAF...  5.7 us
    pallas_call x1, Pallas kernels, down(): pl.pallas_call(down_kernel, out_shape=jax.ShapeDtypeStruct((RHS, n * LEAF...  5.59 us
    ppermute x1, starting transfers between devices, per_device(): eb = lax.ppermute(ext, both, [(i, i + 1) for i in range(every - 1)])  3.32 us
  transfers between devices with their start and end apart: 6, of which 1 were waited for; matrix products, arithmetic and copies ran while one was open for 0% of the time, Pallas kernels for 23%

profile of v2, /device:TPU:1, one launch (start us, length us, event | category | flops | bytes accessed | tf_op | source)
XLA Modules:
  0.0 64.6 jit_solution(15969704366205768280)
XLA Ops:
  0.0 0.0 copy-start.3
  0.0 0.0 copy-start.4
  0.0 0.0 copy-start.5
  0.0 5.7 %up.1 = (f32[16,6144]{1,0:T(8,128)S(1)}, f32[768,128]{1,0:T(8,128)}) custom-call(f32[16,4096]{1,0:T(8,128)} %x_h.1, f32[1024,128]{1,0:T(8,128)} %bitcast.33, f32[512,128]{1,0:T(8,128)} %bitcast.35, f32[4,1024]{1,0:T(4,128)} %upt.1), custom_call_target="tpu_custom_call" | custom-call | tf_op jit(solution)/shard_map/up/pallas_call | solution.py:185
  5.8 12.0 %all-to-all-start = ((f32[32,24,128]{2,1,0:T(8,128)}), f32[32,24,128]{2,1,0:T(8,128)S(1)}, u32[]{:S(2)}, u32[]{:S(2)}) async-start(f32[32,24,128]{2,1,0:T(8,128)} %bitcast.8), calls=%async_computation | async-start | bytes 786432 | tf_op jit(solution)/shard_map/all_to_all | solution.py:322
  17.8 2.9 %collective-permute-start.1 = (f32[16,6144]{1,0:T(8,128)S(1)}, f32[16,6144]{1,0:T(8,128)S(1)}, u32[]{:S(2)}, u32[]{:S(2)}) collective-permute-start(f32[16,6144]{1,0:T(8,128)S(1)} %get-tuple-element.11.xo.co), channel_id=1, source_target_pairs={{1,0},{2,1},{3,2},{4,3},{5,4},{6,5},{7,6},{8,7},{9,8},{10,9},{11,1... | collective-permute-start | bytes 1179656 | tf_op jit(solution)/shard_map/ppermute | solution.py:324
  20.7 3.3 %collective-permute-start = (f32[16,6144]{1,0:T(8,128)S(1)}, f32[16,6144]{1,0:T(8,128)S(1)}, u32[]{:S(2)}, u32[]{:S(2)}) collective-permute-start(f32[16,6144]{1,0:T(8,128)S(1)} %get-tuple-element.11.xo.co), channel_id=1, source_target_pairs={{0,1},{1,2},{2,3},{3,4},{4,5},{5,6},{6,7},{7,8},{8,9},{9,10},{10,1... | collective-permute-start | bytes 1179656 | tf_op jit(solution)/shard_map/ppermute | solution.py:323
  24.0 0.1 pad_add_fusion.base
  24.1 6.6 %collective-permute-done.1.xa.ca = f32[16,6144]{1,0:T(8,128)S(1)} collective-permute-done((f32[16,6144]{1,0:T(8,128)S(1)}, f32[16,6144]{1,0:T(8,128)S(1)}, u32[]{:S(2)}, u32[]{:S(2)}) %collective-permute-start.1) | collective-permute-done | bytes 393248 | tf_op jit(solution)/shard_map/ppermute | solution.py:324
  30.7 0.0 collective-permute-done.xb.cb
  30.7 8.6 %near.1.near_ref = f32[16,4096]{1,0:T(8,128)S(1)} custom-call(s32[2]{0:T(128)S(1)} %pad_add_fusion.base, s32[8,64]{1,0:T(8,128)} %bitcast.41, s32[64]{0:T(128)} %cnt_h.1, f32[16384,128]{1,0:T(8,128)} %bitcast.39, f32[16,6144]{1,0:T(8,128)S(1)} %collective-permute-done.xb.cb, f32[16,6144]{1,0:T(8,128)S(1)} %get-tuple-element.11.xo.co, ...), custom_call_target="tpu_custom_call" | custom-call | tf_op jit(solution)/shard_map/near/pallas_call | solution.py:105
  39.3 0.0 all-to-all-done
  39.4 2.4 %all_gather.3 = f32[64,24,128]{2,1,0:T(8,128)S(1)} all-gather(f32[32,24,128]{2,1,0:T(8,128)S(1)} %all-to-all-done), channel_id=1, replica_groups={{0,1},{2,3},{4,5},{6,7},{8,9},{10,11},{12,13},{14,15},{16,17},{18,19},{..., dimensions={0}, use_global_device_ids=true | all-gather | bytes 1179648 | tf_op jit(solution)/shard_map/all_gather | solution.py:327
  41.7 0.1 slice_reduce_fusion.s0
  41.8 10.0 %collective-permute-start.4 = (f32[8,128]{1,0:T(8,128)S(1)}, f32[8,128]{1,0:T(8,128)S(1)}, u32[]{:S(2)}, u32[]{:S(2)}) collective-permute-start(f32[8,128]{1,0:T(8,128)S(1)} %slice_reduce_fusion.s0), channel_id=1, source_target_pairs={{0,192},{64,0},{128,64},{192,128},{1,193},{65,1},{129,65},{193,129... | collective-permute-start | bytes 12296 | tf_op jit(solution)/shard_map/ppermute | solution.py:329
  51.8 0.2 collective-permute-start.3
  52.1 0.6 collective-permute-start.2
  52.7 6.2 %far.1.lf = f32[1024,32]{1,0:T(8,128)S(1)} custom-call(s32[2]{0:T(128)S(1)} %pad_add_fusion.base, s32[8,64]{1,0:T(8,128)} %bitcast.42, f32[4096,128]{1,0:T(8,128)} %bitcast.40, f32[16,6144]{1,0:T(8,128)S(1)} %collective-permute-done.xb.cb, f32[16,6144]{1,0:T(8,128)S(1)} %get-tuple-element.11.xo.co, f32[16,6144]{1,0:T(8,128)S(1)} %collective-permute-done.1.xa.ca), custom_call_target="tpu_custom_call" | custom-call | tf_op jit(solution)/shard_map/far/pallas_call | solution.py:232
  58.9 0.0 collective-permute-done.4.s3
  58.9 0.0 collective-permute-done.3.s2
  58.9 0.0 collective-permute-done.2.s1
  58.9 0.0 copy-done
  58.9 0.0 copy-done.1
  59.0 5.6 %down.1 = f32[16,4096]{1,0:T(8,128)} custom-call(s32[2]{0:T(128)S(1)} %pad_add_fusion.base, s32[4,8]{1,0:T(4,128)S(1)} %copy-done.5, f32[1536,128]{1,0:T(8,128)S(1)} %bitcast.32, f32[8,128]{1,0:T(8,128)S(1)} %slice_reduce_fusion.s0, f32[8,128]{1,0:T(8,128)S(1)} %collective-permute-done.2.s1, f32[8,128]{1,0:T(8,128)S(1)} %collective-permute-done.3.s2, ...), custom_call_target="tpu_custom_call" | custom-call | tf_op jit(solution)/shard_map/down/pallas_call | solution.py:305
  (7 shorter events, 0.0 us)
Async XLA Ops:
  0.0 58.9 %copy-start = (f32[64,2048]{1,0:T(8,128)S(1)}, f32[64,2048]{1,0:T(8,128)}, u32[]{:S(2)}) copy-start(f32[64,2048]{1,0:T(8,128)} %param.16) | copy-start | bytes 1572868
  0.0 58.9 %copy-start.1 = (f32[64,1024]{1,0:T(8,128)S(1)}, f32[64,1024]{1,0:T(8,128)}, u32[]{:S(2)}) copy-start(f32[64,1024]{1,0:T(8,128)} %param.19) | copy-start | bytes 786436
  0.0 58.9 %copy-start.2 = (f32[4,8,1024]{2,1,0:T(8,128)S(1)}, f32[4,8,1024]{2,1,0:T(8,128)}, u32[]{:S(2)}) copy-start(f32[4,8,1024]{2,1,0:T(8,128)} %param.21) | copy-start | bytes 393220
  0.0 59.0 %copy-start.3 = (f32[4,1024]{1,0:T(4,128)S(1)}, f32[4,1024]{1,0:T(4,128)}, u32[]{:S(2)}) copy-start(f32[4,1024]{1,0:T(4,128)} %upt.1) | copy-start | bytes 49156
  0.0 59.0 %copy-start.4 = (f32[1,4,1024]{2,1,0:T(4,128)S(1)}, f32[1,4,1024]{2,1,0:T(4,128)}, u32[]{:S(2)}) copy-start(f32[1,4,1024]{2,1,0:T(4,128)} %param.23) | copy-start | bytes 49156
  0.0 59.0 %copy-start.5 = (s32[4,8]{1,0:T(4,128)S(1)}, s32[4,8]{1,0:T(4,128)}, u32[]{:S(2)}) copy-start(s32[4,8]{1,0:T(4,128)} %csrc.1) | copy-start | bytes 388
  5.8 33.6 %all-to-all-start = ((f32[32,24,128]{2,1,0:T(8,128)}), f32[32,24,128]{2,1,0:T(8,128)S(1)}, u32[]{:S(2)}, u32[]{:S(2)}) async-start(f32[32,24,128]{2,1,0:T(8,128)} %bitcast.8), calls=%async_computation | async-start | bytes 786432 | tf_op jit(solution)/shard_map/all_to_all | solution.py:322
  17.8 12.9 %collective-permute-start.1 = (f32[16,6144]{1,0:T(8,128)S(1)}, f32[16,6144]{1,0:T(8,128)S(1)}, u32[]{:S(2)}, u32[]{:S(2)}) collective-permute-start(f32[16,6144]{1,0:T(8,128)S(1)} %get-tuple-element.11.xo.co), channel_id=1, source_target_pairs={{1,0},{2,1},{3,2},{4,3},{5,4},{6,5},{7,6},{8,7},{9,8},{10,9},{11,1... | collective-permute-start | bytes 1179656 | tf_op jit(solution)/shard_map/ppermute | solution.py:324
  20.7 10.0 %collective-permute-start = (f32[16,6144]{1,0:T(8,128)S(1)}, f32[16,6144]{1,0:T(8,128)S(1)}, u32[]{:S(2)}, u32[]{:S(2)}) collective-permute-start(f32[16,6144]{1,0:T(8,128)S(1)} %get-tuple-element.11.xo.co), channel_id=1, source_target_pairs={{0,1},{1,2},{2,3},{3,4},{4,5},{5,6},{6,7},{7,8},{8,9},{9,10},{10,1... | collective-permute-start | bytes 1179656 | tf_op jit(solution)/shard_map/ppermute | solution.py:323
  41.8 17.1 %collective-permute-start.4 = (f32[8,128]{1,0:T(8,128)S(1)}, f32[8,128]{1,0:T(8,128)S(1)}, u32[]{:S(2)}, u32[]{:S(2)}) collective-permute-start(f32[8,128]{1,0:T(8,128)S(1)} %slice_reduce_fusion.s0), channel_id=1, source_target_pairs={{0,192},{64,0},{128,64},{192,128},{1,193},{65,1},{129,65},{193,129... | collective-permute-start | bytes 12296 | tf_op jit(solution)/shard_map/ppermute | solution.py:329
  51.8 7.1 %collective-permute-start.3 = (f32[8,128]{1,0:T(8,128)S(1)}, f32[8,128]{1,0:T(8,128)S(1)}, u32[]{:S(2)}, u32[]{:S(2)}) collective-permute-start(f32[8,128]{1,0:T(8,128)S(1)} %slice_reduce_fusion.s0), channel_id=1, source_target_pairs={{0,128},{64,192},{128,0},{192,64},{1,129},{65,193},{129,1},{193,65... | collective-permute-start | bytes 12296 | tf_op jit(solution)/shard_map/ppermute | solution.py:329
  52.1 6.9 %collective-permute-start.2 = (f32[8,128]{1,0:T(8,128)S(1)}, f32[8,128]{1,0:T(8,128)S(1)}, u32[]{:S(2)}, u32[]{:S(2)}) collective-permute-start(f32[8,128]{1,0:T(8,128)S(1)} %slice_reduce_fusion.s0), channel_id=1, source_target_pairs={{0,64},{64,128},{128,192},{192,0},{1,65},{65,129},{129,193},{193,1... | collective-permute-start | bytes 12296 | tf_op jit(solution)/shard_map/ppermute | solution.py:329

commit v3 on v2

--- a/solution.py
+++ b/solution.py
@@ -39,9 +39,9 @@
     ca=pltpu.make_async_copy(src_h,src,sem2.at[0]); cb=pltpu.make_async_copy(cnt_h,cnt,sem2.at[1])
     ca.start(); cb.start()
     for c in range(chunks): chunk(c).start()
-    point_table(xb,0,n,hi,lo)
     point_table(xo,n,n,hi,lo)
-    point_table(xa,2*n,n,hi,lo)
+    point_table(xb,base[2]*n,n,hi,lo)
+    point_table(xa,(2-base[2])*n,n,hi,lo)
     hi[3*n]=jnp.zeros((RHS,128),bf16)
     lo[3*n]=jnp.zeros((RHS,128),bf16)
     row=lax.broadcasted_iota(jnp.int32,(256,256),0)
@@ -108,6 +108,7 @@
         out_specs=blk,
         scratch_shapes=[pltpu.VMEM((3*leaves+1,RHS,128),bf16)]*2+[pltpu.VMEM((256,256),bf16),pltpu.VMEM((leaves*256,128),f32),
             pltpu.SMEM((8,leaves),jnp.int32),pltpu.SMEM((leaves,),jnp.int32),pltpu.SemaphoreType.DMA((chunks,)),pltpu.SemaphoreType.DMA((2,))],
+        cost_estimate=pl.CostEstimate(flops=10**11,bytes_accessed=10**7,transcendentals=0),
         compiler_params=pltpu.CompilerParams(vmem_limit_bytes=24<<20),
         name="near")(base,in_hbm(src.T),in_hbm(cnt),in_hbm(view),xb,xo,xa)
 
@@ -121,30 +122,41 @@
     block=block+pltpu.roll(block,64,1)
     return block+pltpu.roll(block,32,1)
 def masked4(rows):
-    lane=lax.rem(iota(rows.shape,1),128)//K
-    both=jnp.concatenate([jnp.where(lane==m,rows,0.0) for m in range(4)],axis=0)
-    return split(both)
+    n=rows.shape[1]//128
+    lane=iota((16,128),1)//K
+    half=iota((16,128),0)//8
+    keep=[onehot(lane==half+2*p) for p in range(2)]
+    h=rows.astype(bf16).astype(f32)
+    out=[]
+    for v in (h,rows-h):
+        w=jnp.concatenate([v,v],axis=0).astype(bf16)
+        out.append(jnp.concatenate([w*jnp.concatenate([m]*n,axis=1) for m in keep],axis=0))
+    return out
+
 def mul3(v,w):
     h,l=split(v)
     d=dotnt(jnp.concatenate([h,l],axis=0),w[0])
     return d[:RHS]+d[RHS:]+dotnt(h,w[1])
 
-def up_kernel(x_h,bas_h,tra_h,upt_h,ext,rep,fs,x,bas,tra,upt,sem):
-    moves=[pltpu.make_async_copy(s,d,sem.at[i]) for i,(s,d) in enumerate(((x_h,x),(bas_h,bas),(tra_h,tra),(upt_h,upt)))]
-    for m in moves: m.start()
+def up_kernel(x_h,bas_h,tra_h,upt_h,ext,tra,upt,x,bas,sem,sem2):
+    chunks=sem.shape[0]-1
+    size=bas.shape[0]//chunks
+    first=pltpu.make_async_copy(x_h,x,sem.at[chunks])
+    moves=[pltpu.make_async_copy(bas_h.at[pl.ds(c*size,size),:],bas.at[pl.ds(c*size,size),:],sem.at[c]) for c in range(chunks)]
+    later=[pltpu.make_async_copy(tra_h,tra,sem2.at[0]),pltpu.make_async_copy(upt_h,upt,sem2.at[1])]
+    first.start()
+    for m in moves+later: m.start()
     pts=x.shape[1]
-    lane=iota((RHS,128),1)
-    left=lane<LEAF
-    n=x.shape[1]//LEAF
+    n=pts//LEAF
+    left=iota((RHS,128),1)<LEAF
     row=iota((256,256),0); col=iota((256,256),1)
     k2=lax.rem(row,128)//8
     s2=onehot(col==lax.rem(row,8)*32+2*k2+row//128)
     same=(iota((256,128),0)//32==lax.rem(iota((256,128),1),8))
-    v4=[]
-    moves[0].wait()
-    moves[1].wait()
+    first.wait()
     ext[:,:pts]=x[...]
     for g in range(n//8):
+        if g*128%size==0: moves[g*128//size].wait()
         blks=[]
         for q in range(4):
             t=x[:,pl.ds((g*4+q)*128,128)]
@@ -155,18 +167,29 @@
         bh,bl=split(bas[pl.ds(g*128,128),:])
         d=dotnt(xh,bh)+dotnt(xl,bh)+dotnt(xh,bl)
         d=jnp.where(same,d,0.0).reshape(8,32,128).sum(axis=0)
-        c=exact(jnp.concatenate([d[:RHS],d[RHS:]],axis=1),s2)
-        ext[:,pl.ds(pts+g*256,256)]=c
-        for i in range(8):
-            v4.append(spread4(c[:,(i//4)*128:(i//4)*128+128],i%4))
+        ext[:,pl.ds(pts+g*256,256)]=exact(jnp.concatenate([d[:RHS],d[RHS:]],axis=1),s2)
+    for m in later: m.wait()
+
+def up(x,basis,transfer,upper,chunks=2):
+    n=basis.shape[0]
+    tra=transfer.reshape(n//8,8,8,128).transpose(0,2,1,3).reshape(n*8,128)
+    bas=basis.reshape(n//8,8,16,128).transpose(0,2,1,3).reshape(n*16,128)
+    return pl.pallas_call(up_kernel,
+        out_shape=(jax.ShapeDtypeStruct((RHS,n*(LEAF+K)),f32),jax.ShapeDtypeStruct(tra.shape,f32),jax.ShapeDtypeStruct(upper.shape,f32)),
+        in_specs=[pl.BlockSpec(memory_space=HBM)]*4,
+        scratch_shapes=[pltpu.VMEM(x.shape,f32),pltpu.VMEM(bas.shape,f32),pltpu.SemaphoreType.DMA((chunks+1,)),pltpu.SemaphoreType.DMA((2,))],
+        compiler_params=pltpu.CompilerParams(vmem_limit_bytes=24<<20),name="up")(in_hbm(x),in_hbm(bas),in_hbm(tra),in_hbm(upper))
+
+def lift_kernel(ext,tra,upt,rep,fs):
     nc=upt.shape[0]
+    n=tra.shape[0]//8
     per=n//nc
-    moves[2].wait()
-    moves[3].wait()
+    pts=n*LEAF
     outs=[]
     for u in range(nc):
         e=jnp.concatenate([tra[pl.ds(((u*per+i)//8)*64+(u*per+i)%8,8,stride=8),:] for i in range(per)],axis=1)
-        outs.append(mul3(jnp.concatenate(v4[u*per:(u+1)*per],axis=1),masked4(e)))
+        v=[spread4(ext[:,pl.ds(pts+(u*per+i)//4*128,128)],i%4) for i in range(per)]
+        outs.append(mul3(jnp.concatenate(v,axis=1),masked4(e)))
     row=iota((128,128),0); col=iota((128,128),1)
     s3=onehot(col==row//32*32+lax.rem(row,8)*4+lax.rem(row,32)//8)
     cc=exact(jnp.concatenate(outs,axis=1),s3)
@@ -177,16 +200,12 @@
     pay=jnp.concatenate([cc,jnp.concatenate([pr[0:8],pr[8:16],jnp.zeros((8,64),f32)],axis=1)],axis=0)
     for c in range(rep.shape[0]//24): rep[pl.ds(c*24,24),:]=pay
 
-def up(x,basis,transfer,upper,copies):
-    n=basis.shape[0]
-    bas=basis.reshape(n//8,8,16,128).transpose(0,2,1,3).reshape(n*16,128)
-    tra=transfer.reshape(n//8,8,8,128).transpose(0,2,1,3).reshape(n*8,128)
-    args=(x,bas,tra,upper)
-    return pl.pallas_call(up_kernel,
-        out_shape=(jax.ShapeDtypeStruct((RHS,n*(LEAF+K)),f32),jax.ShapeDtypeStruct((copies*24,128),f32)),
-        in_specs=[pl.BlockSpec(memory_space=HBM)]*4,
-        scratch_shapes=[pltpu.VMEM((8*upper.shape[0],128),f32)]+[pltpu.VMEM(v.shape,f32) for v in args]+[pltpu.SemaphoreType.DMA((4,))],
-        compiler_params=pltpu.CompilerParams(vmem_limit_bytes=24<<20),name="up")(*[in_hbm(v) for v in args])
+def lift(ext,tra,upper,copies):
+    return pl.pallas_call(lift_kernel,
+        out_shape=jax.ShapeDtypeStruct((copies*24,128),f32),
+        in_specs=[pl.BlockSpec(memory_space=pltpu.VMEM)]*3,
+        scratch_shapes=[pltpu.VMEM((8*upper.shape[0],128),f32)],
+        compiler_params=pltpu.CompilerParams(vmem_limit_bytes=24<<20),name="lift")(ext,tra,upper)
 
 def far_kernel(base,src_h,cpl_h,cb,co,ca,out,hi,lo,cpl,src,sem,sem2):
     tiles=co.shape[1]//128
@@ -197,7 +216,7 @@
     idx=pltpu.make_async_copy(src_h,src,sem2.at[0])
     idx.start()
     for c in range(chunks): chunk(c).start()
-    for w,ref in enumerate((cb,co,ca)):
+    for w,ref in ((base[2],cb),(1,co),(2-base[2],ca)):
         def body(q,_):
             t=ref[:,pl.ds(pl.multiple_of(q*128,128),128)]
             for m in range(4):
@@ -296,10 +315,9 @@
                 at=pl.ds(g*512+m*128,128)
                 out[:,at]=near_ref[:,at]+r
 
-def down(base,csrc,pays,sums,gcp,ccp,upper,transfer,basis,lf,nearv):
+def down(base,csrc,pays,sums,gcp,ccp,upper,tra,basis,lf,nearv):
     n=basis.shape[0]; nc=upper.shape[0]; ng=gcp.shape[0]
     bas=basis.reshape(n//8,8,16,128).transpose(0,2,1,3).reshape(n*16,128)
-    tra=transfer.reshape(n//8,8,8,128).transpose(0,2,1,3).reshape(n*8,128)
     ccv=ccp.reshape(nc,8,8,128).transpose(0,2,1,3).reshape(nc*64,128)
     vm=pl.BlockSpec(memory_space=pltpu.VMEM)
     return pl.pallas_call(down_kernel,
@@ -317,11 +335,12 @@
     devs=lax.axis_size("leaf")
     every=lax.axis_size(both)
     ng=lax.axis_size("group")
-    base=jnp.stack([(lax.axis_index(both)-1)*leaves,lax.axis_index("group")]).astype(jnp.int32)
-    ext,rep=up(right_sides,basis,leaf_transfer,cluster_transfer,devs//2)
+    base=jnp.stack([(lax.axis_index(both)-1)*leaves,lax.axis_index("group"),2*lax.rem(lax.axis_index("leaf")+1,2)]).astype(jnp.int32)
+    ext,tra,upper=up(right_sides,basis,leaf_transfer,cluster_transfer)
+    eb=lax.ppermute(ext,both,[(i,i^1) for i in range(every)])
+    ea=lax.ppermute(ext,both,[p for i in range(1,every-1,2) for p in ((i,i+1),(i+1,i))])
+    rep=lift(ext,tra,upper,devs//2)
     some=lax.all_to_all(rep.reshape(devs//2,24,128),"leaf",0,0,tiled=True,axis_index_groups=across(devs))
-    eb=lax.ppermute(ext,both,[(i,i+1) for i in range(every-1)])
-    ea=lax.ppermute(ext,both,[(i+1,i) for i in range(every-1)])
     nearv=near(base,near_source,near_count,eb,ext,ea,near_blocks)
     some,nearv=lax.optimization_barrier((some,nearv))
     pays=lax.all_gather(some,"leaf",axis=0,tiled=True,axis_index_groups=[[2*i,2*i+1] for i in range(devs//2)])
@@ -329,7 +348,7 @@
     sums=[total]+[lax.ppermute(total,"group",[(i,(i+k)%ng) for i in range(ng)]) for k in range(1,ng)]
     base2,_=lax.optimization_barrier((base,total))
     lf=far(base2,leaf_source,eb,ext,ea,leaf_coupling)
-    return down(base,cluster_source,pays.reshape(devs*24,128),sums,group_coupling.reshape(-1,1024),cluster_coupling,cluster_transfer,leaf_transfer,basis,lf,nearv)
+    return down(base,cluster_source,pays.reshape(devs*24,128),sums,group_coupling.reshape(-1,1024),cluster_coupling,upper,tra,basis,lf,nearv)
 
 def solution(mesh):
     both=("group","leaf")

time: 65.2 us -> 55.6 us (0.85)
  starting transfers between devices: 29.1 us -> 19.3 us
  blocking collectives: 2.37 us -> 4.47 us
  waiting for transfers between devices: 6.64 us -> 5.05 us
    ppermute x3, starting transfers between devices: 10.9 us -> 3.68 us  [per_device(): lax.ppermute(total, 'group', [(i, (i + k) % ng) for i in range(ng)])]
    ppermute x2, waiting for transfers between devices: 6.63 us -> 0.01 us  [the longest x1 0.01 us: per_device(): lax.ppermute(ext, both, [p for i in range(1, every - 1, 2) for p in ((i,...]
    all_to_all x1, waiting for transfers between devices: 0.01 us -> 5.03 us  [per_device(): lax.all_to_all(rep.reshape(devs // 2, 24, 128), 'leaf', 0, 0, tiled=True,...]
    all_gather x1, blocking collectives: 2.37 us -> 4.47 us  [per_device(): lax.all_gather(some, 'leaf', axis=0, tiled=True, axis_index_groups=[[2 *...]
    pallas_call x0 -> x1, Pallas kernels: none -> 2.06 us  [lift(): pl.pallas_call(lift_kernel, out_shape=jax.ShapeDtypeStruct((copies * 24,...]
    pallas_call x1, Pallas kernels: 5.7 us -> 3.71 us  [up(): pl.pallas_call(up_kernel, out_shape=(jax.ShapeDtypeStruct((RHS, n * (LEAF...]
    ppermute x2, starting transfers between devices: 6.18 us -> 4.69 us  [the longest x1 4.59 us: per_device(): lax.ppermute(ext, both, [p for i in range(1, every - 1, 2) for p in ((i,...]
    all_to_all x1, starting transfers between devices: 12 us -> 10.9 us  [per_device(): lax.all_to_all(rep.reshape(devs // 2, 24, 128), 'leaf', 0, 0, tiled=True,...]
  transfers between devices with their start and end apart: 6 -> 6, of which waited for: 1 -> 1; matrix products, arithmetic and copies ran while one was open for 0% -> 0% of each run, Pallas kernels for 23% -> 31%
where the time goes in v3:
time: 55.6 us; the launch traced here: 55.4 us
  Pallas kernels  26.3 us (47%)
  starting transfers between devices  19.3 us (35%)
  waiting for transfers between devices  5.05 us (9%)
  blocking collectives  4.47 us (8%)
    all_to_all x1, starting transfers between devices, per_device(): lax.all_to_all(rep.reshape(devs // 2, 24, 128), 'leaf', 0, 0, tiled=True,...  10.9 us
    pallas_call x1, Pallas kernels, near(): pl.pallas_call(functools.partial(near_kernel, var), out_shape=jax.ShapeDt...  8.62 us
    pallas_call x1, Pallas kernels, far(): pl.pallas_call(far_kernel, out_shape=jax.ShapeDtypeStruct((n * RHS, K), f...  6.3 us
    pallas_call x1, Pallas kernels, down(): pl.pallas_call(down_kernel, out_shape=jax.ShapeDtypeStruct((RHS, n * LEAF...  5.58 us
    all_to_all x1, waiting for transfers between devices, per_device(): lax.all_to_all(rep.reshape(devs // 2, 24, 128), 'leaf', 0, 0, tiled=True,...  5.03 us
    ppermute x1, starting transfers between devices, per_device(): lax.ppermute(ext, both, [p for i in range(1, every - 1, 2) for p in ((i,...  4.59 us
    all_gather x1, blocking collectives, per_device(): lax.all_gather(some, 'leaf', axis=0, tiled=True, axis_index_groups=[[2 *...  4.47 us
    pallas_call x1, Pallas kernels, up(): pl.pallas_call(up_kernel, out_shape=(jax.ShapeDtypeStruct((RHS, n * (LEAF...  3.71 us
  transfers between devices with their start and end apart: 6, of which 1 were waited for; matrix products, arithmetic and copies ran while one was open for 0% of the time, Pallas kernels for 31%

profile of v3, /device:TPU:1, one launch (start us, length us, event | category | flops | bytes accessed | tf_op | source)
XLA Modules:
  0.0 55.4 jit_solution(14025777543565955255)
XLA Ops:
  0.0 3.7 %up.1 = (f32[16,6144]{1,0:T(8,128)S(1)}, f32[512,128]{1,0:T(8,128)S(1)}, f32[4,1024]{1,0:T(4,128)S(1)}) custom-call(f32[16,4096]{1,0:T(8,128)} %x_h.1, f32[1024,128]{1,0:T(8,128)} %bitcast.34, f32[512,128]{1,0:T(8,128)} %bitcast.39, f32[4,1024]{1,0:T(4,128)} %upt_h.1), custom_call_target="tpu_custom_call" | custom-call | tf_op jit(solution)/shard_map/up/pallas_call | solution.py:177
  3.7 4.6 %collective-permute-start.1 = (f32[16,6144]{1,0:T(8,128)S(1)}, f32[16,6144]{1,0:T(8,128)S(1)}, u32[]{:S(2)}, u32[]{:S(2)}) collective-permute-start(f32[16,6144]{1,0:T(8,128)S(1)} %get-tuple-element.11.ext.xo.co), channel_id=1, source_target_pairs={{1,2},{2,1},{3,4},{4,3},{5,6},{6,5},{7,8},{8,7},{9,10},{10,9},{11,... | collective-permute-start | bytes 1179656 | tf_op jit(solution)/shard_map/ppermute | solution.py:341
  8.3 0.1 collective-permute-start
  8.4 2.1 %lift.1 = f32[768,128]{1,0:T(8,128)} custom-call(f32[16,6144]{1,0:T(8,128)S(1)} %get-tuple-element.11.ext.xo.co, f32[512,128]{1,0:T(8,128)S(1)} %get-tuple-element.12.tra, f32[4,1024]{1,0:T(4,128)S(1)} %get-tuple-element.13.upt), custom_call_target="tpu_custom_call" | custom-call | tf_op jit(solution)/shard_map/lift/pallas_call | solution.py:204
  10.5 10.9 %all-to-all-start = ((f32[32,24,128]{2,1,0:T(8,128)}), f32[32,24,128]{2,1,0:T(8,128)S(1)}, u32[]{:S(2)}, u32[]{:S(2)}) async-start(f32[32,24,128]{2,1,0:T(8,128)} %bitcast.9), calls=%async_computation | async-start | bytes 786432 | tf_op jit(solution)/shard_map/all_to_all | solution.py:343
  21.4 0.1 pad_add_fusion.base
  21.5 0.0 collective-permute-done.1.xa.ca
  21.5 0.0 collective-permute-done.xb.cb
  21.5 0.0 copy-start.1
  21.5 0.0 copy-start.2
  21.5 0.0 copy-start.3
  21.5 8.6 %near.1.near_ref = f32[16,4096]{1,0:T(8,128)S(1)} custom-call(s32[3]{0:T(128)S(1)} %pad_add_fusion.base, s32[8,64]{1,0:T(8,128)} %bitcast.42, s32[64]{0:T(128)} %cnt_h.1, f32[16384,128]{1,0:T(8,128)} %bitcast.41, f32[16,6144]{1,0:T(8,128)S(1)} %collective-permute-done.xb.cb, f32[16,6144]{1,0:T(8,128)S(1)} %get-tuple-element.11.ext.xo.co, ...), custom_call_target="tpu_custom_call" | custom-call | flops 99999997952 | bytes 10000000 | tf_op jit(solution)/shard_map/near/pallas_call | solution.py:105
  30.2 5.0 %all-to-all-done = f32[32,24,128]{2,1,0:T(8,128)S(1)} async-done(((f32[32,24,128]{2,1,0:T(8,128)}), f32[32,24,128]{2,1,0:T(8,128)S(1)}, u32[]{:S(2)}, u32[]{:S(2)}) %all-to-all-start) | async-done | bytes 393248 | tf_op jit(solution)/shard_map/all_to_all | solution.py:343
  35.2 4.5 %all_gather.3 = f32[64,24,128]{2,1,0:T(8,128)S(1)} all-gather(f32[32,24,128]{2,1,0:T(8,128)S(1)} %all-to-all-done), channel_id=1, replica_groups={{0,1},{2,3},{4,5},{6,7},{8,9},{10,11},{12,13},{14,15},{16,17},{18,19},{..., dimensions={0}, use_global_device_ids=true | all-gather | bytes 1179648 | tf_op jit(solution)/shard_map/all_gather | solution.py:346
  39.7 0.1 slice_reduce_fusion.s0
  39.7 2.5 %collective-permute-start.4 = (f32[8,128]{1,0:T(8,128)S(1)}, f32[8,128]{1,0:T(8,128)S(1)}, u32[]{:S(2)}, u32[]{:S(2)}) collective-permute-start(f32[8,128]{1,0:T(8,128)S(1)} %slice_reduce_fusion.s0), channel_id=1, source_target_pairs={{0,192},{64,0},{128,64},{192,128},{1,193},{65,1},{129,65},{193,129... | collective-permute-start | bytes 12296 | tf_op jit(solution)/shard_map/ppermute | solution.py:348
  42.3 0.5 collective-permute-start.3
  42.8 0.6 %collective-permute-start.2 = (f32[8,128]{1,0:T(8,128)S(1)}, f32[8,128]{1,0:T(8,128)S(1)}, u32[]{:S(2)}, u32[]{:S(2)}) collective-permute-start(f32[8,128]{1,0:T(8,128)S(1)} %slice_reduce_fusion.s0), channel_id=1, source_target_pairs={{0,64},{64,128},{128,192},{192,0},{1,65},{65,129},{129,193},{193,1... | collective-permute-start | bytes 12296 | tf_op jit(solution)/shard_map/ppermute | solution.py:348
  43.4 6.3 %far.1.lf = f32[1024,32]{1,0:T(8,128)S(1)} custom-call(s32[3]{0:T(128)S(1)} %pad_add_fusion.base, s32[8,64]{1,0:T(8,128)} %bitcast.40, f32[4096,128]{1,0:T(8,128)} %bitcast.38, f32[16,6144]{1,0:T(8,128)S(1)} %collective-permute-done.xb.cb, f32[16,6144]{1,0:T(8,128)S(1)} %get-tuple-element.11.ext.xo.co, f32[16,6144]{1,0:T(8,128)S(1)} %collective-permute-done.1.xa.ca), custom_call_target="tpu_custom_call" | custom-call | tf_op jit(solution)/shard_map/far/pallas_call | solution.py:251
  49.7 0.0 collective-permute-done.4.s3
  49.7 0.0 collective-permute-done.3.s2
  49.7 0.0 collective-permute-done.2.s1
  49.8 0.0 copy-done
  49.8 5.6 %down.1 = f32[16,4096]{1,0:T(8,128)} custom-call(s32[3]{0:T(128)S(1)} %pad_add_fusion.base, s32[4,8]{1,0:T(4,128)S(1)} %copy-done.3, f32[1536,128]{1,0:T(8,128)S(1)} %bitcast.33, f32[8,128]{1,0:T(8,128)S(1)} %slice_reduce_fusion.s0, f32[8,128]{1,0:T(8,128)S(1)} %collective-permute-done.2.s1, f32[8,128]{1,0:T(8,128)S(1)} %collective-permute-done.3.s2, ...), custom_call_target="tpu_custom_call" | custom-call | tf_op jit(solution)/shard_map/down/pallas_call | solution.py:323
  (4 shorter events, 0.0 us)
Async XLA Ops:
  3.7 17.8 %collective-permute-start.1 = (f32[16,6144]{1,0:T(8,128)S(1)}, f32[16,6144]{1,0:T(8,128)S(1)}, u32[]{:S(2)}, u32[]{:S(2)}) collective-permute-start(f32[16,6144]{1,0:T(8,128)S(1)} %get-tuple-element.11.ext.xo.co), channel_id=1, source_target_pairs={{1,2},{2,1},{3,4},{4,3},{5,6},{6,5},{7,8},{8,7},{9,10},{10,9},{11,... | collective-permute-start | bytes 1179656 | tf_op jit(solution)/shard_map/ppermute | solution.py:341
  8.3 13.2 %collective-permute-start = (f32[16,6144]{1,0:T(8,128)S(1)}, f32[16,6144]{1,0:T(8,128)S(1)}, u32[]{:S(2)}, u32[]{:S(2)}) collective-permute-start(f32[16,6144]{1,0:T(8,128)S(1)} %get-tuple-element.11.ext.xo.co), channel_id=1, source_target_pairs={{0,1},{1,0},{2,3},{3,2},{4,5},{5,4},{6,7},{7,6},{8,9},{9,8},{10,11... | collective-permute-start | bytes 1179656 | tf_op jit(solution)/shard_map/ppermute | solution.py:340
  10.5 24.7 %all-to-all-start = ((f32[32,24,128]{2,1,0:T(8,128)}), f32[32,24,128]{2,1,0:T(8,128)S(1)}, u32[]{:S(2)}, u32[]{:S(2)}) async-start(f32[32,24,128]{2,1,0:T(8,128)} %bitcast.9), calls=%async_computation | async-start | bytes 786432 | tf_op jit(solution)/shard_map/all_to_all | solution.py:343
  21.5 28.3 %copy-start = (f32[64,2048]{1,0:T(8,128)S(1)}, f32[64,2048]{1,0:T(8,128)}, u32[]{:S(2)}) copy-start(f32[64,2048]{1,0:T(8,128)} %param.16) | copy-start | bytes 1572868
  21.5 28.3 %copy-start.1 = (f32[4,8,1024]{2,1,0:T(8,128)S(1)}, f32[4,8,1024]{2,1,0:T(8,128)}, u32[]{:S(2)}) copy-start(f32[4,8,1024]{2,1,0:T(8,128)} %param.21) | copy-start | bytes 393220
  21.5 28.3 %copy-start.2 = (f32[1,4,1024]{2,1,0:T(4,128)S(1)}, f32[1,4,1024]{2,1,0:T(4,128)}, u32[]{:S(2)}) copy-start(f32[1,4,1024]{2,1,0:T(4,128)} %param.23) | copy-start | bytes 49156
  21.5 28.3 %copy-start.3 = (s32[4,8]{1,0:T(4,128)S(1)}, s32[4,8]{1,0:T(4,128)}, u32[]{:S(2)}) copy-start(s32[4,8]{1,0:T(4,128)} %csrc.1) | copy-start | bytes 388
  39.7 10.0 %collective-permute-start.4 = (f32[8,128]{1,0:T(8,128)S(1)}, f32[8,128]{1,0:T(8,128)S(1)}, u32[]{:S(2)}, u32[]{:S(2)}) collective-permute-start(f32[8,128]{1,0:T(8,128)S(1)} %slice_reduce_fusion.s0), channel_id=1, source_target_pairs={{0,192},{64,0},{128,64},{192,128},{1,193},{65,1},{129,65},{193,129... | collective-permute-start | bytes 12296 | tf_op jit(solution)/shard_map/ppermute | solution.py:348
  42.3 7.4 %collective-permute-start.3 = (f32[8,128]{1,0:T(8,128)S(1)}, f32[8,128]{1,0:T(8,128)S(1)}, u32[]{:S(2)}, u32[]{:S(2)}) collective-permute-start(f32[8,128]{1,0:T(8,128)S(1)} %slice_reduce_fusion.s0), channel_id=1, source_target_pairs={{0,128},{64,192},{128,0},{192,64},{1,129},{65,193},{129,1},{193,65... | collective-permute-start | bytes 12296 | tf_op jit(solution)/shard_map/ppermute | solution.py:348
  42.8 6.9 %collective-permute-start.2 = (f32[8,128]{1,0:T(8,128)S(1)}, f32[8,128]{1,0:T(8,128)S(1)}, u32[]{:S(2)}, u32[]{:S(2)}) collective-permute-start(f32[8,128]{1,0:T(8,128)S(1)} %slice_reduce_fusion.s0), channel_id=1, source_target_pairs={{0,64},{64,128},{128,192},{192,0},{1,65},{65,129},{129,193},{193,1... | collective-permute-start | bytes 12296 | tf_op jit(solution)/shard_map/ppermute | solution.py:348

commit v4 on v3

--- a/solution.py
+++ b/solution.py
@@ -197,12 +197,13 @@
         fs[pl.ds(q*nc,nc),:]=upt[:,pl.ds(q*128,128)]
     f=jnp.concatenate([fs[pl.ds(u,8,stride=nc),:] for u in range(nc)],axis=1)
     pr=mul3(jnp.concatenate([spread4(cc,u) for u in range(nc)],axis=1),masked4(f))
-    pay=jnp.concatenate([cc,jnp.concatenate([pr[0:8],pr[8:16],jnp.zeros((8,64),f32)],axis=1)],axis=0)
-    for c in range(rep.shape[0]//24): rep[pl.ds(c*24,24),:]=pay
+    pay=[cc[4*i:4*i+4] for i in range(4)]+[jnp.concatenate([pr[4*i:4*i+4] for i in range(4)],axis=1)]
+    for c in range(rep.shape[0]):
+        for i in range(5): rep[c,i]=pay[i]
 
 def lift(ext,tra,upper,copies):
     return pl.pallas_call(lift_kernel,
-        out_shape=jax.ShapeDtypeStruct((copies*24,128),f32),
+        out_shape=jax.ShapeDtypeStruct((copies,5,4,128),f32),
         in_specs=[pl.BlockSpec(memory_space=pltpu.VMEM)]*3,
         scratch_shapes=[pltpu.VMEM((8*upper.shape[0],128),f32)],
         compiler_params=pltpu.CompilerParams(vmem_limit_bytes=24<<20),name="lift")(ext,tra,upper)
@@ -256,10 +257,31 @@
             pltpu.SemaphoreType.DMA((chunks,)),pltpu.SemaphoreType.DMA((1,))],
         compiler_params=pltpu.CompilerParams(vmem_limit_bytes=24<<20),name="far")(base,in_hbm(src.T),in_hbm(view),eb,eo,ea)
 
-def down_kernel(base,csrc,pays,s0,s1,s2,s3,gcp,ccp,upt,tra,bas,lf,near_ref,out,gs,fs):
+def gather_kernel(csrc,pays,ccp,out):
+    nc=ccp.shape[0]//64
+    devs=pays.shape[0]
+    for u in range(nc):
+        w=jnp.concatenate([ccp[pl.ds(u*64+j,8,stride=8),:] for j in range(8)],axis=1)
+        vs=[]
+        for j in range(8):
+            s=csrc[u,j]
+            place=lax.rem(s//nc,2)*(devs//2)+s//(2*nc)
+            vs.append(spread4(jnp.concatenate([pays[place,i] for i in range(4)],axis=0),lax.rem(s,nc)))
+        out[pl.ds(u*RHS,RHS),:]=mul3(jnp.concatenate(vs,axis=1),masked4(w))
+
+def gather(csrc,pays,ccp):
+    nc=ccp.shape[0]
+    view=ccp.reshape(nc,8,8,128).transpose(0,2,1,3).reshape(nc*64,128)
+    vm=pl.BlockSpec(memory_space=pltpu.VMEM)
+    return pl.pallas_call(gather_kernel,
+        out_shape=jax.ShapeDtypeStruct((nc*RHS,K),f32),
+        in_specs=[pl.BlockSpec(memory_space=pltpu.SMEM),vm,vm],
+        cost_estimate=pl.CostEstimate(flops=10**10,bytes_accessed=10**7,transcendentals=0),
+        compiler_params=pltpu.CompilerParams(vmem_limit_bytes=24<<20),name="gather")(csrc,pays,view)
+
+def down_kernel(base,s0,s1,s2,s3,cfar,gcp,upt,tra,bas,lf,near_ref,out,gs,fs):
     nc=upt.shape[0]; ng=gcp.shape[0]
     n=lf.shape[0]//RHS
-    devs=pays.shape[0]//24
     row=iota((K,128),0); col=lax.rem(iota((K,128),1),K)
     s4=onehot(col==lax.rem(row,8)*4+row//8)
     for q in range(8):
@@ -268,7 +290,7 @@
     gv=[]
     for h in range(ng):
         t=(s0,s1,s2,s3)[h][...]
-        gv.append(exact(jnp.concatenate([t[:,0:K],t[:,K:2*K]],axis=0),s4))
+        gv.append(exact(jnp.concatenate([t[:,i*K:(i+1)*K] for i in range(4)],axis=0),s4))
     gw=jnp.concatenate([gs[pl.ds(lax.rem(base[1]+ng-h,ng),8,stride=ng),:] for h in range(ng)],axis=1)
     gf=mul3(jnp.concatenate(gv,axis=1),masked4(gw))
     fw=jnp.concatenate([fs[pl.ds(u,8,stride=nc),:] for u in range(nc)],axis=1)
@@ -287,13 +309,7 @@
     left=iota((RHS,128),1)<LEAF
     per=n//nc
     for u in range(nc):
-        w=jnp.concatenate([ccp[pl.ds(u*64+j,8,stride=8),:] for j in range(8)],axis=1)
-        vs=[]
-        for j in range(8):
-            s=csrc[u,j]
-            place=lax.rem(s//nc,2)*(devs//2)+s//(2*nc)
-            vs.append(spread4(pays[pl.ds(pl.multiple_of(place*24,8),RHS),:],lax.rem(s,nc)))
-        cf=mul3(jnp.concatenate(vs,axis=1),masked4(w))+down[u*RHS:(u+1)*RHS]
+        cf=cfar[pl.ds(u*RHS,RHS),:]+down[u*RHS:(u+1)*RHS]
         e=jnp.concatenate([tra[pl.ds(((u*per+i)//8)*64+(u*per+i)%8,8,stride=8),:] for i in range(per)],axis=1)
         eh,el=masked4(e)
         ch,cl=split(cf)
@@ -315,16 +331,15 @@
                 at=pl.ds(g*512+m*128,128)
                 out[:,at]=near_ref[:,at]+r
 
-def down(base,csrc,pays,sums,gcp,ccp,upper,tra,basis,lf,nearv):
+def down(base,sums,cfar,gcp,upper,tra,basis,lf,nearv):
     n=basis.shape[0]; nc=upper.shape[0]; ng=gcp.shape[0]
     bas=basis.reshape(n//8,8,16,128).transpose(0,2,1,3).reshape(n*16,128)
-    ccv=ccp.reshape(nc,8,8,128).transpose(0,2,1,3).reshape(nc*64,128)
     vm=pl.BlockSpec(memory_space=pltpu.VMEM)
     return pl.pallas_call(down_kernel,
         out_shape=jax.ShapeDtypeStruct((RHS,n*LEAF),f32),
-        in_specs=[pl.BlockSpec(memory_space=pltpu.SMEM)]*2+[vm]*12,
+        in_specs=[pl.BlockSpec(memory_space=pltpu.SMEM)]+[vm]*11,
         scratch_shapes=[pltpu.VMEM((8*ng,128),f32),pltpu.VMEM((8*nc,128),f32)],
-        compiler_params=pltpu.CompilerParams(vmem_limit_bytes=24<<20),name="down")(base,csrc,pays,*sums,gcp,ccv,upper,tra,bas,lf,nearv)
+        compiler_params=pltpu.CompilerParams(vmem_limit_bytes=24<<20),name="down")(base,*sums,cfar,gcp,upper,tra,bas,lf,nearv)
 
 def across(devs):
     return [[2*i+c for i in range(devs//2)] for c in range(2)]
@@ -340,15 +355,15 @@
     eb=lax.ppermute(ext,both,[(i,i^1) for i in range(every)])
     ea=lax.ppermute(ext,both,[p for i in range(1,every-1,2) for p in ((i,i+1),(i+1,i))])
     rep=lift(ext,tra,upper,devs//2)
-    some=lax.all_to_all(rep.reshape(devs//2,24,128),"leaf",0,0,tiled=True,axis_index_groups=across(devs))
+    some=lax.all_to_all(rep,"leaf",0,0,tiled=True,axis_index_groups=across(devs))
     nearv=near(base,near_source,near_count,eb,ext,ea,near_blocks)
-    some,nearv=lax.optimization_barrier((some,nearv))
+    lf=far(base,leaf_source,eb,ext,ea,leaf_coupling)
+    some,nearv,lf=lax.optimization_barrier((some,nearv,lf))
     pays=lax.all_gather(some,"leaf",axis=0,tiled=True,axis_index_groups=[[2*i,2*i+1] for i in range(devs//2)])
-    total=pays[:,RHS:,:].sum(axis=0)
+    total=pays[:,4].sum(axis=0)
     sums=[total]+[lax.ppermute(total,"group",[(i,(i+k)%ng) for i in range(ng)]) for k in range(1,ng)]
-    base2,_=lax.optimization_barrier((base,total))
-    lf=far(base2,leaf_source,eb,ext,ea,leaf_coupling)
-    return down(base,cluster_source,pays.reshape(devs*24,128),sums,group_coupling.reshape(-1,1024),cluster_coupling,upper,tra,basis,lf,nearv)
+    cfar=gather(cluster_source,pays,cluster_coupling)
+    return down(base,sums,cfar,group_coupling.reshape(-1,1024),upper,tra,basis,lf,nearv)
 
 def solution(mesh):
     both=("group","leaf")

time: 55.6 us -> 50.7 us (0.912)
  waiting for transfers between devices: 5.05 us -> 0.31 us
  blocking collectives: 4.47 us -> 2.28 us
  starting transfers between devices: 19.3 us -> 20.5 us
    all_to_all x1, waiting for transfers between devices: 5.03 us -> 0.01 us  [per_device(): lax.all_to_all(rep, 'leaf', 0, 0, tiled=True, axis_index_groups=across(de...]
    ppermute x1, starting transfers between devices: 0.09 us -> 3.33 us  [per_device(): eb = lax.ppermute(ext, both, [(i, i ^ 1) for i in range(every)])]
    ppermute x1, starting transfers between devices: 4.59 us -> 1.91 us  [per_device(): lax.ppermute(ext, both, [p for i in range(1, every - 1, 2) for p in ((i,...]
    all_gather x1, blocking collectives: 4.47 us -> 2.28 us  [per_device(): lax.all_gather(some, 'leaf', axis=0, tiled=True, axis_index_groups=[[2 *...]
    ppermute x3, starting transfers between devices: 3.68 us -> 4.89 us  [per_device(): lax.ppermute(total, 'group', [(i, (i + k) % ng) for i in range(ng)])]
    pallas_call x1 -> x2, Pallas kernels: 2.06 us -> 3.27 us  [the longest x1 2.06 us: lift(): pl.pallas_call(lift_kernel, out_shape=jax.ShapeDtypeStruct((copies, 5, 4,...]
    pallas_call x1, Pallas kernels: 5.58 us -> 4.77 us  [down(): pl.pallas_call(down_kernel, out_shape=jax.ShapeDtypeStruct((RHS, n * LEAF...]
  transfers between devices with their start and end apart: 6 -> 6, of which waited for: 1 -> 1; matrix products, arithmetic and copies ran while one was open for 0% -> 0% of each run, Pallas kernels for 31% -> 36%
where the time goes in v4:
time: 50.7 us; the launch traced here: 50 us
  Pallas kernels  26.7 us (53%)
  starting transfers between devices  20.5 us (40%)
  blocking collectives  2.28 us (4%)
    all_to_all x1, starting transfers between devices, per_device(): lax.all_to_all(rep, 'leaf', 0, 0, tiled=True, axis_index_groups=across(de...  10.4 us
    pallas_call x1, Pallas kernels, near(): pl.pallas_call(functools.partial(near_kernel, var), out_shape=jax.ShapeDt...  8.61 us
    pallas_call x1, Pallas kernels, far(): pl.pallas_call(far_kernel, out_shape=jax.ShapeDtypeStruct((n * RHS, K), f...  6.3 us
    ppermute x3, starting transfers between devices, per_device(): lax.ppermute(total, 'group', [(i, (i + k) % ng) for i in range(ng)])  4.89 us
    pallas_call x1, Pallas kernels, down(): pl.pallas_call(down_kernel, out_shape=jax.ShapeDtypeStruct((RHS, n * LEAF...  4.77 us
    pallas_call x1, Pallas kernels, up(): pl.pallas_call(up_kernel, out_shape=(jax.ShapeDtypeStruct((RHS, n * (LEAF...  3.71 us
    ppermute x1, starting transfers between devices, per_device(): eb = lax.ppermute(ext, both, [(i, i ^ 1) for i in range(every)])  3.33 us
    all_gather x1, blocking collectives, per_device(): lax.all_gather(some, 'leaf', axis=0, tiled=True, axis_index_groups=[[2 *...  2.28 us
  transfers between devices with their start and end apart: 6, of which 1 were waited for; matrix products, arithmetic and copies ran while one was open for 0% of the time, Pallas kernels for 36%

profile of v4, /device:TPU:1, one launch (start us, length us, event | category | flops | bytes accessed | tf_op | source)
XLA Modules:
  0.0 50.0 jit_solution(13200965369222805245)
XLA Ops:
  0.0 3.7 %up.1 = (f32[16,6144]{1,0:T(8,128)S(1)}, f32[512,128]{1,0:T(8,128)S(1)}, f32[4,1024]{1,0:T(4,128)S(1)}) custom-call(f32[16,4096]{1,0:T(8,128)} %x_h.1, f32[1024,128]{1,0:T(8,128)} %bitcast.31, f32[512,128]{1,0:T(8,128)} %bitcast.36, f32[4,1024]{1,0:T(4,128)} %upt_h.1), custom_call_target="tpu_custom_call" | custom-call | tf_op jit(solution)/shard_map/up/pallas_call | solution.py:177
  3.7 3.3 %collective-permute-start = (f32[16,6144]{1,0:T(8,128)S(1)}, f32[16,6144]{1,0:T(8,128)S(1)}, u32[]{:S(2)}, u32[]{:S(2)}) collective-permute-start(f32[16,6144]{1,0:T(8,128)S(1)} %get-tuple-element.11.ext.xo.co), channel_id=1, source_target_pairs={{0,1},{1,0},{2,3},{3,2},{4,5},{5,4},{6,7},{7,6},{8,9},{9,8},{10,11... | collective-permute-start | bytes 1179656 | tf_op jit(solution)/shard_map/ppermute | solution.py:355
  7.0 1.9 %collective-permute-start.1 = (f32[16,6144]{1,0:T(8,128)S(1)}, f32[16,6144]{1,0:T(8,128)S(1)}, u32[]{:S(2)}, u32[]{:S(2)}) collective-permute-start(f32[16,6144]{1,0:T(8,128)S(1)} %get-tuple-element.11.ext.xo.co), channel_id=1, source_target_pairs={{1,2},{2,1},{3,4},{4,3},{5,6},{6,5},{7,8},{8,7},{9,10},{10,9},{11,... | collective-permute-start | bytes 1179656 | tf_op jit(solution)/shard_map/ppermute | solution.py:356
  9.0 2.1 %lift.1 = f32[32,5,4,128]{3,2,1,0:T(4,128)} custom-call(f32[16,6144]{1,0:T(8,128)S(1)} %get-tuple-element.11.ext.xo.co, f32[512,128]{1,0:T(8,128)S(1)} %get-tuple-element.12.tra, f32[4,1024]{1,0:T(4,128)S(1)} %get-tuple-element.13.upt), custom_call_target="tpu_custom_call" | custom-call | tf_op jit(solution)/shard_map/lift/pallas_call | solution.py:205
  11.0 10.4 %all-to-all-start = ((f32[32,5,4,128]{3,2,1,0:T(4,128)}), f32[32,5,4,128]{3,2,1,0:T(4,128)S(1)}, u32[]{:S(2)}, u32[]{:S(2)}) async-start(f32[32,5,4,128]{3,2,1,0:T(4,128)} %lift.1), calls=%async_computation | async-start | bytes 655360 | tf_op jit(solution)/shard_map/all_to_all | solution.py:358
  21.4 0.1 pad_add_fusion.base
  21.5 0.0 collective-permute-done.xb.cb
  21.5 0.0 collective-permute-done.1.xa.ca
  21.5 0.0 copy-start.3
  21.5 8.6 %near.1.near_ref = f32[16,4096]{1,0:T(8,128)S(1)} custom-call(s32[3]{0:T(128)S(1)} %pad_add_fusion.base, s32[8,64]{1,0:T(8,128)} %bitcast.39, s32[64]{0:T(128)} %cnt_h.1, f32[16384,128]{1,0:T(8,128)} %bitcast.38, f32[16,6144]{1,0:T(8,128)S(1)} %collective-permute-done.xb.cb, f32[16,6144]{1,0:T(8,128)S(1)} %get-tuple-element.11.ext.xo.co, ...), custom_call_target="tpu_custom_call" | custom-call | flops 99999997952 | bytes 10000000 | tf_op jit(solution)/shard_map/near/pallas_call | solution.py:105
  30.1 6.3 %far.1.lf = f32[1024,32]{1,0:T(8,128)S(1)} custom-call(s32[3]{0:T(128)S(1)} %pad_add_fusion.base, s32[8,64]{1,0:T(8,128)} %bitcast.37, f32[4096,128]{1,0:T(8,128)} %bitcast.35, f32[16,6144]{1,0:T(8,128)S(1)} %collective-permute-done.xb.cb, f32[16,6144]{1,0:T(8,128)S(1)} %get-tuple-element.11.ext.xo.co, f32[16,6144]{1,0:T(8,128)S(1)} %collective-permute-done.1.xa.ca), custom_call_target="tpu_custom_call" | custom-call | tf_op jit(solution)/shard_map/far/pallas_call | solution.py:252
  36.4 0.0 all-to-all-done
  36.4 2.3 %all_gather.3.pays = f32[64,5,4,128]{3,2,1,0:T(4,128)S(1)} all-gather(f32[32,5,4,128]{3,2,1,0:T(4,128)S(1)} %all-to-all-done), channel_id=1, replica_groups={{0,1},{2,3},{4,5},{6,7},{8,9},{10,11},{12,13},{14,15},{16,17},{18,19},{..., dimensions={0}, use_global_device_ids=true | all-gather | bytes 983040 | tf_op jit(solution)/shard_map/all_gather | solution.py:362
  38.7 0.1 slice_reduce_fusion.s0
  38.8 1.3 %collective-permute-start.2 = (f32[4,128]{1,0:T(4,128)S(1)}, f32[4,128]{1,0:T(4,128)S(1)}, u32[]{:S(2)}, u32[]{:S(2)}) collective-permute-start(f32[4,128]{1,0:T(4,128)S(1)} %slice_reduce_fusion.s0), channel_id=1, source_target_pairs={{0,64},{64,128},{128,192},{192,0},{1,65},{65,129},{129,193},{193,1... | collective-permute-start | bytes 6152 | tf_op jit(solution)/shard_map/ppermute | solution.py:364
  40.1 2.5 %collective-permute-start.3 = (f32[4,128]{1,0:T(4,128)S(1)}, f32[4,128]{1,0:T(4,128)S(1)}, u32[]{:S(2)}, u32[]{:S(2)}) collective-permute-start(f32[4,128]{1,0:T(4,128)S(1)} %slice_reduce_fusion.s0), channel_id=1, source_target_pairs={{0,128},{64,192},{128,0},{192,64},{1,129},{65,193},{129,1},{193,65... | collective-permute-start | bytes 6152 | tf_op jit(solution)/shard_map/ppermute | solution.py:364
  42.6 1.1 %collective-permute-start.4 = (f32[4,128]{1,0:T(4,128)S(1)}, f32[4,128]{1,0:T(4,128)S(1)}, u32[]{:S(2)}, u32[]{:S(2)}) collective-permute-start(f32[4,128]{1,0:T(4,128)S(1)} %slice_reduce_fusion.s0), channel_id=1, source_target_pairs={{0,192},{64,0},{128,64},{192,128},{1,193},{65,1},{129,65},{193,129... | collective-permute-start | bytes 6152 | tf_op jit(solution)/shard_map/ppermute | solution.py:364
  43.7 0.0 copy-done.2
  43.7 1.2 %gather.1.cfar = f32[64,32]{1,0:T(8,128)S(1)} custom-call(s32[4,8]{1,0:T(4,128)S(1)} %copy-done.3, f32[64,5,4,128]{3,2,1,0:T(4,128)S(1)} %all_gather.3.pays, f32[256,128]{1,0:T(8,128)S(1)} %bitcast.34), custom_call_target="tpu_custom_call" | custom-call | flops 10000000000 | bytes 10000000 | tf_op jit(solution)/shard_map/gather/pallas_call | solution.py:276
  44.9 0.0 collective-permute-done.2.s1
  44.9 0.0 collective-permute-done.3.s2
  44.9 0.3 collective-permute-done.4.s3
  45.2 0.0 copy-done
  45.2 4.8 %down.1 = f32[16,4096]{1,0:T(8,128)} custom-call(s32[3]{0:T(128)S(1)} %pad_add_fusion.base, f32[4,128]{1,0:T(4,128)S(1)} %slice_reduce_fusion.s0, f32[4,128]{1,0:T(4,128)S(1)} %collective-permute-done.2.s1, f32[4,128]{1,0:T(4,128)S(1)} %collective-permute-done.3.s2, f32[4,128]{1,0:T(4,128)S(1)} %collective-permute-done.4.s3, f32[64,32]{1,0:T(8,128)S(1)} %gather.1.cfar, ...), custom_call_target="tpu_custom_call" | custom-call | tf_op jit(solution)/shard_map/down/pallas_call | solution.py:338
  (5 shorter events, 0.0 us)
Async XLA Ops:
  3.7 17.8 %collective-permute-start = (f32[16,6144]{1,0:T(8,128)S(1)}, f32[16,6144]{1,0:T(8,128)S(1)}, u32[]{:S(2)}, u32[]{:S(2)}) collective-permute-start(f32[16,6144]{1,0:T(8,128)S(1)} %get-tuple-element.11.ext.xo.co), channel_id=1, source_target_pairs={{0,1},{1,0},{2,3},{3,2},{4,5},{5,4},{6,7},{7,6},{8,9},{9,8},{10,11... | collective-permute-start | bytes 1179656 | tf_op jit(solution)/shard_map/ppermute | solution.py:355
  7.0 14.4 %collective-permute-start.1 = (f32[16,6144]{1,0:T(8,128)S(1)}, f32[16,6144]{1,0:T(8,128)S(1)}, u32[]{:S(2)}, u32[]{:S(2)}) collective-permute-start(f32[16,6144]{1,0:T(8,128)S(1)} %get-tuple-element.11.ext.xo.co), channel_id=1, source_target_pairs={{1,2},{2,1},{3,4},{4,3},{5,6},{6,5},{7,8},{8,7},{9,10},{10,9},{11,... | collective-permute-start | bytes 1179656 | tf_op jit(solution)/shard_map/ppermute | solution.py:356
  11.0 25.4 %all-to-all-start = ((f32[32,5,4,128]{3,2,1,0:T(4,128)}), f32[32,5,4,128]{3,2,1,0:T(4,128)S(1)}, u32[]{:S(2)}, u32[]{:S(2)}) async-start(f32[32,5,4,128]{3,2,1,0:T(4,128)} %lift.1), calls=%async_computation | async-start | bytes 655360 | tf_op jit(solution)/shard_map/all_to_all | solution.py:358
  21.5 22.2 %copy-start.2 = (f32[4,8,1024]{2,1,0:T(8,128)S(1)}, f32[4,8,1024]{2,1,0:T(8,128)}, u32[]{:S(2)}) copy-start(f32[4,8,1024]{2,1,0:T(8,128)} %param.21) | copy-start | bytes 393220
  21.5 22.2 %copy-start.3 = (s32[4,8]{1,0:T(4,128)S(1)}, s32[4,8]{1,0:T(4,128)}, u32[]{:S(2)}) copy-start(s32[4,8]{1,0:T(4,128)} %csrc.1) | copy-start | bytes 388
  38.8 6.1 %collective-permute-start.2 = (f32[4,128]{1,0:T(4,128)S(1)}, f32[4,128]{1,0:T(4,128)S(1)}, u32[]{:S(2)}, u32[]{:S(2)}) collective-permute-start(f32[4,128]{1,0:T(4,128)S(1)} %slice_reduce_fusion.s0), channel_id=1, source_target_pairs={{0,64},{64,128},{128,192},{192,0},{1,65},{65,129},{129,193},{193,1... | collective-permute-start | bytes 6152 | tf_op jit(solution)/shard_map/ppermute | solution.py:364
  40.1 4.8 %collective-permute-start.3 = (f32[4,128]{1,0:T(4,128)S(1)}, f32[4,128]{1,0:T(4,128)S(1)}, u32[]{:S(2)}, u32[]{:S(2)}) collective-permute-start(f32[4,128]{1,0:T(4,128)S(1)} %slice_reduce_fusion.s0), channel_id=1, source_target_pairs={{0,128},{64,192},{128,0},{192,64},{1,129},{65,193},{129,1},{193,65... | collective-permute-start | bytes 6152 | tf_op jit(solution)/shard_map/ppermute | solution.py:364
  42.6 2.6 %collective-permute-start.4 = (f32[4,128]{1,0:T(4,128)S(1)}, f32[4,128]{1,0:T(4,128)S(1)}, u32[]{:S(2)}, u32[]{:S(2)}) collective-permute-start(f32[4,128]{1,0:T(4,128)S(1)} %slice_reduce_fusion.s0), channel_id=1, source_target_pairs={{0,192},{64,0},{128,64},{192,128},{1,193},{65,1},{129,65},{193,129... | collective-permute-start | bytes 6152 | tf_op jit(solution)/shard_map/ppermute | solution.py:364
  43.7 1.5 %copy-start = (f32[64,2048]{1,0:T(8,128)S(1)}, f32[64,2048]{1,0:T(8,128)}, u32[]{:S(2)}) copy-start(f32[64,2048]{1,0:T(8,128)} %param.16) | copy-start | bytes 1572868
  43.7 1.5 %copy-start.1 = (f32[1,4,1024]{2,1,0:T(4,128)S(1)}, f32[1,4,1024]{2,1,0:T(4,128)}, u32[]{:S(2)}) copy-start(f32[1,4,1024]{2,1,0:T(4,128)} %param.23) | copy-start | bytes 49156

commit v5 on v4

--- a/solution.py
+++ b/solution.py
@@ -31,7 +31,7 @@
         return 0
     lax.fori_loop(0,leaves//2,body,0,unroll=4)
 
-def near_kernel(var, base, src_h, cnt_h, nb_h, xb, xo, xa, out, hi, lo, weave, nb, src, cnt, sem, sem2):
+def near_kernel(base, src_h, cnt_h, nb_h, xb, xo, xa, out, hi, lo, weave, nb, src, cnt, sem, sem2):
     n=out.shape[1]//LEAF
     chunks=sem.shape[0]
     size=nb.shape[0]//chunks
@@ -44,10 +44,10 @@
     point_table(xa,(2-base[2])*n,n,hi,lo)
     hi[3*n]=jnp.zeros((RHS,128),bf16)
     lo[3*n]=jnp.zeros((RHS,128),bf16)
-    row=lax.broadcasted_iota(jnp.int32,(256,256),0)
-    col=lax.broadcasted_iota(jnp.int32,(256,256),1)
+    row=lax.broadcasted_iota(jnp.int32,(256,128),0)
+    col=lax.broadcasted_iota(jnp.int32,(256,128),1)
     a=lax.rem(col,64)
-    weave[...]=(row==col-a+lax.rem(a,2)*32+a//2).astype(f32).astype(bf16)
+    weave[...]=((row//128==col//64)&(lax.rem(row,64)==lax.rem(a,2)*32+a//2)).astype(f32).astype(bf16)
     ca.wait(); cb.wait()
     per=n//chunks
     first=base[0]
@@ -56,57 +56,38 @@
     def join(table,at): return jnp.concatenate([jnp.where(left,table[at[2*p]],table[at[2*p+1]]) for p in range(4)],axis=1)
     def step(c,_):
         chunk(c).wait()
-        for quad in range(per//4):
+        for pair in range(per//2):
             parts=[]
-            for m in range(4):
-                t=c*per+quad*4+m
+            for m in range(2):
+                t=c*per+pair*2+m
                 off=pl.multiple_of(t*256,256)
                 even=[];odd=[]
                 for p in range(4):
                     a=nb[pl.ds(off+2*p,32,stride=8),:]
                     b=nb[pl.ds(off+2*p+1,32,stride=8),:]
-                    if var=="f32":
-                        even.append(jnp.where(left32,a,pltpu.roll(b,LEAF,1)))
-                        odd.append(jnp.where(left32,pltpu.roll(a,LEAF,1),b))
-                    else:
-                        even.append((a,b))
-                if var=="f32":
-                    w=jnp.concatenate([jnp.concatenate(even,axis=1),jnp.concatenate(odd,axis=1)],axis=0)
-                    ah,al=split(w)
-                else:
-                    res=[]
-                    es=[(split(a),split(b)) for a,b in even]
-                    for k in range(2):
-                        e=jnp.concatenate([jnp.concatenate([a[k][:,:64],b[k][:,:64]],axis=1) for a,b in es],axis=1)
-                        o=jnp.concatenate([jnp.concatenate([a[k][:,64:],b[k][:,64:]],axis=1) for a,b in es],axis=1)
-                        res.append(jnp.concatenate([e,o],axis=0))
-                    ah,al=res
+                    even.append(jnp.where(left32,a,pltpu.roll(b,LEAF,1)))
+                    odd.append(jnp.where(left32,pltpu.roll(a,LEAF,1),b))
+                w=jnp.concatenate([jnp.concatenate(even,axis=1),jnp.concatenate(odd,axis=1)],axis=0)
                 live=cnt[t]
                 at=[jnp.where(j<live,src[j,t]-first,3*n) for j in range(8)]
-                xh=join(hi,at); xl=join(lo,at)
-                if var=="n128":
-                    d=dotnt(jnp.concatenate([xh,xl],axis=0),jnp.concatenate([ah,al],axis=0))
-                    parts.append(d[:RHS,:64]+d[RHS:,:64]+d[:RHS,64:])
-                else:
-                    d=dotnt(jnp.concatenate([xh,xl],axis=0),ah)
-                    parts.append(d[:RHS]+d[RHS:]+dotnt(xh,al))
-            h,l=split(jnp.concatenate(parts,axis=1))
-            d=dotnn(jnp.concatenate([h,l],axis=0),weave[...])
-            out[:,pl.ds(pl.multiple_of((c*per+quad*4)*LEAF,256),256)]=d[:RHS]+d[RHS:]
+                parts.append(dotnt(jnp.concatenate([join(hi,at),join(lo,at)],axis=0),jnp.concatenate(split(w),axis=0)))
+            d=dotnn(jnp.concatenate(split(jnp.concatenate(parts,axis=1)),axis=0),weave[...])
+            d=d[:2*RHS]+d[2*RHS:]
+            out[:,pl.ds(pl.multiple_of((c*per+pair*2)*LEAF,128),128)]=d[:RHS]+d[RHS:]
         return 0
     lax.fori_loop(0,chunks,step,0)
 
-def near(base,src,cnt,xb,xo,xa,nb,chunks=4,var="f32"):
+def near(base,src,cnt,xb,xo,xa,nb,chunks=2):
     leaves=nb.shape[0]
     view=nb.reshape(leaves,8,32,128).transpose(0,2,1,3).reshape(leaves*256,128)
     pts=leaves*LEAF
     blk=pl.BlockSpec((RHS,pts),lambda g:(0,0))
     hbm=pl.BlockSpec(memory_space=HBM)
-    return pl.pallas_call(functools.partial(near_kernel,var),
+    return pl.pallas_call(near_kernel,
         out_shape=jax.ShapeDtypeStruct((RHS,pts),f32),grid=(1,),
         in_specs=[pl.BlockSpec(memory_space=pltpu.SMEM),hbm,hbm,hbm,blk,blk,blk],
         out_specs=blk,
-        scratch_shapes=[pltpu.VMEM((3*leaves+1,RHS,128),bf16)]*2+[pltpu.VMEM((256,256),bf16),pltpu.VMEM((leaves*256,128),f32),
+        scratch_shapes=[pltpu.VMEM((3*leaves+1,RHS,128),bf16)]*2+[pltpu.VMEM((256,128),bf16),pltpu.VMEM((leaves*256,128),f32),
             pltpu.SMEM((8,leaves),jnp.int32),pltpu.SMEM((leaves,),jnp.int32),pltpu.SemaphoreType.DMA((chunks,)),pltpu.SemaphoreType.DMA((2,))],
         cost_estimate=pl.CostEstimate(flops=10**11,bytes_accessed=10**7,transcendentals=0),
         compiler_params=pltpu.CompilerParams(vmem_limit_bytes=24<<20),
@@ -115,8 +96,11 @@
 def iota(shape,d): return lax.broadcasted_iota(jnp.int32,shape,d)
 def onehot(cond): return cond.astype(f32).astype(bf16)
 def exact(v,m):
-    h,l=split(v)
-    return dotnn(h,m)+dotnn(l,m)
+    d=dotnn(jnp.concatenate(split(v),axis=0),m)
+    return d[:v.shape[0]]+d[v.shape[0]:]
+def wide(v,w):
+    d=dotnt(jnp.concatenate(split(v),axis=0),jnp.concatenate(w,axis=0))
+    return d[:RHS]+d[RHS:]
 def spread4(tile,m):
     block=jnp.where(iota(tile.shape,1)//K==m,tile,0.0)
     block=block+pltpu.roll(block,64,1)
@@ -134,9 +118,9 @@
     return out
 
 def mul3(v,w):
-    h,l=split(v)
-    d=dotnt(jnp.concatenate([h,l],axis=0),w[0])
-    return d[:RHS]+d[RHS:]+dotnt(h,w[1])
+    d=wide(v,w)
+    n=w[0].shape[0]
+    return d[:,:n]+d[:,n:]
 
 def up_kernel(x_h,bas_h,tra_h,upt_h,ext,tra,upt,x,bas,sem,sem2):
     chunks=sem.shape[0]-1
@@ -165,8 +149,8 @@
                 blks+= [jnp.where(left,a,0.0),jnp.where(left,0.0,b)]
         xh,xl=split(jnp.concatenate(blks,axis=0))
         bh,bl=split(bas[pl.ds(g*128,128),:])
-        d=dotnt(xh,bh)+dotnt(xl,bh)+dotnt(xh,bl)
-        d=jnp.where(same,d,0.0).reshape(8,32,128).sum(axis=0)
+        d=dotnt(jnp.concatenate([xh,xl],axis=1),jnp.concatenate([jnp.concatenate([bh,bh],axis=1),jnp.concatenate([bl,jnp.zeros_like(bl)],axis=1)],axis=0))
+        d=jnp.where(same,d[:,:128]+d[:,128:],0.0).reshape(8,32,128).sum(axis=0)
         ext[:,pl.ds(pts+g*256,256)]=exact(jnp.concatenate([d[:RHS],d[RHS:]],axis=1),s2)
     for m in later: m.wait()
 
@@ -208,7 +192,7 @@
         scratch_shapes=[pltpu.VMEM((8*upper.shape[0],128),f32)],
         compiler_params=pltpu.CompilerParams(vmem_limit_bytes=24<<20),name="lift")(ext,tra,upper)
 
-def far_kernel(base,src_h,cpl_h,cb,co,ca,out,hi,lo,cpl,src,sem,sem2):
+def far_kernel(base,src_h,cpl_h,cb,co,ca,out,table,cpl,src,sem,sem2):
     tiles=co.shape[1]//128
     n=src.shape[1]
     chunks=sem.shape[0]
@@ -220,40 +204,41 @@
     for w,ref in ((base[2],cb),(1,co),(2-base[2],ca)):
         def body(q,_):
             t=ref[:,pl.ds(pl.multiple_of(q*128,128),128)]
-            for m in range(4):
-                h,l=split(spread4(t,m))
-                hi[(w*tiles+q)*4+m]=h
-                lo[(w*tiles+q)*4+m]=l
+            for m in range(4): table[(w*tiles+q)*4+m]=jnp.concatenate(split(spread4(t,m)),axis=0)
             return 0
         lax.fori_loop(0,tiles,body,0,unroll=4)
     idx.wait()
     per=n//chunks
     first=base[0]
+    block=iota((8,128),1)//K
+    block32=iota((2*RHS,128),1)//K
+    def pick(where,four):
+        return jnp.where(where<2,jnp.where(where<1,four[0],four[1]),jnp.where(where<3,four[2],four[3]))
     def step(c,_):
         chunk(c).wait()
         for i in range(per):
             t=c*per+i
             off=pl.multiple_of(t*64,64)
-            w=jnp.concatenate([cpl[pl.ds(off+j,8,stride=8),:] for j in range(8)],axis=1)
-            wh,wl=masked4(w)
+            cs=[cpl[pl.ds(off+j,8,stride=8),:] for j in range(8)]
+            w=[[pick(block,[pltpu.roll(cs[4*h+p],(p-km)%4*K,1) if p!=km else cs[4*h+p] for p in range(4)]) for h in range(2)] for km in range(4)]
+            w=jnp.concatenate([jnp.concatenate(v,axis=1) for v in w],axis=0)
             at=[src[j,t]-first for j in range(8)]
-            vh=jnp.concatenate([hi[s] for s in at],axis=1)
-            vl=jnp.concatenate([lo[s] for s in at],axis=1)
-            d=dotnt(jnp.concatenate([vh,vl],axis=0),wh)
-            out[pl.ds(pl.multiple_of(t*RHS,RHS),RHS),:]=d[:RHS]+d[RHS:]+dotnt(vh,wl)
+            v=jnp.concatenate([pick(block32,[table[at[4*h+p]] for p in range(4)]) for h in range(2)],axis=1)
+            d=dotnt(v,jnp.concatenate(split(w),axis=0))
+            out[pl.ds(pl.multiple_of(t*RHS,RHS),RHS),:]=d[:RHS]+d[RHS:]
         return 0
     lax.fori_loop(0,chunks,step,0)
 
-def far(base,src,eb,eo,ea,coupling,chunks=4):
+def far(base,src,eb,eo,ea,coupling,chunks=2):
     n=coupling.shape[0]
     view=coupling.reshape(n,8,8,128).transpose(0,2,1,3).reshape(n*64,128)
     blk=pl.BlockSpec((RHS,n*K),lambda g:(0,LEAF//K))
     hbm=pl.BlockSpec(memory_space=HBM)
     return pl.pallas_call(far_kernel,
-        out_shape=jax.ShapeDtypeStruct((n*RHS,K),f32),grid=(1,),
+        out_shape=jax.ShapeDtypeStruct((n*RHS,2*K),f32),grid=(1,),
         in_specs=[pl.BlockSpec(memory_space=pltpu.SMEM),hbm,hbm,blk,blk,blk],
-        out_specs=pl.BlockSpec((n*RHS,K),lambda g:(0,0)),
-        scratch_shapes=[pltpu.VMEM((3*n,RHS,128),bf16)]*2+[pltpu.VMEM((n*64,128),f32),pltpu.SMEM((8,n),jnp.int32),
+        out_specs=pl.BlockSpec((n*RHS,2*K),lambda g:(0,0)),
+        scratch_shapes=[pltpu.VMEM((3*n,2*RHS,128),bf16),pltpu.VMEM((n*64,128),f32),pltpu.SMEM((8,n),jnp.int32),
             pltpu.SemaphoreType.DMA((chunks,)),pltpu.SemaphoreType.DMA((1,))],
         compiler_params=pltpu.CompilerParams(vmem_limit_bytes=24<<20),name="far")(base,in_hbm(src.T),in_hbm(view),eb,eo,ea)
 
@@ -287,10 +272,8 @@
     for q in range(8):
         fs[pl.ds(q*nc,nc),:]=upt[:,pl.ds(q*128,128)]
         gs[pl.ds(q*ng,ng),:]=gcp[:,pl.ds(q*128,128)]
-    gv=[]
-    for h in range(ng):
-        t=(s0,s1,s2,s3)[h][...]
-        gv.append(exact(jnp.concatenate([t[:,i*K:(i+1)*K] for i in range(4)],axis=0),s4))
+    gv=exact(jnp.concatenate([s[:,i*K:(i+1)*K] for s in (s0,s1,s2,s3) for i in range(4)],axis=0),s4)
+    gv=[gv[h*RHS:(h+1)*RHS] for h in range(ng)]
     gw=jnp.concatenate([gs[pl.ds(lax.rem(base[1]+ng-h,ng),8,stride=ng),:] for h in range(ng)],axis=1)
     gf=mul3(jnp.concatenate(gv,axis=1),masked4(gw))
     fw=jnp.concatenate([fs[pl.ds(u,8,stride=nc),:] for u in range(nc)],axis=1)
@@ -303,9 +286,10 @@
     down=exact(down,s5)
     row=lax.rem(iota((128,256),0),K); col=iota((128,256),1)
     p1=onehot(row==2*(lax.rem(col,128)//8)+col//128)
-    row=iota((K,256),0); col=iota((K,256),1)
+    row=lax.rem(iota((2*K,256),0),K); col=iota((2*K,256),1)
     nat=2*(lax.rem(col,128)//8)+col//128
     p2=onehot(row==lax.rem(nat,4)*8+nat//4)
+    p12=jnp.concatenate([p1,p1,p2,p2],axis=0)
     left=iota((RHS,128),1)<LEAF
     per=n//nc
     for u in range(nc):
@@ -315,7 +299,7 @@
         ch,cl=split(cf)
         d=dotnn(jnp.concatenate([ch,cl,ch],axis=1),jnp.concatenate([eh,eh,el],axis=0))
         d=jnp.concatenate([d[:,i*128:(i+1)*128] for i in range(per)],axis=0)
-        q=exact(d,p1)+exact(lf[pl.ds(u*per*RHS,per*RHS),:],p2)
+        q=dotnn(jnp.concatenate([*split(d),*split(lf[pl.ds(u*per*RHS,per*RHS),:])],axis=1),p12)
         for b in range(per//8):
             g=(u*per)//8+b
             z=q[b*128:(b+1)*128].reshape(8,RHS,256)
@@ -323,7 +307,8 @@
             same=(iota((256,128),0)//32==lax.rem(iota((256,128),1),8))
             zh,zl=split(jnp.where(same,z,0.0))
             bh,bl=split(bas[pl.ds(g*128,128),:])
-            o=(dotnn(zh,bh)+dotnn(zl,bh)+dotnn(zh,bl)).reshape(8,2,RHS,128)
+            o=dotnn(jnp.concatenate([zh,zl],axis=1),jnp.concatenate([jnp.concatenate([bh,bl],axis=1),jnp.concatenate([bh,jnp.zeros_like(bl)],axis=1)],axis=0))
+            o=(o[:,:128]+o[:,128:]).reshape(8,2,RHS,128)
             for m in range(4):
                 a=jnp.where(left,o[2*m,0],o[2*m,1])
                 c=jnp.where(left,o[2*m+1,0],o[2*m+1,1])

time: 50.7 us -> 48.5 us (0.957)
  Pallas kernels: 26.7 us -> 24.2 us
  blocking collectives: 2.28 us -> 2.79 us
    pallas_call x2, Pallas kernels: 14.9 us -> 14 us  [the longest x1 9.23 us: near(): pl.pallas_call(near_kernel, out_shape=jax.ShapeDtypeStruct((RHS, pts), f3...]
    pallas_call x1, Pallas kernels: 4.77 us -> 3.94 us  [down(): pl.pallas_call(down_kernel, out_shape=jax.ShapeDtypeStruct((RHS, n * LEAF...]
    pallas_call x1, Pallas kernels: 3.71 us -> 2.91 us  [up(): pl.pallas_call(up_kernel, out_shape=(jax.ShapeDtypeStruct((RHS, n * (LEAF...]
    all_gather x1, blocking collectives: 2.28 us -> 2.79 us  [per_device(): lax.all_gather(some, 'leaf', axis=0, tiled=True, axis_index_groups=[[2 *...]
where the time goes in v5:
time: 48.5 us; the launch traced here: 48.2 us
  Pallas kernels  24.2 us (50%)
  starting transfers between devices  20.5 us (42%)
  blocking collectives  2.79 us (6%)
    all_to_all x1, starting transfers between devices, per_device(): lax.all_to_all(rep, 'leaf', 0, 0, tiled=True, axis_index_groups=across(de...  10.4 us
    pallas_call x1, Pallas kernels, near(): pl.pallas_call(near_kernel, out_shape=jax.ShapeDtypeStruct((RHS, pts), f3...  9.23 us
    ppermute x3, starting transfers between devices, per_device(): lax.ppermute(total, 'group', [(i, (i + k) % ng) for i in range(ng)])  4.93 us
    pallas_call x1, Pallas kernels, far(): pl.pallas_call(far_kernel, out_shape=jax.ShapeDtypeStruct((n * RHS, 2 * K...  4.78 us
    pallas_call x1, Pallas kernels, down(): pl.pallas_call(down_kernel, out_shape=jax.ShapeDtypeStruct((RHS, n * LEAF...  3.94 us
    ppermute x1, starting transfers between devices, per_device(): eb = lax.ppermute(ext, both, [(i, i ^ 1) for i in range(every)])  3.33 us
    pallas_call x1, Pallas kernels, up(): pl.pallas_call(up_kernel, out_shape=(jax.ShapeDtypeStruct((RHS, n * (LEAF...  2.91 us
    all_gather x1, blocking collectives, per_device(): lax.all_gather(some, 'leaf', axis=0, tiled=True, axis_index_groups=[[2 *...  2.79 us
  transfers between devices with their start and end apart: 6, of which 1 were waited for; matrix products, arithmetic and copies ran while one was open for 0% of the time, Pallas kernels for 36%

profile of v5, /device:TPU:1, one launch (start us, length us, event | category | flops | bytes accessed | tf_op | source)
XLA Modules:
  0.0 48.2 jit_solution(8554595842927686530)
XLA Ops:
  0.0 2.9 %up.1 = (f32[16,6144]{1,0:T(8,128)S(1)}, f32[512,128]{1,0:T(8,128)S(1)}, f32[4,1024]{1,0:T(4,128)S(1)}) custom-call(f32[16,4096]{1,0:T(8,128)} %x_h.1, f32[1024,128]{1,0:T(8,128)} %bitcast.31, f32[512,128]{1,0:T(8,128)} %bitcast.36, f32[4,1024]{1,0:T(4,128)} %upt_h.1), custom_call_target="tpu_custom_call" | custom-call | tf_op jit(solution)/shard_map/up/pallas_call | solution.py:161
  2.9 3.3 %collective-permute-start = (f32[16,6144]{1,0:T(8,128)S(1)}, f32[16,6144]{1,0:T(8,128)S(1)}, u32[]{:S(2)}, u32[]{:S(2)}) collective-permute-start(f32[16,6144]{1,0:T(8,128)S(1)} %get-tuple-element.11.ext.xo.co), channel_id=1, source_target_pairs={{0,1},{1,0},{2,3},{3,2},{4,5},{5,4},{6,7},{7,6},{8,9},{9,8},{10,11... | collective-permute-start | bytes 1179656 | tf_op jit(solution)/shard_map/ppermute | solution.py:340
  6.2 1.9 %collective-permute-start.1 = (f32[16,6144]{1,0:T(8,128)S(1)}, f32[16,6144]{1,0:T(8,128)S(1)}, u32[]{:S(2)}, u32[]{:S(2)}) collective-permute-start(f32[16,6144]{1,0:T(8,128)S(1)} %get-tuple-element.11.ext.xo.co), channel_id=1, source_target_pairs={{1,2},{2,1},{3,4},{4,3},{5,6},{6,5},{7,8},{8,7},{9,10},{10,9},{11,... | collective-permute-start | bytes 1179656 | tf_op jit(solution)/shard_map/ppermute | solution.py:341
  8.2 2.1 %lift.1 = f32[32,5,4,128]{3,2,1,0:T(4,128)} custom-call(f32[16,6144]{1,0:T(8,128)S(1)} %get-tuple-element.11.ext.xo.co, f32[512,128]{1,0:T(8,128)S(1)} %get-tuple-element.12.tra, f32[4,1024]{1,0:T(4,128)S(1)} %get-tuple-element.13.upt), custom_call_target="tpu_custom_call" | custom-call | tf_op jit(solution)/shard_map/lift/pallas_call | solution.py:189
  10.3 10.4 %all-to-all-start = ((f32[32,5,4,128]{3,2,1,0:T(4,128)}), f32[32,5,4,128]{3,2,1,0:T(4,128)S(1)}, u32[]{:S(2)}, u32[]{:S(2)}) async-start(f32[32,5,4,128]{3,2,1,0:T(4,128)} %lift.1), calls=%async_computation | async-start | bytes 655360 | tf_op jit(solution)/shard_map/all_to_all | solution.py:343
  20.6 0.1 pad_add_fusion.base
  20.7 0.0 collective-permute-done.xb.cb
  20.7 0.0 collective-permute-done.1.xa.ca
  20.7 0.0 copy-start.3
  20.7 9.2 %near.1.near_ref = f32[16,4096]{1,0:T(8,128)S(1)} custom-call(s32[3]{0:T(128)S(1)} %pad_add_fusion.base, s32[8,64]{1,0:T(8,128)} %bitcast.39, s32[64]{0:T(128)} %cnt_h.1, f32[16384,128]{1,0:T(8,128)} %bitcast.38, f32[16,6144]{1,0:T(8,128)S(1)} %collective-permute-done.xb.cb, f32[16,6144]{1,0:T(8,128)S(1)} %get-tuple-element.11.ext.xo.co, ...), custom_call_target="tpu_custom_call" | custom-call | flops 99999997952 | bytes 10000000 | tf_op jit(solution)/shard_map/near/pallas_call | solution.py:86
  30.0 4.8 %far.1.lf = f32[1024,64]{1,0:T(8,128)S(1)} custom-call(s32[3]{0:T(128)S(1)} %pad_add_fusion.base, s32[8,64]{1,0:T(8,128)} %bitcast.37, f32[4096,128]{1,0:T(8,128)} %bitcast.35, f32[16,6144]{1,0:T(8,128)S(1)} %collective-permute-done.xb.cb, f32[16,6144]{1,0:T(8,128)S(1)} %get-tuple-element.11.ext.xo.co, f32[16,6144]{1,0:T(8,128)S(1)} %collective-permute-done.1.xa.ca), custom_call_target="tpu_custom_call" | custom-call | tf_op jit(solution)/shard_map/far/pallas_call | solution.py:237
  34.8 0.0 all-to-all-done
  34.8 2.8 %all_gather.3.pays = f32[64,5,4,128]{3,2,1,0:T(4,128)S(1)} all-gather(f32[32,5,4,128]{3,2,1,0:T(4,128)S(1)} %all-to-all-done), channel_id=1, replica_groups={{0,1},{2,3},{4,5},{6,7},{8,9},{10,11},{12,13},{14,15},{16,17},{18,19},{..., dimensions={0}, use_global_device_ids=true | all-gather | bytes 983040 | tf_op jit(solution)/shard_map/all_gather | solution.py:347
  37.6 0.1 slice_reduce_fusion.s0
  37.6 1.3 %collective-permute-start.2 = (f32[4,128]{1,0:T(4,128)S(1)}, f32[4,128]{1,0:T(4,128)S(1)}, u32[]{:S(2)}, u32[]{:S(2)}) collective-permute-start(f32[4,128]{1,0:T(4,128)S(1)} %slice_reduce_fusion.s0), channel_id=1, source_target_pairs={{0,64},{64,128},{128,192},{192,0},{1,65},{65,129},{129,193},{193,1... | collective-permute-start | bytes 6152 | tf_op jit(solution)/shard_map/ppermute | solution.py:349
  39.0 2.6 %collective-permute-start.3 = (f32[4,128]{1,0:T(4,128)S(1)}, f32[4,128]{1,0:T(4,128)S(1)}, u32[]{:S(2)}, u32[]{:S(2)}) collective-permute-start(f32[4,128]{1,0:T(4,128)S(1)} %slice_reduce_fusion.s0), channel_id=1, source_target_pairs={{0,128},{64,192},{128,0},{192,64},{1,129},{65,193},{129,1},{193,65... | collective-permute-start | bytes 6152 | tf_op jit(solution)/shard_map/ppermute | solution.py:349
  41.6 1.0 %collective-permute-start.4 = (f32[4,128]{1,0:T(4,128)S(1)}, f32[4,128]{1,0:T(4,128)S(1)}, u32[]{:S(2)}, u32[]{:S(2)}) collective-permute-start(f32[4,128]{1,0:T(4,128)S(1)} %slice_reduce_fusion.s0), channel_id=1, source_target_pairs={{0,192},{64,0},{128,64},{192,128},{1,193},{65,1},{129,65},{193,129... | collective-permute-start | bytes 6152 | tf_op jit(solution)/shard_map/ppermute | solution.py:349
  42.6 0.0 copy-done.2
  42.6 1.2 %gather.1.cfar = f32[64,32]{1,0:T(8,128)S(1)} custom-call(s32[4,8]{1,0:T(4,128)S(1)} %copy-done.3, f32[64,5,4,128]{3,2,1,0:T(4,128)S(1)} %all_gather.3.pays, f32[256,128]{1,0:T(8,128)S(1)} %bitcast.34), custom_call_target="tpu_custom_call" | custom-call | flops 10000000000 | bytes 10000000 | tf_op jit(solution)/shard_map/gather/pallas_call | solution.py:261
  43.8 0.0 collective-permute-done.2.s1
  43.8 0.0 collective-permute-done.3.s2
  43.8 0.4 collective-permute-done.4.s3
  44.3 0.0 copy-done
  44.3 3.9 %down.1 = f32[16,4096]{1,0:T(8,128)} custom-call(s32[3]{0:T(128)S(1)} %pad_add_fusion.base, f32[4,128]{1,0:T(4,128)S(1)} %slice_reduce_fusion.s0, f32[4,128]{1,0:T(4,128)S(1)} %collective-permute-done.2.s1, f32[4,128]{1,0:T(4,128)S(1)} %collective-permute-done.3.s2, f32[4,128]{1,0:T(4,128)S(1)} %collective-permute-done.4.s3, f32[64,32]{1,0:T(8,128)S(1)} %gather.1.cfar, ...), custom_call_target="tpu_custom_call" | custom-call | tf_op jit(solution)/shard_map/down/pallas_call | solution.py:323
  (5 shorter events, 0.0 us)
Async XLA Ops:
  2.9 17.8 %collective-permute-start = (f32[16,6144]{1,0:T(8,128)S(1)}, f32[16,6144]{1,0:T(8,128)S(1)}, u32[]{:S(2)}, u32[]{:S(2)}) collective-permute-start(f32[16,6144]{1,0:T(8,128)S(1)} %get-tuple-element.11.ext.xo.co), channel_id=1, source_target_pairs={{0,1},{1,0},{2,3},{3,2},{4,5},{5,4},{6,7},{7,6},{8,9},{9,8},{10,11... | collective-permute-start | bytes 1179656 | tf_op jit(solution)/shard_map/ppermute | solution.py:340
  6.2 14.5 %collective-permute-start.1 = (f32[16,6144]{1,0:T(8,128)S(1)}, f32[16,6144]{1,0:T(8,128)S(1)}, u32[]{:S(2)}, u32[]{:S(2)}) collective-permute-start(f32[16,6144]{1,0:T(8,128)S(1)} %get-tuple-element.11.ext.xo.co), channel_id=1, source_target_pairs={{1,2},{2,1},{3,4},{4,3},{5,6},{6,5},{7,8},{8,7},{9,10},{10,9},{11,... | collective-permute-start | bytes 1179656 | tf_op jit(solution)/shard_map/ppermute | solution.py:341
  10.3 24.5 %all-to-all-start = ((f32[32,5,4,128]{3,2,1,0:T(4,128)}), f32[32,5,4,128]{3,2,1,0:T(4,128)S(1)}, u32[]{:S(2)}, u32[]{:S(2)}) async-start(f32[32,5,4,128]{3,2,1,0:T(4,128)} %lift.1), calls=%async_computation | async-start | bytes 655360 | tf_op jit(solution)/shard_map/all_to_all | solution.py:343
  20.7 21.9 %copy-start.2 = (f32[4,8,1024]{2,1,0:T(8,128)S(1)}, f32[4,8,1024]{2,1,0:T(8,128)}, u32[]{:S(2)}) copy-start(f32[4,8,1024]{2,1,0:T(8,128)} %param.21) | copy-start | bytes 393220
  20.7 21.8 %copy-start.3 = (s32[4,8]{1,0:T(4,128)S(1)}, s32[4,8]{1,0:T(4,128)}, u32[]{:S(2)}) copy-start(s32[4,8]{1,0:T(4,128)} %csrc.1) | copy-start | bytes 388
  37.6 6.2 %collective-permute-start.2 = (f32[4,128]{1,0:T(4,128)S(1)}, f32[4,128]{1,0:T(4,128)S(1)}, u32[]{:S(2)}, u32[]{:S(2)}) collective-permute-start(f32[4,128]{1,0:T(4,128)S(1)} %slice_reduce_fusion.s0), channel_id=1, source_target_pairs={{0,64},{64,128},{128,192},{192,0},{1,65},{65,129},{129,193},{193,1... | collective-permute-start | bytes 6152 | tf_op jit(solution)/shard_map/ppermute | solution.py:349
  39.0 4.9 %collective-permute-start.3 = (f32[4,128]{1,0:T(4,128)S(1)}, f32[4,128]{1,0:T(4,128)S(1)}, u32[]{:S(2)}, u32[]{:S(2)}) collective-permute-start(f32[4,128]{1,0:T(4,128)S(1)} %slice_reduce_fusion.s0), channel_id=1, source_target_pairs={{0,128},{64,192},{128,0},{192,64},{1,129},{65,193},{129,1},{193,65... | collective-permute-start | bytes 6152 | tf_op jit(solution)/shard_map/ppermute | solution.py:349
  41.6 2.7 %collective-permute-start.4 = (f32[4,128]{1,0:T(4,128)S(1)}, f32[4,128]{1,0:T(4,128)S(1)}, u32[]{:S(2)}, u32[]{:S(2)}) collective-permute-start(f32[4,128]{1,0:T(4,128)S(1)} %slice_reduce_fusion.s0), channel_id=1, source_target_pairs={{0,192},{64,0},{128,64},{192,128},{1,193},{65,1},{129,65},{193,129... | collective-permute-start | bytes 6152 | tf_op jit(solution)/shard_map/ppermute | solution.py:349
  42.6 1.7 %copy-start = (f32[64,2048]{1,0:T(8,128)S(1)}, f32[64,2048]{1,0:T(8,128)}, u32[]{:S(2)}) copy-start(f32[64,2048]{1,0:T(8,128)} %param.16) | copy-start | bytes 1572868
  42.6 1.7 %copy-start.1 = (f32[1,4,1024]{2,1,0:T(4,128)S(1)}, f32[1,4,1024]{2,1,0:T(4,128)}, u32[]{:S(2)}) copy-start(f32[1,4,1024]{2,1,0:T(4,128)} %param.23) | copy-start | bytes 49156

commit v6 on v5

--- a/solution.py
+++ b/solution.py
@@ -31,7 +31,7 @@
         return 0
     lax.fori_loop(0,leaves//2,body,0,unroll=4)
 
-def near_kernel(base, src_h, cnt_h, nb_h, xb, xo, xa, out, hi, lo, weave, nb, src, cnt, sem, sem2):
+def near_kernel(base, src_h, cnt_h, nb_h, xb, xo, xa, out, hi, lo, weave, acc, nb, src, cnt, sem, sem2):
     n=out.shape[1]//LEAF
     chunks=sem.shape[0]
     size=nb.shape[0]//chunks
@@ -57,7 +57,6 @@
     def step(c,_):
         chunk(c).wait()
         for pair in range(per//2):
-            parts=[]
             for m in range(2):
                 t=c*per+pair*2+m
                 off=pl.multiple_of(t*256,256)
@@ -70,24 +69,24 @@
                 w=jnp.concatenate([jnp.concatenate(even,axis=1),jnp.concatenate(odd,axis=1)],axis=0)
                 live=cnt[t]
                 at=[jnp.where(j<live,src[j,t]-first,3*n) for j in range(8)]
-                parts.append(dotnt(jnp.concatenate([join(hi,at),join(lo,at)],axis=0),jnp.concatenate(split(w),axis=0)))
-            d=dotnn(jnp.concatenate(split(jnp.concatenate(parts,axis=1)),axis=0),weave[...])
-            d=d[:2*RHS]+d[2*RHS:]
-            out[:,pl.ds(pl.multiple_of((c*per+pair*2)*LEAF,128),128)]=d[:RHS]+d[RHS:]
+                d=dotnt(jnp.concatenate([join(hi,at),join(lo,at)],axis=0),jnp.concatenate(split(w),axis=0))
+                acc[pl.ds(pl.multiple_of((c*per+pair*2)*(RHS//2),RHS),RHS),m*128:(m+1)*128]=d[:RHS]+d[RHS:]
         return 0
     lax.fori_loop(0,chunks,step,0)
-
-def near(base,src,cnt,xb,xo,xa,nb,chunks=2):
+    d=dotnn(jnp.concatenate(split(acc[...]),axis=0),weave[...])
+    d=d[:n*RHS//2]+d[n*RHS//2:]
+    for q in range(n//2): out[:,q*128:(q+1)*128]=d[q*RHS:(q+1)*RHS]
+
+def near(base,src,cnt,xb,xo,xa,nb,chunks=4):
     leaves=nb.shape[0]
     view=nb.reshape(leaves,8,32,128).transpose(0,2,1,3).reshape(leaves*256,128)
-    pts=leaves*LEAF
-    blk=pl.BlockSpec((RHS,pts),lambda g:(0,0))
     hbm=pl.BlockSpec(memory_space=HBM)
+    vm=pl.BlockSpec(memory_space=pltpu.VMEM)
     return pl.pallas_call(near_kernel,
-        out_shape=jax.ShapeDtypeStruct((RHS,pts),f32),grid=(1,),
-        in_specs=[pl.BlockSpec(memory_space=pltpu.SMEM),hbm,hbm,hbm,blk,blk,blk],
-        out_specs=blk,
-        scratch_shapes=[pltpu.VMEM((3*leaves+1,RHS,128),bf16)]*2+[pltpu.VMEM((256,128),bf16),pltpu.VMEM((leaves*256,128),f32),
+        out_shape=jax.ShapeDtypeStruct((RHS,leaves*LEAF),f32),
+        in_specs=[pl.BlockSpec(memory_space=pltpu.SMEM),hbm,hbm,hbm,vm,vm,vm],
+        out_specs=vm,
+        scratch_shapes=[pltpu.VMEM((3*leaves+1,RHS,128),bf16)]*2+[pltpu.VMEM((256,128),bf16),pltpu.VMEM((leaves//2*RHS,256),f32),pltpu.VMEM((leaves*256,128),f32),
             pltpu.SMEM((8,leaves),jnp.int32),pltpu.SMEM((leaves,),jnp.int32),pltpu.SemaphoreType.DMA((chunks,)),pltpu.SemaphoreType.DMA((2,))],
         cost_estimate=pl.CostEstimate(flops=10**11,bytes_accessed=10**7,transcendentals=0),
         compiler_params=pltpu.CompilerParams(vmem_limit_bytes=24<<20),
@@ -139,6 +138,7 @@
     same=(iota((256,128),0)//32==lax.rem(iota((256,128),1),8))
     first.wait()
     ext[:,:pts]=x[...]
+    rows=[]
     for g in range(n//8):
         if g*128%size==0: moves[g*128//size].wait()
         blks=[]
@@ -151,7 +151,9 @@
         bh,bl=split(bas[pl.ds(g*128,128),:])
         d=dotnt(jnp.concatenate([xh,xl],axis=1),jnp.concatenate([jnp.concatenate([bh,bh],axis=1),jnp.concatenate([bl,jnp.zeros_like(bl)],axis=1)],axis=0))
         d=jnp.where(same,d[:,:128]+d[:,128:],0.0).reshape(8,32,128).sum(axis=0)
-        ext[:,pl.ds(pts+g*256,256)]=exact(jnp.concatenate([d[:RHS],d[RHS:]],axis=1),s2)
+        rows.append(jnp.concatenate([d[:RHS],d[RHS:]],axis=1))
+    d=exact(jnp.concatenate(rows,axis=0),s2)
+    for g in range(n//8): ext[:,pl.ds(pts+g*256,256)]=d[g*RHS:(g+1)*RHS]
     for m in later: m.wait()
 
 def up(x,basis,transfer,upper,chunks=2):
@@ -193,8 +195,9 @@
         compiler_params=pltpu.CompilerParams(vmem_limit_bytes=24<<20),name="lift")(ext,tra,upper)
 
 def far_kernel(base,src_h,cpl_h,cb,co,ca,out,table,cpl,src,sem,sem2):
-    tiles=co.shape[1]//128
     n=src.shape[1]
+    tiles=n*K//128
+    skip=n*LEAF
     chunks=sem.shape[0]
     size=cpl.shape[0]//chunks
     def chunk(c): return pltpu.make_async_copy(cpl_h.at[pl.ds(c*size,size),:],cpl.at[pl.ds(c*size,size),:],sem.at[c])
@@ -203,10 +206,10 @@
     for c in range(chunks): chunk(c).start()
     for w,ref in ((base[2],cb),(1,co),(2-base[2],ca)):
         def body(q,_):
-            t=ref[:,pl.ds(pl.multiple_of(q*128,128),128)]
+            t=ref[:,pl.ds(pl.multiple_of(skip+q*128,128),128)]
             for m in range(4): table[(w*tiles+q)*4+m]=jnp.concatenate(split(spread4(t,m)),axis=0)
             return 0
-        lax.fori_loop(0,tiles,body,0,unroll=4)
+        lax.fori_loop(0,tiles,body,0,unroll=8)
     idx.wait()
     per=n//chunks
     first=base[0]
@@ -232,12 +235,12 @@
 def far(base,src,eb,eo,ea,coupling,chunks=2):
     n=coupling.shape[0]
     view=coupling.reshape(n,8,8,128).transpose(0,2,1,3).reshape(n*64,128)
-    blk=pl.BlockSpec((RHS,n*K),lambda g:(0,LEAF//K))
+    vm=pl.BlockSpec(memory_space=pltpu.VMEM)
     hbm=pl.BlockSpec(memory_space=HBM)
     return pl.pallas_call(far_kernel,
-        out_shape=jax.ShapeDtypeStruct((n*RHS,2*K),f32),grid=(1,),
-        in_specs=[pl.BlockSpec(memory_space=pltpu.SMEM),hbm,hbm,blk,blk,blk],
-        out_specs=pl.BlockSpec((n*RHS,2*K),lambda g:(0,0)),
+        out_shape=jax.ShapeDtypeStruct((n*RHS,2*K),f32),
+        in_specs=[pl.BlockSpec(memory_space=pltpu.SMEM),hbm,hbm,vm,vm,vm],
+        out_specs=vm,
         scratch_shapes=[pltpu.VMEM((3*n,2*RHS,128),bf16),pltpu.VMEM((n*64,128),f32),pltpu.SMEM((8,n),jnp.int32),
             pltpu.SemaphoreType.DMA((chunks,)),pltpu.SemaphoreType.DMA((1,))],
         compiler_params=pltpu.CompilerParams(vmem_limit_bytes=24<<20),name="far")(base,in_hbm(src.T),in_hbm(view),eb,eo,ea)
@@ -292,29 +295,29 @@
     p12=jnp.concatenate([p1,p1,p2,p2],axis=0)
     left=iota((RHS,128),1)<LEAF
     per=n//nc
+    ds=[]
     for u in range(nc):
         cf=cfar[pl.ds(u*RHS,RHS),:]+down[u*RHS:(u+1)*RHS]
         e=jnp.concatenate([tra[pl.ds(((u*per+i)//8)*64+(u*per+i)%8,8,stride=8),:] for i in range(per)],axis=1)
         eh,el=masked4(e)
         ch,cl=split(cf)
         d=dotnn(jnp.concatenate([ch,cl,ch],axis=1),jnp.concatenate([eh,eh,el],axis=0))
-        d=jnp.concatenate([d[:,i*128:(i+1)*128] for i in range(per)],axis=0)
-        q=dotnn(jnp.concatenate([*split(d),*split(lf[pl.ds(u*per*RHS,per*RHS),:])],axis=1),p12)
-        for b in range(per//8):
-            g=(u*per)//8+b
-            z=q[b*128:(b+1)*128].reshape(8,RHS,256)
-            z=jnp.stack([z[:,:,:128],z[:,:,128:]],axis=1).reshape(256,128)
-            same=(iota((256,128),0)//32==lax.rem(iota((256,128),1),8))
-            zh,zl=split(jnp.where(same,z,0.0))
-            bh,bl=split(bas[pl.ds(g*128,128),:])
-            o=dotnn(jnp.concatenate([zh,zl],axis=1),jnp.concatenate([jnp.concatenate([bh,bl],axis=1),jnp.concatenate([bh,jnp.zeros_like(bl)],axis=1)],axis=0))
-            o=(o[:,:128]+o[:,128:]).reshape(8,2,RHS,128)
-            for m in range(4):
-                a=jnp.where(left,o[2*m,0],o[2*m,1])
-                c=jnp.where(left,o[2*m+1,0],o[2*m+1,1])
-                r=jnp.where(left,a,c)+pltpu.roll(jnp.where(left,c,a),LEAF,1)
-                at=pl.ds(g*512+m*128,128)
-                out[:,at]=near_ref[:,at]+r
+        ds+=[d[:,i*128:(i+1)*128] for i in range(per)]
+    q=dotnn(jnp.concatenate([*split(jnp.concatenate(ds,axis=0)),*split(lf[...])],axis=1),p12)
+    same=(iota((256,128),0)//32==lax.rem(iota((256,128),1),8))
+    for g in range(n//8):
+        z=q[g*128:(g+1)*128].reshape(8,RHS,256)
+        z=jnp.stack([z[:,:,:128],z[:,:,128:]],axis=1).reshape(256,128)
+        zh,zl=split(jnp.where(same,z,0.0))
+        bh,bl=split(bas[pl.ds(g*128,128),:])
+        o=dotnn(jnp.concatenate([zh,zl],axis=1),jnp.concatenate([jnp.concatenate([bh,bl],axis=1),jnp.concatenate([bh,jnp.zeros_like(bl)],axis=1)],axis=0))
+        o=(o[:,:128]+o[:,128:]).reshape(8,2,RHS,128)
+        for m in range(4):
+            a=jnp.where(left,o[2*m,0],o[2*m,1])
+            c=jnp.where(left,o[2*m+1,0],o[2*m+1,1])
+            r=jnp.where(left,a,c)+pltpu.roll(jnp.where(left,c,a),LEAF,1)
+            at=pl.ds(g*512+m*128,128)
+            out[:,at]=near_ref[:,at]+r
 
 def down(base,sums,cfar,gcp,upper,tra,basis,lf,nearv):
     n=basis.shape[0]; nc=upper.shape[0]; ng=gcp.shape[0]

time: 48.5 us -> 46.8 us (0.965)
  Pallas kernels: 24.2 us -> 19.3 us
  waiting for transfers between devices: 0.47 us -> 3.01 us
  blocking collectives: 2.79 us -> 3.48 us
    pallas_call x1, Pallas kernels: 9.23 us -> 6.57 us  [near(): pl.pallas_call(near_kernel, out_shape=jax.ShapeDtypeStruct((RHS, leaves *...]
    all_to_all x1, waiting for transfers between devices: 0.01 us -> 2.54 us  [per_device(): lax.all_to_all(rep, 'leaf', 0, 0, tiled=True, axis_index_groups=across(de...]
    pallas_call x1, Pallas kernels: 2.91 us -> 1.9 us  [up(): pl.pallas_call(up_kernel, out_shape=(jax.ShapeDtypeStruct((RHS, n * (LEAF...]
    all_gather x1, blocking collectives: 2.79 us -> 3.48 us  [per_device(): lax.all_gather(some, 'leaf', axis=0, tiled=True, axis_index_groups=[[2 *...]
    pallas_call x1, Pallas kernels: 3.94 us -> 3.33 us  [down(): pl.pallas_call(down_kernel, out_shape=jax.ShapeDtypeStruct((RHS, n * LEAF...]
    pallas_call x1, Pallas kernels: 4.78 us -> 4.22 us  [far(): pl.pallas_call(far_kernel, out_shape=jax.ShapeDtypeStruct((n * RHS, 2 * K...]
  transfers between devices with their start and end apart: 6 -> 6, of which waited for: 1 -> 2; matrix products, arithmetic and copies ran while one was open for 0% -> 0% of each run, Pallas kernels for 36% -> 30%
where the time goes in v6:
time: 46.8 us; the launch traced here: 46.6 us
  starting transfers between devices  20.5 us (44%)
  Pallas kernels  19.3 us (41%)
  blocking collectives  3.48 us (7%)
  waiting for transfers between devices  3.01 us (6%)
    all_to_all x1, starting transfers between devices, per_device(): lax.all_to_all(rep, 'leaf', 0, 0, tiled=True, axis_index_groups=across(de...  10.4 us
    pallas_call x1, Pallas kernels, near(): pl.pallas_call(near_kernel, out_shape=jax.ShapeDtypeStruct((RHS, leaves *...  6.57 us
    ppermute x3, starting transfers between devices, per_device(): lax.ppermute(total, 'group', [(i, (i + k) % ng) for i in range(ng)])  4.91 us
    pallas_call x1, Pallas kernels, far(): pl.pallas_call(far_kernel, out_shape=jax.ShapeDtypeStruct((n * RHS, 2 * K...  4.22 us
    all_gather x1, blocking collectives, per_device(): lax.all_gather(some, 'leaf', axis=0, tiled=True, axis_index_groups=[[2 *...  3.48 us
    pallas_call x1, Pallas kernels, down(): pl.pallas_call(down_kernel, out_shape=jax.ShapeDtypeStruct((RHS, n * LEAF...  3.33 us
    ppermute x1, starting transfers between devices, per_device(): eb = lax.ppermute(ext, both, [(i, i ^ 1) for i in range(every)])  3.33 us
    all_to_all x1, waiting for transfers between devices, per_device(): lax.all_to_all(rep, 'leaf', 0, 0, tiled=True, axis_index_groups=across(de...  2.54 us
  transfers between devices with their start and end apart: 6, of which 2 were waited for; matrix products, arithmetic and copies ran while one was open for 0% of the time, Pallas kernels for 30%

profile of v6, /device:TPU:1, one launch (start us, length us, event | category | flops | bytes accessed | tf_op | source)
XLA Modules:
  0.0 46.6 jit_solution(14342304176124010263)
XLA Ops:
  0.0 1.9 %up.1 = (f32[16,6144]{1,0:T(8,128)S(1)}, f32[512,128]{1,0:T(8,128)S(1)}, f32[4,1024]{1,0:T(4,128)S(1)}) custom-call(f32[16,4096]{1,0:T(8,128)} %x_h.1, f32[1024,128]{1,0:T(8,128)} %bitcast.31, f32[512,128]{1,0:T(8,128)} %bitcast.36, f32[4,1024]{1,0:T(4,128)} %upt_h.1), custom_call_target="tpu_custom_call" | custom-call | tf_op jit(solution)/shard_map/up/pallas_call | solution.py:163
  1.9 3.3 %collective-permute-start = (f32[16,6144]{1,0:T(8,128)S(1)}, f32[16,6144]{1,0:T(8,128)S(1)}, u32[]{:S(2)}, u32[]{:S(2)}) collective-permute-start(f32[16,6144]{1,0:T(8,128)S(1)} %get-tuple-element.11.ext.xo.co), channel_id=1, source_target_pairs={{0,1},{1,0},{2,3},{3,2},{4,5},{5,4},{6,7},{7,6},{8,9},{9,8},{10,11... | collective-permute-start | bytes 1179656 | tf_op jit(solution)/shard_map/ppermute | solution.py:343
  5.2 1.9 %collective-permute-start.1 = (f32[16,6144]{1,0:T(8,128)S(1)}, f32[16,6144]{1,0:T(8,128)S(1)}, u32[]{:S(2)}, u32[]{:S(2)}) collective-permute-start(f32[16,6144]{1,0:T(8,128)S(1)} %get-tuple-element.11.ext.xo.co), channel_id=1, source_target_pairs={{1,2},{2,1},{3,4},{4,3},{5,6},{6,5},{7,8},{8,7},{9,10},{10,9},{11,... | collective-permute-start | bytes 1179656 | tf_op jit(solution)/shard_map/ppermute | solution.py:344
  7.2 2.1 %lift.1 = f32[32,5,4,128]{3,2,1,0:T(4,128)} custom-call(f32[16,6144]{1,0:T(8,128)S(1)} %get-tuple-element.11.ext.xo.co, f32[512,128]{1,0:T(8,128)S(1)} %get-tuple-element.12.tra, f32[4,1024]{1,0:T(4,128)S(1)} %get-tuple-element.13.upt), custom_call_target="tpu_custom_call" | custom-call | tf_op jit(solution)/shard_map/lift/pallas_call | solution.py:191
  9.2 10.4 %all-to-all-start = ((f32[32,5,4,128]{3,2,1,0:T(4,128)}), f32[32,5,4,128]{3,2,1,0:T(4,128)S(1)}, u32[]{:S(2)}, u32[]{:S(2)}) async-start(f32[32,5,4,128]{3,2,1,0:T(4,128)} %lift.1), calls=%async_computation | async-start | bytes 655360 | tf_op jit(solution)/shard_map/all_to_all | solution.py:346
  19.6 0.1 pad_add_fusion.base
  19.7 0.0 collective-permute-done.xb.cb
  19.7 0.0 collective-permute-done.1.xa.ca
  19.7 0.0 copy-start.3
  19.7 6.6 %near.1.near_ref = f32[16,4096]{1,0:T(8,128)S(1)} custom-call(s32[3]{0:T(128)S(1)} %pad_add_fusion.base, s32[8,64]{1,0:T(8,128)} %bitcast.39, s32[64]{0:T(128)} %cnt_h.1, f32[16384,128]{1,0:T(8,128)} %bitcast.38, f32[16,6144]{1,0:T(8,128)S(1)} %collective-permute-done.xb.cb, f32[16,6144]{1,0:T(8,128)S(1)} %get-tuple-element.11.ext.xo.co, ...), custom_call_target="tpu_custom_call" | custom-call | flops 99999997952 | bytes 10000000 | tf_op jit(solution)/shard_map/near/pallas_call | solution.py:85
  26.3 4.2 %far.1.lf = f32[1024,64]{1,0:T(8,128)S(1)} custom-call(s32[3]{0:T(128)S(1)} %pad_add_fusion.base, s32[8,64]{1,0:T(8,128)} %bitcast.37, f32[4096,128]{1,0:T(8,128)} %bitcast.35, f32[16,6144]{1,0:T(8,128)S(1)} %collective-permute-done.xb.cb, f32[16,6144]{1,0:T(8,128)S(1)} %get-tuple-element.11.ext.xo.co, f32[16,6144]{1,0:T(8,128)S(1)} %collective-permute-done.1.xa.ca), custom_call_target="tpu_custom_call" | custom-call | tf_op jit(solution)/shard_map/far/pallas_call | solution.py:240
  30.5 2.5 %all-to-all-done = f32[32,5,4,128]{3,2,1,0:T(4,128)S(1)} async-done(((f32[32,5,4,128]{3,2,1,0:T(4,128)}), f32[32,5,4,128]{3,2,1,0:T(4,128)S(1)}, u32[]{:S(2)}, u32[]{:S(2)}) %all-to-all-start) | async-done | bytes 327712 | tf_op jit(solution)/shard_map/all_to_all | solution.py:346
  33.1 3.5 %all_gather.3.pays = f32[64,5,4,128]{3,2,1,0:T(4,128)S(1)} all-gather(f32[32,5,4,128]{3,2,1,0:T(4,128)S(1)} %all-to-all-done), channel_id=1, replica_groups={{0,1},{2,3},{4,5},{6,7},{8,9},{10,11},{12,13},{14,15},{16,17},{18,19},{..., dimensions={0}, use_global_device_ids=true | all-gather | bytes 983040 | tf_op jit(solution)/shard_map/all_gather | solution.py:350
  36.6 0.1 slice_reduce_fusion.s0
  36.6 1.3 %collective-permute-start.2 = (f32[4,128]{1,0:T(4,128)S(1)}, f32[4,128]{1,0:T(4,128)S(1)}, u32[]{:S(2)}, u32[]{:S(2)}) collective-permute-start(f32[4,128]{1,0:T(4,128)S(1)} %slice_reduce_fusion.s0), channel_id=1, source_target_pairs={{0,64},{64,128},{128,192},{192,0},{1,65},{65,129},{129,193},{193,1... | collective-permute-start | bytes 6152 | tf_op jit(solution)/shard_map/ppermute | solution.py:352
  37.9 2.6 %collective-permute-start.3 = (f32[4,128]{1,0:T(4,128)S(1)}, f32[4,128]{1,0:T(4,128)S(1)}, u32[]{:S(2)}, u32[]{:S(2)}) collective-permute-start(f32[4,128]{1,0:T(4,128)S(1)} %slice_reduce_fusion.s0), channel_id=1, source_target_pairs={{0,128},{64,192},{128,0},{192,64},{1,129},{65,193},{129,1},{193,65... | collective-permute-start | bytes 6152 | tf_op jit(solution)/shard_map/ppermute | solution.py:352
  40.5 1.0 %collective-permute-start.4 = (f32[4,128]{1,0:T(4,128)S(1)}, f32[4,128]{1,0:T(4,128)S(1)}, u32[]{:S(2)}, u32[]{:S(2)}) collective-permute-start(f32[4,128]{1,0:T(4,128)S(1)} %slice_reduce_fusion.s0), channel_id=1, source_target_pairs={{0,192},{64,0},{128,64},{192,128},{1,193},{65,1},{129,65},{193,129... | collective-permute-start | bytes 6152 | tf_op jit(solution)/shard_map/ppermute | solution.py:352
  41.5 0.0 copy-done.2
  41.6 1.2 %gather.1.cfar = f32[64,32]{1,0:T(8,128)S(1)} custom-call(s32[4,8]{1,0:T(4,128)S(1)} %copy-done.3, f32[64,5,4,128]{3,2,1,0:T(4,128)S(1)} %all_gather.3.pays, f32[256,128]{1,0:T(8,128)S(1)} %bitcast.34), custom_call_target="tpu_custom_call" | custom-call | flops 10000000000 | bytes 10000000 | tf_op jit(solution)/shard_map/gather/pallas_call | solution.py:264
  42.8 0.0 collective-permute-done.2.s1
  42.8 0.0 collective-permute-done.3.s2
  42.8 0.5 collective-permute-done.4.s3
  43.3 0.0 copy-done.1
  43.3 3.3 %down.1 = f32[16,4096]{1,0:T(8,128)} custom-call(s32[3]{0:T(128)S(1)} %pad_add_fusion.base, f32[4,128]{1,0:T(4,128)S(1)} %slice_reduce_fusion.s0, f32[4,128]{1,0:T(4,128)S(1)} %collective-permute-done.2.s1, f32[4,128]{1,0:T(4,128)S(1)} %collective-permute-done.3.s2, f32[4,128]{1,0:T(4,128)S(1)} %collective-permute-done.4.s3, f32[64,32]{1,0:T(8,128)S(1)} %gather.1.cfar, ...), custom_call_target="tpu_custom_call" | custom-call | tf_op jit(solution)/shard_map/down/pallas_call | solution.py:326
  (5 shorter events, 0.0 us)
Async XLA Ops:
  1.9 17.8 %collective-permute-start = (f32[16,6144]{1,0:T(8,128)S(1)}, f32[16,6144]{1,0:T(8,128)S(1)}, u32[]{:S(2)}, u32[]{:S(2)}) collective-permute-start(f32[16,6144]{1,0:T(8,128)S(1)} %get-tuple-element.11.ext.xo.co), channel_id=1, source_target_pairs={{0,1},{1,0},{2,3},{3,2},{4,5},{5,4},{6,7},{7,6},{8,9},{9,8},{10,11... | collective-permute-start | bytes 1179656 | tf_op jit(solution)/shard_map/ppermute | solution.py:343
  5.2 14.5 %collective-permute-start.1 = (f32[16,6144]{1,0:T(8,128)S(1)}, f32[16,6144]{1,0:T(8,128)S(1)}, u32[]{:S(2)}, u32[]{:S(2)}) collective-permute-start(f32[16,6144]{1,0:T(8,128)S(1)} %get-tuple-element.11.ext.xo.co), channel_id=1, source_target_pairs={{1,2},{2,1},{3,4},{4,3},{5,6},{6,5},{7,8},{8,7},{9,10},{10,9},{11,... | collective-permute-start | bytes 1179656 | tf_op jit(solution)/shard_map/ppermute | solution.py:344
  9.2 23.8 %all-to-all-start = ((f32[32,5,4,128]{3,2,1,0:T(4,128)}), f32[32,5,4,128]{3,2,1,0:T(4,128)S(1)}, u32[]{:S(2)}, u32[]{:S(2)}) async-start(f32[32,5,4,128]{3,2,1,0:T(4,128)} %lift.1), calls=%async_computation | async-start | bytes 655360 | tf_op jit(solution)/shard_map/all_to_all | solution.py:346
  19.7 21.8 %copy-start.2 = (f32[4,8,1024]{2,1,0:T(8,128)S(1)}, f32[4,8,1024]{2,1,0:T(8,128)}, u32[]{:S(2)}) copy-start(f32[4,8,1024]{2,1,0:T(8,128)} %param.21) | copy-start | bytes 393220
  19.7 21.8 %copy-start.3 = (s32[4,8]{1,0:T(4,128)S(1)}, s32[4,8]{1,0:T(4,128)}, u32[]{:S(2)}) copy-start(s32[4,8]{1,0:T(4,128)} %csrc.1) | copy-start | bytes 388
  36.6 6.2 %collective-permute-start.2 = (f32[4,128]{1,0:T(4,128)S(1)}, f32[4,128]{1,0:T(4,128)S(1)}, u32[]{:S(2)}, u32[]{:S(2)}) collective-permute-start(f32[4,128]{1,0:T(4,128)S(1)} %slice_reduce_fusion.s0), channel_id=1, source_target_pairs={{0,64},{64,128},{128,192},{192,0},{1,65},{65,129},{129,193},{193,1... | collective-permute-start | bytes 6152 | tf_op jit(solution)/shard_map/ppermute | solution.py:352
  37.9 4.9 %collective-permute-start.3 = (f32[4,128]{1,0:T(4,128)S(1)}, f32[4,128]{1,0:T(4,128)S(1)}, u32[]{:S(2)}, u32[]{:S(2)}) collective-permute-start(f32[4,128]{1,0:T(4,128)S(1)} %slice_reduce_fusion.s0), channel_id=1, source_target_pairs={{0,128},{64,192},{128,0},{192,64},{1,129},{65,193},{129,1},{193,65... | collective-permute-start | bytes 6152 | tf_op jit(solution)/shard_map/ppermute | solution.py:352
  40.5 2.7 %collective-permute-start.4 = (f32[4,128]{1,0:T(4,128)S(1)}, f32[4,128]{1,0:T(4,128)S(1)}, u32[]{:S(2)}, u32[]{:S(2)}) collective-permute-start(f32[4,128]{1,0:T(4,128)S(1)} %slice_reduce_fusion.s0), channel_id=1, source_target_pairs={{0,192},{64,0},{128,64},{192,128},{1,193},{65,1},{129,65},{193,129... | collective-permute-start | bytes 6152 | tf_op jit(solution)/shard_map/ppermute | solution.py:352
  41.6 1.7 %copy-start = (f32[64,2048]{1,0:T(8,128)S(1)}, f32[64,2048]{1,0:T(8,128)}, u32[]{:S(2)}) copy-start(f32[64,2048]{1,0:T(8,128)} %param.16) | copy-start | bytes 1572868
  41.6 1.7 %copy-start.1 = (f32[1,4,1024]{2,1,0:T(4,128)S(1)}, f32[1,4,1024]{2,1,0:T(4,128)}, u32[]{:S(2)}) copy-start(f32[1,4,1024]{2,1,0:T(4,128)} %param.23) | copy-start | bytes 49156

commit v7 on v6

--- a/solution.py
+++ b/solution.py
@@ -166,33 +166,45 @@
         scratch_shapes=[pltpu.VMEM(x.shape,f32),pltpu.VMEM(bas.shape,f32),pltpu.SemaphoreType.DMA((chunks+1,)),pltpu.SemaphoreType.DMA((2,))],
         compiler_params=pltpu.CompilerParams(vmem_limit_bytes=24<<20),name="up")(in_hbm(x),in_hbm(bas),in_hbm(tra),in_hbm(upper))
 
-def lift_kernel(ext,tra,upt,rep,fs):
-    nc=upt.shape[0]
-    n=tra.shape[0]//8
-    per=n//nc
-    pts=n*LEAF
-    outs=[]
-    for u in range(nc):
-        e=jnp.concatenate([tra[pl.ds(((u*per+i)//8)*64+(u*per+i)%8,8,stride=8),:] for i in range(per)],axis=1)
-        v=[spread4(ext[:,pl.ds(pts+(u*per+i)//4*128,128)],i%4) for i in range(per)]
-        outs.append(mul3(jnp.concatenate(v,axis=1),masked4(e)))
-    row=iota((128,128),0); col=iota((128,128),1)
-    s3=onehot(col==row//32*32+lax.rem(row,8)*4+lax.rem(row,32)//8)
-    cc=exact(jnp.concatenate(outs,axis=1),s3)
-    for q in range(8):
-        fs[pl.ds(q*nc,nc),:]=upt[:,pl.ds(q*128,128)]
-    f=jnp.concatenate([fs[pl.ds(u,8,stride=nc),:] for u in range(nc)],axis=1)
-    pr=mul3(jnp.concatenate([spread4(cc,u) for u in range(nc)],axis=1),masked4(f))
-    pay=[cc[4*i:4*i+4] for i in range(4)]+[jnp.concatenate([pr[4*i:4*i+4] for i in range(4)],axis=1)]
-    for c in range(rep.shape[0]):
-        for i in range(5): rep[c,i]=pay[i]
-
-def lift(ext,tra,upper,copies):
-    return pl.pallas_call(lift_kernel,
-        out_shape=jax.ShapeDtypeStruct((copies,5,4,128),f32),
-        in_specs=[pl.BlockSpec(memory_space=pltpu.VMEM)]*3,
-        scratch_shapes=[pltpu.VMEM((8*upper.shape[0],128),f32)],
-        compiler_params=pltpu.CompilerParams(vmem_limit_bytes=24<<20),name="lift")(ext,tra,upper)
+def lift_kernel(turn,base,ext,tra,upt,*rest):
+    out,fs,rep,sem=rest[-4:]
+    @pl.when(base[3]==turn)
+    def _():
+        nc=upt.shape[0]
+        n=tra.shape[0]//8
+        per=n//nc
+        pts=n*LEAF
+        outs=[]
+        for u in range(nc):
+            e=jnp.concatenate([tra[pl.ds(((u*per+i)//8)*64+(u*per+i)%8,8,stride=8),:] for i in range(per)],axis=1)
+            v=[spread4(ext[:,pl.ds(pts+(u*per+i)//4*128,128)],i%4) for i in range(per)]
+            outs.append(mul3(jnp.concatenate(v,axis=1),masked4(e)))
+        row=iota((128,128),0); col=iota((128,128),1)
+        s3=onehot(col==row//32*32+lax.rem(row,8)*4+lax.rem(row,32)//8)
+        cc=exact(jnp.concatenate(outs,axis=1),s3)
+        for q in range(8):
+            fs[pl.ds(q*nc,nc),:]=upt[:,pl.ds(q*128,128)]
+        f=jnp.concatenate([fs[pl.ds(u,8,stride=nc),:] for u in range(nc)],axis=1)
+        pr=mul3(jnp.concatenate([spread4(cc,u) for u in range(nc)],axis=1),masked4(f))
+        pay=[cc[4*i:4*i+4] for i in range(4)]+[jnp.concatenate([pr[4*i:4*i+4] for i in range(4)],axis=1)]
+        for c in range(rep.shape[0]):
+            for i in range(5): rep[c,i]=pay[i]
+        move=pltpu.make_async_copy(rep,out,sem)
+        move.start()
+        move.wait()
+
+def lift(turn,base,ext,tra,upper,copies,given=None):
+    vm=pl.BlockSpec(memory_space=pltpu.VMEM)
+    hbm=pl.BlockSpec(memory_space=HBM)
+    more=[] if given is None else [given]
+    shape=(copies,5,4,128)
+    return pl.pallas_call(functools.partial(lift_kernel,turn),
+        out_shape=jax.ShapeDtypeStruct(shape,f32),
+        in_specs=[pl.BlockSpec(memory_space=pltpu.SMEM)]+[vm]*3+[hbm]*len(more),
+        out_specs=hbm,
+        input_output_aliases={4:0} if more else {},
+        scratch_shapes=[pltpu.VMEM((8*upper.shape[0],128),f32),pltpu.VMEM(shape,f32),pltpu.SemaphoreType.DMA],
+        compiler_params=pltpu.CompilerParams(vmem_limit_bytes=24<<20),name="lift")(base,ext,tra,upper,*more)
 
 def far_kernel(base,src_h,cpl_h,cb,co,ca,out,table,cpl,src,sem,sem2):
     n=src.shape[1]
@@ -338,11 +350,13 @@
     devs=lax.axis_size("leaf")
     every=lax.axis_size(both)
     ng=lax.axis_size("group")
-    base=jnp.stack([(lax.axis_index(both)-1)*leaves,lax.axis_index("group"),2*lax.rem(lax.axis_index("leaf")+1,2)]).astype(jnp.int32)
+    base=jnp.stack([(lax.axis_index(both)-1)*leaves,lax.axis_index("group"),2*lax.rem(lax.axis_index("leaf")+1,2),lax.axis_index("leaf")//(devs-1)]).astype(jnp.int32)
     ext,tra,upper=up(right_sides,basis,leaf_transfer,cluster_transfer)
     eb=lax.ppermute(ext,both,[(i,i^1) for i in range(every)])
-    ea=lax.ppermute(ext,both,[p for i in range(1,every-1,2) for p in ((i,i+1),(i+1,i))])
-    rep=lift(ext,tra,upper,devs//2)
+    rep=lift(0,base,ext,tra,upper,devs//2)
+    ext2,rep=lax.optimization_barrier((ext,rep))
+    ea=lax.ppermute(ext2,both,[p for i in range(1,every-1,2) for p in ((i,i+1),(i+1,i))])
+    rep=lift(1,base,ext,tra,upper,devs//2,rep)
     some=lax.all_to_all(rep,"leaf",0,0,tiled=True,axis_index_groups=across(devs))
     nearv=near(base,near_source,near_count,eb,ext,ea,near_blocks)
     lf=far(base,leaf_source,eb,ext,ea,leaf_coupling)

time: 46.8 us -> 48.2 us (1.030)
  Pallas kernels: 19.3 us -> 20.5 us
  starting transfers between devices: 20.5 us -> 19.3 us
  blocking collectives: 3.48 us -> 4.3 us
  waiting for transfers between devices: 3.01 us -> 3.6 us
    ppermute x1, starting transfers between devices: 3.33 us -> 0.09 us  [per_device(): eb = lax.ppermute(ext, both, [(i, i ^ 1) for i in range(every)])]
    ppermute x1, starting transfers between devices: 1.91 us -> 4.59 us  [per_device(): lax.ppermute(ext2, both, [p for i in range(1, every - 1, 2) for p in ((i,...]
    ppermute x3, waiting for transfers between devices: 0.47 us -> 1.79 us  [per_device(): lax.ppermute(total, 'group', [(i, (i + k) % ng) for i in range(ng)])]
    ppermute x3, starting transfers between devices: 4.91 us -> 3.67 us  [per_device(): lax.ppermute(total, 'group', [(i, (i + k) % ng) for i in range(ng)])]
    pallas_call x1 -> x2, Pallas kernels: 2.09 us -> 3.2 us  [lift(): pl.pallas_call(functools.partial(lift_kernel, turn), out_shape=jax.ShapeD...]
    all_gather x1, blocking collectives: 3.48 us -> 4.3 us  [per_device(): lax.all_gather(some, 'leaf', axis=0, tiled=True, axis_index_groups=[[2 *...]
    all_to_all x1, waiting for transfers between devices: 2.54 us -> 1.8 us  [per_device(): lax.all_to_all(rep, 'leaf', 0, 0, tiled=True, axis_index_groups=across(de...]
    all_to_all x1, starting transfers between devices: 10.4 us -> 10.9 us  [per_device(): lax.all_to_all(rep, 'leaf', 0, 0, tiled=True, axis_index_groups=across(de...]
  transfers between devices with their start and end apart: 6 -> 6, of which waited for: 2 -> 3; matrix products, arithmetic and copies ran while one was open for 0% -> 0% of each run, Pallas kernels for 30% -> 26%
where the time goes in v7:
time: 48.2 us; the launch traced here: 47.9 us
  Pallas kernels  20.5 us (43%)
  starting transfers between devices  19.3 us (40%)
  blocking collectives  4.3 us (9%)
  waiting for transfers between devices  3.6 us (7%)
    all_to_all x1, starting transfers between devices, per_device(): lax.all_to_all(rep, 'leaf', 0, 0, tiled=True, axis_index_groups=across(de...  10.9 us
    pallas_call x1, Pallas kernels, near(): pl.pallas_call(near_kernel, out_shape=jax.ShapeDtypeStruct((RHS, leaves *...  6.58 us
    ppermute x1, starting transfers between devices, per_device(): lax.ppermute(ext2, both, [p for i in range(1, every - 1, 2) for p in ((i,...  4.59 us
    all_gather x1, blocking collectives, per_device(): lax.all_gather(some, 'leaf', axis=0, tiled=True, axis_index_groups=[[2 *...  4.3 us
    pallas_call x1, Pallas kernels, far(): pl.pallas_call(far_kernel, out_shape=jax.ShapeDtypeStruct((n * RHS, 2 * K...  4.22 us
    ppermute x3, starting transfers between devices, per_device(): lax.ppermute(total, 'group', [(i, (i + k) % ng) for i in range(ng)])  3.67 us
    pallas_call x1, Pallas kernels, down(): pl.pallas_call(down_kernel, out_shape=jax.ShapeDtypeStruct((RHS, n * LEAF...  3.33 us
    pallas_call x2, Pallas kernels, lift(): pl.pallas_call(functools.partial(lift_kernel, turn), out_shape=jax.ShapeD...  3.2 us
  transfers between devices with their start and end apart: 6, of which 3 were waited for; matrix products, arithmetic and copies ran while one was open for 0% of the time, Pallas kernels for 26%

profile of v7, /device:TPU:1, one launch (start us, length us, event | category | flops | bytes accessed | tf_op | source)
XLA Modules:
  0.0 47.9 jit_solution(13452897199807963046)
XLA Ops:
  0.0 0.1 pad_add_fusion.base
  0.1 1.9 %up.1 = (f32[16,6144]{1,0:T(8,128)S(1)}, f32[512,128]{1,0:T(8,128)S(1)}, f32[4,1024]{1,0:T(4,128)S(1)}) custom-call(f32[16,4096]{1,0:T(8,128)} %x_h.1, f32[1024,128]{1,0:T(8,128)} %bitcast.32, f32[512,128]{1,0:T(8,128)} %bitcast.37, f32[4,1024]{1,0:T(4,128)} %upt_h.1), custom_call_target="tpu_custom_call" | custom-call | tf_op jit(solution)/shard_map/up/pallas_call | solution.py:163
  2.0 2.6 %lift.2.rest_0_ = f32[32,5,4,128]{3,2,1,0:T(4,128)} custom-call(s32[4]{0:T(128)S(1)} %pad_add_fusion.base, f32[16,6144]{1,0:T(8,128)S(1)} %get-tuple-element.17.ext.xo.co, f32[512,128]{1,0:T(8,128)S(1)} %get-tuple-element.14.tra, f32[4,1024]{1,0:T(4,128)S(1)} %get-tuple-element.15.upt), custom_call_target="tpu_custom_call" | custom-call | tf_op jit(solution)/shard_map/lift/pallas_call | solution.py:201
  4.6 4.6 %collective-permute-start.1 = (f32[16,6144]{1,0:T(8,128)S(1)}, f32[16,6144]{1,0:T(8,128)S(1)}, u32[]{:S(2)}, u32[]{:S(2)}) collective-permute-start(f32[16,6144]{1,0:T(8,128)S(1)} %get-tuple-element.17.ext.xo.co), channel_id=1, source_target_pairs={{1,2},{2,1},{3,4},{4,3},{5,6},{6,5},{7,8},{8,7},{9,10},{10,9},{11,... | collective-permute-start | bytes 1179656 | tf_op jit(solution)/shard_map/ppermute | solution.py:358
  9.2 0.1 collective-permute-start
  9.3 0.6 %lift.3 = f32[32,5,4,128]{3,2,1,0:T(4,128)} custom-call(s32[4]{0:T(128)S(1)} %pad_add_fusion.base, f32[16,6144]{1,0:T(8,128)S(1)} %get-tuple-element.17.ext.xo.co, f32[512,128]{1,0:T(8,128)S(1)} %get-tuple-element.14.tra, f32[4,1024]{1,0:T(4,128)S(1)} %get-tuple-element.15.upt, f32[32,5,4,128]{3,2,1,0:T(4,128)} %lift.2.rest_0_), custom_call_target="tpu_custom_call", output_to_operand_aliasing={{}: (4, {})} | custom-call | tf_op jit(solution)/shard_map/lift/pallas_call | solution.py:201
  9.9 10.9 %all-to-all-start = ((f32[32,5,4,128]{3,2,1,0:T(4,128)}), f32[32,5,4,128]{3,2,1,0:T(4,128)S(1)}, u32[]{:S(2)}, u32[]{:S(2)}) async-start(f32[32,5,4,128]{3,2,1,0:T(4,128)} %lift.3), calls=%async_computation | async-start | bytes 655360 | tf_op jit(solution)/shard_map/all_to_all | solution.py:360
  20.8 0.0 collective-permute-done.1.xa.ca
  20.9 0.0 collective-permute-done.xb.cb
  20.9 0.0 copy-start.2
  20.9 0.0 copy-start.3
  20.9 6.6 %near.1.near_ref = f32[16,4096]{1,0:T(8,128)S(1)} custom-call(s32[4]{0:T(128)S(1)} %pad_add_fusion.base, s32[8,64]{1,0:T(8,128)} %bitcast.40, s32[64]{0:T(128)} %cnt_h.1, f32[16384,128]{1,0:T(8,128)} %bitcast.39, f32[16,6144]{1,0:T(8,128)S(1)} %collective-permute-done.xb.cb, f32[16,6144]{1,0:T(8,128)S(1)} %get-tuple-element.17.ext.xo.co, ...), custom_call_target="tpu_custom_call" | custom-call | flops 99999997952 | bytes 10000000 | tf_op jit(solution)/shard_map/near/pallas_call | solution.py:85
  27.5 4.2 %far.1.lf = f32[1024,64]{1,0:T(8,128)S(1)} custom-call(s32[4]{0:T(128)S(1)} %pad_add_fusion.base, s32[8,64]{1,0:T(8,128)} %bitcast.38, f32[4096,128]{1,0:T(8,128)} %bitcast.36, f32[16,6144]{1,0:T(8,128)S(1)} %collective-permute-done.xb.cb, f32[16,6144]{1,0:T(8,128)S(1)} %get-tuple-element.17.ext.xo.co, f32[16,6144]{1,0:T(8,128)S(1)} %collective-permute-done.1.xa.ca), custom_call_target="tpu_custom_call" | custom-call | tf_op jit(solution)/shard_map/far/pallas_call | solution.py:252
  31.7 1.8 %all-to-all-done = f32[32,5,4,128]{3,2,1,0:T(4,128)S(1)} async-done(((f32[32,5,4,128]{3,2,1,0:T(4,128)}), f32[32,5,4,128]{3,2,1,0:T(4,128)S(1)}, u32[]{:S(2)}, u32[]{:S(2)}) %all-to-all-start) | async-done | bytes 327712 | tf_op jit(solution)/shard_map/all_to_all | solution.py:360
  33.5 4.3 %all_gather.3.pays = f32[64,5,4,128]{3,2,1,0:T(4,128)S(1)} all-gather(f32[32,5,4,128]{3,2,1,0:T(4,128)S(1)} %all-to-all-done), channel_id=1, replica_groups={{0,1},{2,3},{4,5},{6,7},{8,9},{10,11},{12,13},{14,15},{16,17},{18,19},{..., dimensions={0}, use_global_device_ids=true | all-gather | bytes 983040 | tf_op jit(solution)/shard_map/all_gather | solution.py:364
  37.8 0.1 slice_reduce_fusion.s0
  37.9 2.5 %collective-permute-start.4 = (f32[4,128]{1,0:T(4,128)S(1)}, f32[4,128]{1,0:T(4,128)S(1)}, u32[]{:S(2)}, u32[]{:S(2)}) collective-permute-start(f32[4,128]{1,0:T(4,128)S(1)} %slice_reduce_fusion.s0), channel_id=1, source_target_pairs={{0,192},{64,0},{128,64},{192,128},{1,193},{65,1},{129,65},{193,129... | collective-permute-start | bytes 6152 | tf_op jit(solution)/shard_map/ppermute | solution.py:366
  40.4 0.5 %collective-permute-start.3 = (f32[4,128]{1,0:T(4,128)S(1)}, f32[4,128]{1,0:T(4,128)S(1)}, u32[]{:S(2)}, u32[]{:S(2)}) collective-permute-start(f32[4,128]{1,0:T(4,128)S(1)} %slice_reduce_fusion.s0), channel_id=1, source_target_pairs={{0,128},{64,192},{128,0},{192,64},{1,129},{65,193},{129,1},{193,65... | collective-permute-start | bytes 6152 | tf_op jit(solution)/shard_map/ppermute | solution.py:366
  40.9 0.6 %collective-permute-start.2 = (f32[4,128]{1,0:T(4,128)S(1)}, f32[4,128]{1,0:T(4,128)S(1)}, u32[]{:S(2)}, u32[]{:S(2)}) collective-permute-start(f32[4,128]{1,0:T(4,128)S(1)} %slice_reduce_fusion.s0), channel_id=1, source_target_pairs={{0,64},{64,128},{128,192},{192,0},{1,65},{65,129},{129,193},{193,1... | collective-permute-start | bytes 6152 | tf_op jit(solution)/shard_map/ppermute | solution.py:366
  41.6 1.2 %gather.1.cfar = f32[64,32]{1,0:T(8,128)S(1)} custom-call(s32[4,8]{1,0:T(4,128)S(1)} %copy-done.3, f32[64,5,4,128]{3,2,1,0:T(4,128)S(1)} %all_gather.3.pays, f32[256,128]{1,0:T(8,128)S(1)} %bitcast.35), custom_call_target="tpu_custom_call" | custom-call | flops 10000000000 | bytes 10000000 | tf_op jit(solution)/shard_map/gather/pallas_call | solution.py:276
  42.8 0.0 collective-permute-done.4.s3
  42.8 1.6 %collective-permute-done.3.s2 = f32[4,128]{1,0:T(4,128)S(1)} collective-permute-done((f32[4,128]{1,0:T(4,128)S(1)}, f32[4,128]{1,0:T(4,128)S(1)}, u32[]{:S(2)}, u32[]{:S(2)}) %collective-permute-start.3) | collective-permute-done | bytes 2080 | tf_op jit(solution)/shard_map/ppermute | solution.py:366
  44.4 0.2 collective-permute-done.2.s1
  44.6 3.3 %down.1 = f32[16,4096]{1,0:T(8,128)} custom-call(s32[4]{0:T(128)S(1)} %pad_add_fusion.base, f32[4,128]{1,0:T(4,128)S(1)} %slice_reduce_fusion.s0, f32[4,128]{1,0:T(4,128)S(1)} %collective-permute-done.2.s1, f32[4,128]{1,0:T(4,128)S(1)} %collective-permute-done.3.s2, f32[4,128]{1,0:T(4,128)S(1)} %collective-permute-done.4.s3, f32[64,32]{1,0:T(8,128)S(1)} %gather.1.cfar, ...), custom_call_target="tpu_custom_call" | custom-call | tf_op jit(solution)/shard_map/down/pallas_call | solution.py:338
  (6 shorter events, 0.0 us)
Async XLA Ops:
  4.6 16.2 %collective-permute-start.1 = (f32[16,6144]{1,0:T(8,128)S(1)}, f32[16,6144]{1,0:T(8,128)S(1)}, u32[]{:S(2)}, u32[]{:S(2)}) collective-permute-start(f32[16,6144]{1,0:T(8,128)S(1)} %get-tuple-element.17.ext.xo.co), channel_id=1, source_target_pairs={{1,2},{2,1},{3,4},{4,3},{5,6},{6,5},{7,8},{8,7},{9,10},{10,9},{11,... | collective-permute-start | bytes 1179656 | tf_op jit(solution)/shard_map/ppermute | solution.py:358
  9.2 11.6 %collective-permute-start = (f32[16,6144]{1,0:T(8,128)S(1)}, f32[16,6144]{1,0:T(8,128)S(1)}, u32[]{:S(2)}, u32[]{:S(2)}) collective-permute-start(f32[16,6144]{1,0:T(8,128)S(1)} %get-tuple-element.17.ext.xo.co), channel_id=1, source_target_pairs={{0,1},{1,0},{2,3},{3,2},{4,5},{5,4},{6,7},{7,6},{8,9},{9,8},{10,11... | collective-permute-start | bytes 1179656 | tf_op jit(solution)/shard_map/ppermute | solution.py:355
  9.9 23.6 %all-to-all-start = ((f32[32,5,4,128]{3,2,1,0:T(4,128)}), f32[32,5,4,128]{3,2,1,0:T(4,128)S(1)}, u32[]{:S(2)}, u32[]{:S(2)}) async-start(f32[32,5,4,128]{3,2,1,0:T(4,128)} %lift.3), calls=%async_computation | async-start | bytes 655360 | tf_op jit(solution)/shard_map/all_to_all | solution.py:360
  20.9 20.7 %copy-start.2 = (f32[4,8,1024]{2,1,0:T(8,128)S(1)}, f32[4,8,1024]{2,1,0:T(8,128)}, u32[]{:S(2)}) copy-start(f32[4,8,1024]{2,1,0:T(8,128)} %param.21) | copy-start | bytes 393220
  20.9 20.7 %copy-start.3 = (s32[4,8]{1,0:T(4,128)S(1)}, s32[4,8]{1,0:T(4,128)}, u32[]{:S(2)}) copy-start(s32[4,8]{1,0:T(4,128)} %csrc.1) | copy-start | bytes 388
  37.9 4.9 %collective-permute-start.4 = (f32[4,128]{1,0:T(4,128)S(1)}, f32[4,128]{1,0:T(4,128)S(1)}, u32[]{:S(2)}, u32[]{:S(2)}) collective-permute-start(f32[4,128]{1,0:T(4,128)S(1)} %slice_reduce_fusion.s0), channel_id=1, source_target_pairs={{0,192},{64,0},{128,64},{192,128},{1,193},{65,1},{129,65},{193,129... | collective-permute-start | bytes 6152 | tf_op jit(solution)/shard_map/ppermute | solution.py:366
  40.4 3.9 %collective-permute-start.3 = (f32[4,128]{1,0:T(4,128)S(1)}, f32[4,128]{1,0:T(4,128)S(1)}, u32[]{:S(2)}, u32[]{:S(2)}) collective-permute-start(f32[4,128]{1,0:T(4,128)S(1)} %slice_reduce_fusion.s0), channel_id=1, source_target_pairs={{0,128},{64,192},{128,0},{192,64},{1,129},{65,193},{129,1},{193,65... | collective-permute-start | bytes 6152 | tf_op jit(solution)/shard_map/ppermute | solution.py:366
  40.9 3.6 %collective-permute-start.2 = (f32[4,128]{1,0:T(4,128)S(1)}, f32[4,128]{1,0:T(4,128)S(1)}, u32[]{:S(2)}, u32[]{:S(2)}) collective-permute-start(f32[4,128]{1,0:T(4,128)S(1)} %slice_reduce_fusion.s0), channel_id=1, source_target_pairs={{0,64},{64,128},{128,192},{192,0},{1,65},{65,129},{129,193},{193,1... | collective-permute-start | bytes 6152 | tf_op jit(solution)/shard_map/ppermute | solution.py:366
  41.6 3.0 %copy-start = (f32[64,2048]{1,0:T(8,128)S(1)}, f32[64,2048]{1,0:T(8,128)}, u32[]{:S(2)}) copy-start(f32[64,2048]{1,0:T(8,128)} %param.16) | copy-start | bytes 1572868
  41.6 3.0 %copy-start.1 = (f32[1,4,1024]{2,1,0:T(4,128)S(1)}, f32[1,4,1024]{2,1,0:T(4,128)}, u32[]{:S(2)}) copy-start(f32[1,4,1024]{2,1,0:T(4,128)} %param.23) | copy-start | bytes 49156

commit v8 on v6

--- a/solution.py
+++ b/solution.py
@@ -116,6 +116,15 @@
         out.append(jnp.concatenate([w*jnp.concatenate([m]*n,axis=1) for m in keep],axis=0))
     return out
 
+def pick(where,four):
+    return jnp.where(where<2,jnp.where(where<1,four[0],four[1]),jnp.where(where<3,four[2],four[3]))
+def join4(four):
+    block=iota((8,128),1)//K
+    return jnp.concatenate([pick(block,[pltpu.roll(c,(p-km)%4*K,1) if p!=km else c for p,c in enumerate(four)]) for km in range(4)],axis=0)
+def natural():
+    row=iota((128,128),0); col=iota((128,128),1)
+    return onehot(col==row//32*32+lax.rem(row,8)*4+lax.rem(row,32)//8)
+
 def mul3(v,w):
     d=wide(v,w)
     n=w[0].shape[0]
@@ -166,32 +175,34 @@
         scratch_shapes=[pltpu.VMEM(x.shape,f32),pltpu.VMEM(bas.shape,f32),pltpu.SemaphoreType.DMA((chunks+1,)),pltpu.SemaphoreType.DMA((2,))],
         compiler_params=pltpu.CompilerParams(vmem_limit_bytes=24<<20),name="up")(in_hbm(x),in_hbm(bas),in_hbm(tra),in_hbm(upper))
 
-def lift_kernel(ext,tra,upt,rep,fs):
+def lift_kernel(ext,tra,upt,rep,ejh,ejl,fs):
     nc=upt.shape[0]
     n=tra.shape[0]//8
     per=n//nc
     pts=n*LEAF
     outs=[]
     for u in range(nc):
-        e=jnp.concatenate([tra[pl.ds(((u*per+i)//8)*64+(u*per+i)%8,8,stride=8),:] for i in range(per)],axis=1)
-        v=[spread4(ext[:,pl.ds(pts+(u*per+i)//4*128,128)],i%4) for i in range(per)]
-        outs.append(mul3(jnp.concatenate(v,axis=1),masked4(e)))
-    row=iota((128,128),0); col=iota((128,128),1)
-    s3=onehot(col==row//32*32+lax.rem(row,8)*4+lax.rem(row,32)//8)
-    cc=exact(jnp.concatenate(outs,axis=1),s3)
+        es=[tra[pl.ds(((u*per+i)//8)*64+(u*per+i)%8,8,stride=8),:] for i in range(per)]
+        w=split(jnp.concatenate([join4(es[i:i+4]) for i in range(0,per,4)],axis=1))
+        ejh[pl.ds(u*K,K),:]=w[0]
+        ejl[pl.ds(u*K,K),:]=w[1]
+        outs.append(mul3(ext[:,pl.ds(pts+u*per*K,per*K)],w))
+    cc=exact(jnp.concatenate(outs,axis=1),natural())
     for q in range(8):
         fs[pl.ds(q*nc,nc),:]=upt[:,pl.ds(q*128,128)]
-    f=jnp.concatenate([fs[pl.ds(u,8,stride=nc),:] for u in range(nc)],axis=1)
-    pr=mul3(jnp.concatenate([spread4(cc,u) for u in range(nc)],axis=1),masked4(f))
+    pr=mul3(cc,split(join4([fs[pl.ds(u,8,stride=nc),:] for u in range(nc)])))
     pay=[cc[4*i:4*i+4] for i in range(4)]+[jnp.concatenate([pr[4*i:4*i+4] for i in range(4)],axis=1)]
     for c in range(rep.shape[0]):
         for i in range(5): rep[c,i]=pay[i]
 
 def lift(ext,tra,upper,copies):
+    vm=pl.BlockSpec(memory_space=pltpu.VMEM)
+    nc=upper.shape[0]
+    join=jax.ShapeDtypeStruct((nc*K,tra.shape[0]//8//nc*K),bf16)
     return pl.pallas_call(lift_kernel,
-        out_shape=jax.ShapeDtypeStruct((copies,5,4,128),f32),
-        in_specs=[pl.BlockSpec(memory_space=pltpu.VMEM)]*3,
-        scratch_shapes=[pltpu.VMEM((8*upper.shape[0],128),f32)],
+        out_shape=(jax.ShapeDtypeStruct((copies,5,4,128),f32),join,join),
+        in_specs=[vm]*3,out_specs=(vm,)*3,
+        scratch_shapes=[pltpu.VMEM((8*nc,128),f32)],
         compiler_params=pltpu.CompilerParams(vmem_limit_bytes=24<<20),name="lift")(ext,tra,upper)
 
 def far_kernel(base,src_h,cpl_h,cb,co,ca,out,table,cpl,src,sem,sem2):
@@ -213,18 +224,14 @@
     idx.wait()
     per=n//chunks
     first=base[0]
-    block=iota((8,128),1)//K
     block32=iota((2*RHS,128),1)//K
-    def pick(where,four):
-        return jnp.where(where<2,jnp.where(where<1,four[0],four[1]),jnp.where(where<3,four[2],four[3]))
     def step(c,_):
         chunk(c).wait()
         for i in range(per):
             t=c*per+i
             off=pl.multiple_of(t*64,64)
             cs=[cpl[pl.ds(off+j,8,stride=8),:] for j in range(8)]
-            w=[[pick(block,[pltpu.roll(cs[4*h+p],(p-km)%4*K,1) if p!=km else cs[4*h+p] for p in range(4)]) for h in range(2)] for km in range(4)]
-            w=jnp.concatenate([jnp.concatenate(v,axis=1) for v in w],axis=0)
+            w=jnp.concatenate([join4(cs[:4]),join4(cs[4:])],axis=1)
             at=[src[j,t]-first for j in range(8)]
             v=jnp.concatenate([pick(block32,[table[at[4*h+p]] for p in range(4)]) for h in range(2)],axis=1)
             d=dotnt(v,jnp.concatenate(split(w),axis=0))
@@ -248,14 +255,17 @@
 def gather_kernel(csrc,pays,ccp,out):
     nc=ccp.shape[0]//64
     devs=pays.shape[0]
+    block=iota((RHS,128),1)//K
     for u in range(nc):
-        w=jnp.concatenate([ccp[pl.ds(u*64+j,8,stride=8),:] for j in range(8)],axis=1)
+        cs=[ccp[pl.ds(u*64+j,8,stride=8),:] for j in range(8)]
         vs=[]
         for j in range(8):
             s=csrc[u,j]
             place=lax.rem(s//nc,2)*(devs//2)+s//(2*nc)
-            vs.append(spread4(jnp.concatenate([pays[place,i] for i in range(4)],axis=0),lax.rem(s,nc)))
-        out[pl.ds(u*RHS,RHS),:]=mul3(jnp.concatenate(vs,axis=1),masked4(w))
+            v=jnp.concatenate([pays[place,i] for i in range(4)],axis=0)
+            vs.append(pltpu.roll(v,lax.rem(nc+j%4-lax.rem(s,nc),nc)*K,1))
+        v=jnp.concatenate([pick(block,vs[:4]),pick(block,vs[4:])],axis=1)
+        out[pl.ds(u*RHS,RHS),:]=mul3(v,split(jnp.concatenate([join4(cs[:4]),join4(cs[4:])],axis=1)))
 
 def gather(csrc,pays,ccp):
     nc=ccp.shape[0]
@@ -267,26 +277,20 @@
         cost_estimate=pl.CostEstimate(flops=10**10,bytes_accessed=10**7,transcendentals=0),
         compiler_params=pltpu.CompilerParams(vmem_limit_bytes=24<<20),name="gather")(csrc,pays,view)
 
-def down_kernel(base,s0,s1,s2,s3,cfar,gcp,upt,tra,bas,lf,near_ref,out,gs,fs):
+def down_kernel(base,s0,s1,s2,s3,cfar,gcp,upt,ejh,ejl,bas,lf,near_ref,out,gs,fs):
     nc=upt.shape[0]; ng=gcp.shape[0]
     n=lf.shape[0]//RHS
-    row=iota((K,128),0); col=lax.rem(iota((K,128),1),K)
-    s4=onehot(col==lax.rem(row,8)*4+row//8)
     for q in range(8):
         fs[pl.ds(q*nc,nc),:]=upt[:,pl.ds(q*128,128)]
         gs[pl.ds(q*ng,ng),:]=gcp[:,pl.ds(q*128,128)]
-    gv=exact(jnp.concatenate([s[:,i*K:(i+1)*K] for s in (s0,s1,s2,s3) for i in range(4)],axis=0),s4)
-    gv=[gv[h*RHS:(h+1)*RHS] for h in range(ng)]
-    gw=jnp.concatenate([gs[pl.ds(lax.rem(base[1]+ng-h,ng),8,stride=ng),:] for h in range(ng)],axis=1)
-    gf=mul3(jnp.concatenate(gv,axis=1),masked4(gw))
-    fw=jnp.concatenate([fs[pl.ds(u,8,stride=nc),:] for u in range(nc)],axis=1)
-    wh,wl=masked4(fw)
+    gv=jnp.concatenate([jnp.concatenate([s[:,i*K:(i+1)*K] for i in range(4)],axis=0) for s in (s0,s1,s2,s3)],axis=1)
+    gw=join4([gs[pl.ds(lax.rem(base[1]+ng-h,ng),8,stride=ng),:] for h in range(ng)])
+    gf=mul3(exact(gv,natural()),split(gw))
+    wh,wl=split(join4([fs[pl.ds(u,8,stride=nc),:] for u in range(nc)]))
     gh,gl=split(gf)
-    down=dotnn(gh,wh)+dotnn(gl,wh)+dotnn(gh,wl)
-    row=lax.rem(iota((128,K),0),K); col=iota((128,K),1)
-    s5=onehot(row==lax.rem(col,8)*4+col//8)
-    down=jnp.concatenate([down[:,u*128:(u+1)*128] for u in range(nc)],axis=0)
-    down=exact(down,s5)
+    down=dotnn(jnp.concatenate([gh,gl,gh],axis=1),jnp.concatenate([wh,wh,wl],axis=0))
+    row=iota((128,128),0); col=iota((128,128),1)
+    down=exact(down,onehot(col==row//32*32+lax.rem(row,4)*8+lax.rem(row,32)//4))
     row=lax.rem(iota((128,256),0),K); col=iota((128,256),1)
     p1=onehot(row==2*(lax.rem(col,128)//8)+col//128)
     row=lax.rem(iota((2*K,256),0),K); col=iota((2*K,256),1)
@@ -296,13 +300,13 @@
     left=iota((RHS,128),1)<LEAF
     per=n//nc
     ds=[]
+    block=iota((RHS,128),1)//K
     for u in range(nc):
-        cf=cfar[pl.ds(u*RHS,RHS),:]+down[u*RHS:(u+1)*RHS]
-        e=jnp.concatenate([tra[pl.ds(((u*per+i)//8)*64+(u*per+i)%8,8,stride=8),:] for i in range(per)],axis=1)
-        eh,el=masked4(e)
+        cf=cfar[pl.ds(u*RHS,RHS),:]+down[:,u*K:(u+1)*K]
         ch,cl=split(cf)
-        d=dotnn(jnp.concatenate([ch,cl,ch],axis=1),jnp.concatenate([eh,eh,el],axis=0))
-        ds+=[d[:,i*128:(i+1)*128] for i in range(per)]
+        eh=ejh[pl.ds(u*K,K),:]
+        d=dotnn(jnp.concatenate([ch,cl,ch],axis=1),jnp.concatenate([eh,eh,ejl[pl.ds(u*K,K),:]],axis=0))
+        ds+=[jnp.where(block==i%4,d[:,i//4*128:i//4*128+128],0.0) for i in range(per)]
     q=dotnn(jnp.concatenate([*split(jnp.concatenate(ds,axis=0)),*split(lf[...])],axis=1),p12)
     same=(iota((256,128),0)//32==lax.rem(iota((256,128),1),8))
     for g in range(n//8):
@@ -319,15 +323,15 @@
             at=pl.ds(g*512+m*128,128)
             out[:,at]=near_ref[:,at]+r
 
-def down(base,sums,cfar,gcp,upper,tra,basis,lf,nearv):
+def down(base,sums,cfar,gcp,upper,ejh,ejl,basis,lf,nearv):
     n=basis.shape[0]; nc=upper.shape[0]; ng=gcp.shape[0]
     bas=basis.reshape(n//8,8,16,128).transpose(0,2,1,3).reshape(n*16,128)
     vm=pl.BlockSpec(memory_space=pltpu.VMEM)
     return pl.pallas_call(down_kernel,
         out_shape=jax.ShapeDtypeStruct((RHS,n*LEAF),f32),
-        in_specs=[pl.BlockSpec(memory_space=pltpu.SMEM)]+[vm]*11,
+        in_specs=[pl.BlockSpec(memory_space=pltpu.SMEM)]+[vm]*12,
         scratch_shapes=[pltpu.VMEM((8*ng,128),f32),pltpu.VMEM((8*nc,128),f32)],
-        compiler_params=pltpu.CompilerParams(vmem_limit_bytes=24<<20),name="down")(base,*sums,cfar,gcp,upper,tra,bas,lf,nearv)
+        compiler_params=pltpu.CompilerParams(vmem_limit_bytes=24<<20),name="down")(base,*sums,cfar,gcp,upper,ejh,ejl,bas,lf,nearv)
 
 def across(devs):
     return [[2*i+c for i in range(devs//2)] for c in range(2)]
@@ -342,7 +346,7 @@
     ext,tra,upper=up(right_sides,basis,leaf_transfer,cluster_transfer)
     eb=lax.ppermute(ext,both,[(i,i^1) for i in range(every)])
     ea=lax.ppermute(ext,both,[p for i in range(1,every-1,2) for p in ((i,i+1),(i+1,i))])
-    rep=lift(ext,tra,upper,devs//2)
+    rep,ejh,ejl=lift(ext,tra,upper,devs//2)
     some=lax.all_to_all(rep,"leaf",0,0,tiled=True,axis_index_groups=across(devs))
     nearv=near(base,near_source,near_count,eb,ext,ea,near_blocks)
     lf=far(base,leaf_source,eb,ext,ea,leaf_coupling)
@@ -351,7 +355,7 @@
     total=pays[:,4].sum(axis=0)
     sums=[total]+[lax.ppermute(total,"group",[(i,(i+k)%ng) for i in range(ng)]) for k in range(1,ng)]
     cfar=gather(cluster_source,pays,cluster_coupling)
-    return down(base,sums,cfar,group_coupling.reshape(-1,1024),upper,tra,basis,lf,nearv)
+    return down(base,sums,cfar,group_coupling.reshape(-1,1024),upper,ejh,ejl,basis,lf,nearv)
 
 def solution(mesh):
     both=("group","leaf")

time: 46.8 us -> 46.4 us (level)
  no operation moved by 1% of the time
where the time goes in v8:
time: 46.4 us; the launch traced here: 46.2 us
  starting transfers between devices  20.5 us (44%)
  Pallas kernels  18.9 us (41%)
  blocking collectives  3.48 us (8%)
  waiting for transfers between devices  3.05 us (7%)
    all_to_all x1, starting transfers between devices, per_device(): lax.all_to_all(rep, 'leaf', 0, 0, tiled=True, axis_index_groups=across(de...  10.4 us
    pallas_call x1, Pallas kernels, near(): pl.pallas_call(near_kernel, out_shape=jax.ShapeDtypeStruct((RHS, leaves *...  6.57 us
    ppermute x3, starting transfers between devices, per_device(): lax.ppermute(total, 'group', [(i, (i + k) % ng) for i in range(ng)])  4.91 us
    pallas_call x1, Pallas kernels, far(): pl.pallas_call(far_kernel, out_shape=jax.ShapeDtypeStruct((n * RHS, 2 * K...  4.21 us
    all_gather x1, blocking collectives, per_device(): lax.all_gather(some, 'leaf', axis=0, tiled=True, axis_index_groups=[[2 *...  3.48 us
    pallas_call x1, Pallas kernels, down(): pl.pallas_call(down_kernel, out_shape=jax.ShapeDtypeStruct((RHS, n * LEAF...  3.35 us
    ppermute x1, starting transfers between devices, per_device(): eb = lax.ppermute(ext, both, [(i, i ^ 1) for i in range(every)])  3.33 us
    all_to_all x1, waiting for transfers between devices, per_device(): lax.all_to_all(rep, 'leaf', 0, 0, tiled=True, axis_index_groups=across(de...  2.54 us
  transfers between devices with their start and end apart: 6, of which 2 were waited for; matrix products, arithmetic and copies ran while one was open for 0% of the time, Pallas kernels for 30%

profile of v8, /device:TPU:1, one launch (start us, length us, event | category | flops | bytes accessed | tf_op | source)
XLA Modules:
  0.0 46.2 jit_solution(17126223705083635190)
XLA Ops:
  0.0 1.9 %up.1 = (f32[16,6144]{1,0:T(8,128)S(1)}, f32[512,128]{1,0:T(8,128)S(1)}, f32[4,1024]{1,0:T(4,128)S(1)}) custom-call(f32[16,4096]{1,0:T(8,128)} %x_h.1, f32[1024,128]{1,0:T(8,128)} %bitcast.31, f32[512,128]{1,0:T(8,128)} %bitcast.36, f32[4,1024]{1,0:T(4,128)} %upt_h.1), custom_call_target="tpu_custom_call" | custom-call | tf_op jit(solution)/shard_map/up/pallas_call | solution.py:172
  1.9 3.3 %collective-permute-start = (f32[16,6144]{1,0:T(8,128)S(1)}, f32[16,6144]{1,0:T(8,128)S(1)}, u32[]{:S(2)}, u32[]{:S(2)}) collective-permute-start(f32[16,6144]{1,0:T(8,128)S(1)} %get-tuple-element.14.ext.xo.co), channel_id=1, source_target_pairs={{0,1},{1,0},{2,3},{3,2},{4,5},{5,4},{6,7},{7,6},{8,9},{9,8},{10,11... | collective-permute-start | bytes 1179656 | tf_op jit(solution)/shard_map/ppermute | solution.py:347
  5.2 1.9 %collective-permute-start.1 = (f32[16,6144]{1,0:T(8,128)S(1)}, f32[16,6144]{1,0:T(8,128)S(1)}, u32[]{:S(2)}, u32[]{:S(2)}) collective-permute-start(f32[16,6144]{1,0:T(8,128)S(1)} %get-tuple-element.14.ext.xo.co), channel_id=1, source_target_pairs={{1,2},{2,1},{3,4},{4,3},{5,6},{6,5},{7,8},{8,7},{9,10},{10,9},{11,... | collective-permute-start | bytes 1179656 | tf_op jit(solution)/shard_map/ppermute | solution.py:348
  7.2 1.7 %lift.1 = (f32[32,5,4,128]{3,2,1,0:T(4,128)}, bf16[128,512]{1,0:T(8,128)(2,1)S(1)}, bf16[128,512]{1,0:T(8,128)(2,1)S(1)}) custom-call(f32[16,6144]{1,0:T(8,128)S(1)} %get-tuple-element.14.ext.xo.co, f32[512,128]{1,0:T(8,128)S(1)} %get-tuple-element.15.tra, f32[4,1024]{1,0:T(4,128)S(1)} %get-tuple-element.16.upt), custom_call_target="tpu_custom_call" | custom-call | tf_op jit(solution)/shard_map/lift/pallas_call | solution.py:202
  8.8 10.4 %all-to-all-start = ((f32[32,5,4,128]{3,2,1,0:T(4,128)}), f32[32,5,4,128]{3,2,1,0:T(4,128)S(1)}, u32[]{:S(2)}, u32[]{:S(2)}) async-start(f32[32,5,4,128]{3,2,1,0:T(4,128)} %get-tuple-element.17), calls=%async_computation | async-start | bytes 655360 | tf_op jit(solution)/shard_map/all_to_all | solution.py:350
  19.2 0.1 pad_add_fusion.base
  19.3 0.0 collective-permute-done.xb.cb
  19.3 0.0 collective-permute-done.1.xa.ca
  19.3 0.0 copy-start.3
  19.3 6.6 %near.1.near_ref = f32[16,4096]{1,0:T(8,128)S(1)} custom-call(s32[3]{0:T(128)S(1)} %pad_add_fusion.base, s32[8,64]{1,0:T(8,128)} %bitcast.39, s32[64]{0:T(128)} %cnt_h.1, f32[16384,128]{1,0:T(8,128)} %bitcast.38, f32[16,6144]{1,0:T(8,128)S(1)} %collective-permute-done.xb.cb, f32[16,6144]{1,0:T(8,128)S(1)} %get-tuple-element.14.ext.xo.co, ...), custom_call_target="tpu_custom_call" | custom-call | flops 99999997952 | bytes 10000000 | tf_op jit(solution)/shard_map/near/pallas_call | solution.py:85
  25.9 4.2 %far.1.lf = f32[1024,64]{1,0:T(8,128)S(1)} custom-call(s32[3]{0:T(128)S(1)} %pad_add_fusion.base, s32[8,64]{1,0:T(8,128)} %bitcast.37, f32[4096,128]{1,0:T(8,128)} %bitcast.35, f32[16,6144]{1,0:T(8,128)S(1)} %collective-permute-done.xb.cb, f32[16,6144]{1,0:T(8,128)S(1)} %get-tuple-element.14.ext.xo.co, f32[16,6144]{1,0:T(8,128)S(1)} %collective-permute-done.1.xa.ca), custom_call_target="tpu_custom_call" | custom-call | tf_op jit(solution)/shard_map/far/pallas_call | solution.py:247
  30.1 2.5 %all-to-all-done = f32[32,5,4,128]{3,2,1,0:T(4,128)S(1)} async-done(((f32[32,5,4,128]{3,2,1,0:T(4,128)}), f32[32,5,4,128]{3,2,1,0:T(4,128)S(1)}, u32[]{:S(2)}, u32[]{:S(2)}) %all-to-all-start) | async-done | bytes 327712 | tf_op jit(solution)/shard_map/all_to_all | solution.py:350
  32.7 3.5 %all_gather.3.pays = f32[64,5,4,128]{3,2,1,0:T(4,128)S(1)} all-gather(f32[32,5,4,128]{3,2,1,0:T(4,128)S(1)} %all-to-all-done), channel_id=1, replica_groups={{0,1},{2,3},{4,5},{6,7},{8,9},{10,11},{12,13},{14,15},{16,17},{18,19},{..., dimensions={0}, use_global_device_ids=true | all-gather | bytes 983040 | tf_op jit(solution)/shard_map/all_gather | solution.py:354
  36.1 0.1 slice_reduce_fusion.s0
  36.2 1.3 %collective-permute-start.2 = (f32[4,128]{1,0:T(4,128)S(1)}, f32[4,128]{1,0:T(4,128)S(1)}, u32[]{:S(2)}, u32[]{:S(2)}) collective-permute-start(f32[4,128]{1,0:T(4,128)S(1)} %slice_reduce_fusion.s0), channel_id=1, source_target_pairs={{0,64},{64,128},{128,192},{192,0},{1,65},{65,129},{129,193},{193,1... | collective-permute-start | bytes 6152 | tf_op jit(solution)/shard_map/ppermute | solution.py:356
  37.5 2.6 %collective-permute-start.3 = (f32[4,128]{1,0:T(4,128)S(1)}, f32[4,128]{1,0:T(4,128)S(1)}, u32[]{:S(2)}, u32[]{:S(2)}) collective-permute-start(f32[4,128]{1,0:T(4,128)S(1)} %slice_reduce_fusion.s0), channel_id=1, source_target_pairs={{0,128},{64,192},{128,0},{192,64},{1,129},{65,193},{129,1},{193,65... | collective-permute-start | bytes 6152 | tf_op jit(solution)/shard_map/ppermute | solution.py:356
  40.1 1.0 %collective-permute-start.4 = (f32[4,128]{1,0:T(4,128)S(1)}, f32[4,128]{1,0:T(4,128)S(1)}, u32[]{:S(2)}, u32[]{:S(2)}) collective-permute-start(f32[4,128]{1,0:T(4,128)S(1)} %slice_reduce_fusion.s0), channel_id=1, source_target_pairs={{0,192},{64,0},{128,64},{192,128},{1,193},{65,1},{129,65},{193,129... | collective-permute-start | bytes 6152 | tf_op jit(solution)/shard_map/ppermute | solution.py:356
  41.1 0.0 copy-done.2
  41.1 0.0 copy-done.3
  41.1 1.2 %gather.1.cfar = f32[64,32]{1,0:T(8,128)S(1)} custom-call(s32[4,8]{1,0:T(4,128)S(1)} %copy-done.3, f32[64,5,4,128]{3,2,1,0:T(4,128)S(1)} %all_gather.3.pays, f32[256,128]{1,0:T(8,128)S(1)} %bitcast.34), custom_call_target="tpu_custom_call" | custom-call | flops 10000000000 | bytes 10000000 | tf_op jit(solution)/shard_map/gather/pallas_call | solution.py:274
  42.3 0.0 collective-permute-done.2.s1
  42.3 0.0 collective-permute-done.3.s2
  42.4 0.5 %collective-permute-done.4.s3 = f32[4,128]{1,0:T(4,128)S(1)} collective-permute-done((f32[4,128]{1,0:T(4,128)S(1)}, f32[4,128]{1,0:T(4,128)S(1)}, u32[]{:S(2)}, u32[]{:S(2)}) %collective-permute-start.4) | collective-permute-done | bytes 2080 | tf_op jit(solution)/shard_map/ppermute | solution.py:356
  42.9 3.4 %down.1 = f32[16,4096]{1,0:T(8,128)} custom-call(s32[3]{0:T(128)S(1)} %pad_add_fusion.base, f32[4,128]{1,0:T(4,128)S(1)} %slice_reduce_fusion.s0, f32[4,128]{1,0:T(4,128)S(1)} %collective-permute-done.2.s1, f32[4,128]{1,0:T(4,128)S(1)} %collective-permute-done.3.s2, f32[4,128]{1,0:T(4,128)S(1)} %collective-permute-done.4.s3, f32[64,32]{1,0:T(8,128)S(1)} %gather.1.cfar, ...), custom_call_target="tpu_custom_call" | custom-call | tf_op jit(solution)/shard_map/down/pallas_call | solution.py:330
  (5 shorter events, 0.0 us)
Async XLA Ops:
  1.9 17.4 %collective-permute-start = (f32[16,6144]{1,0:T(8,128)S(1)}, f32[16,6144]{1,0:T(8,128)S(1)}, u32[]{:S(2)}, u32[]{:S(2)}) collective-permute-start(f32[16,6144]{1,0:T(8,128)S(1)} %get-tuple-element.14.ext.xo.co), channel_id=1, source_target_pairs={{0,1},{1,0},{2,3},{3,2},{4,5},{5,4},{6,7},{7,6},{8,9},{9,8},{10,11... | collective-permute-start | bytes 1179656 | tf_op jit(solution)/shard_map/ppermute | solution.py:347
  5.2 14.1 %collective-permute-start.1 = (f32[16,6144]{1,0:T(8,128)S(1)}, f32[16,6144]{1,0:T(8,128)S(1)}, u32[]{:S(2)}, u32[]{:S(2)}) collective-permute-start(f32[16,6144]{1,0:T(8,128)S(1)} %get-tuple-element.14.ext.xo.co), channel_id=1, source_target_pairs={{1,2},{2,1},{3,4},{4,3},{5,6},{6,5},{7,8},{8,7},{9,10},{10,9},{11,... | collective-permute-start | bytes 1179656 | tf_op jit(solution)/shard_map/ppermute | solution.py:348
  8.8 23.8 %all-to-all-start = ((f32[32,5,4,128]{3,2,1,0:T(4,128)}), f32[32,5,4,128]{3,2,1,0:T(4,128)S(1)}, u32[]{:S(2)}, u32[]{:S(2)}) async-start(f32[32,5,4,128]{3,2,1,0:T(4,128)} %get-tuple-element.17), calls=%async_computation | async-start | bytes 655360 | tf_op jit(solution)/shard_map/all_to_all | solution.py:350
  19.3 21.8 %copy-start.2 = (f32[4,8,1024]{2,1,0:T(8,128)S(1)}, f32[4,8,1024]{2,1,0:T(8,128)}, u32[]{:S(2)}) copy-start(f32[4,8,1024]{2,1,0:T(8,128)} %param.21) | copy-start | bytes 393220
  19.3 21.8 %copy-start.3 = (s32[4,8]{1,0:T(4,128)S(1)}, s32[4,8]{1,0:T(4,128)}, u32[]{:S(2)}) copy-start(s32[4,8]{1,0:T(4,128)} %csrc.1) | copy-start | bytes 388
  36.2 6.1 %collective-permute-start.2 = (f32[4,128]{1,0:T(4,128)S(1)}, f32[4,128]{1,0:T(4,128)S(1)}, u32[]{:S(2)}, u32[]{:S(2)}) collective-permute-start(f32[4,128]{1,0:T(4,128)S(1)} %slice_reduce_fusion.s0), channel_id=1, source_target_pairs={{0,64},{64,128},{128,192},{192,0},{1,65},{65,129},{129,193},{193,1... | collective-permute-start | bytes 6152 | tf_op jit(solution)/shard_map/ppermute | solution.py:356
  37.5 4.8 %collective-permute-start.3 = (f32[4,128]{1,0:T(4,128)S(1)}, f32[4,128]{1,0:T(4,128)S(1)}, u32[]{:S(2)}, u32[]{:S(2)}) collective-permute-start(f32[4,128]{1,0:T(4,128)S(1)} %slice_reduce_fusion.s0), channel_id=1, source_target_pairs={{0,128},{64,192},{128,0},{192,64},{1,129},{65,193},{129,1},{193,65... | collective-permute-start | bytes 6152 | tf_op jit(solution)/shard_map/ppermute | solution.py:356
  40.1 2.7 %collective-permute-start.4 = (f32[4,128]{1,0:T(4,128)S(1)}, f32[4,128]{1,0:T(4,128)S(1)}, u32[]{:S(2)}, u32[]{:S(2)}) collective-permute-start(f32[4,128]{1,0:T(4,128)S(1)} %slice_reduce_fusion.s0), channel_id=1, source_target_pairs={{0,192},{64,0},{128,64},{192,128},{1,193},{65,1},{129,65},{193,129... | collective-permute-start | bytes 6152 | tf_op jit(solution)/shard_map/ppermute | solution.py:356
  41.1 1.7 %copy-start = (f32[64,2048]{1,0:T(8,128)S(1)}, f32[64,2048]{1,0:T(8,128)}, u32[]{:S(2)}) copy-start(f32[64,2048]{1,0:T(8,128)} %param.16) | copy-start | bytes 1572868
  41.1 1.7 %copy-start.1 = (f32[1,4,1024]{2,1,0:T(4,128)S(1)}, f32[1,4,1024]{2,1,0:T(4,128)}, u32[]{:S(2)}) copy-start(f32[1,4,1024]{2,1,0:T(4,128)} %param.23) | copy-start | bytes 49156

commit v9 on v8

--- a/solution.py
+++ b/solution.py
@@ -252,30 +252,31 @@
             pltpu.SemaphoreType.DMA((chunks,)),pltpu.SemaphoreType.DMA((1,))],
         compiler_params=pltpu.CompilerParams(vmem_limit_bytes=24<<20),name="far")(base,in_hbm(src.T),in_hbm(view),eb,eo,ea)
 
-def gather_kernel(csrc,pays,ccp,out):
+def gather_kernel(base,csrc,own,other,ccp,out):
     nc=ccp.shape[0]//64
-    devs=pays.shape[0]
+    mine=1-base[2]//2
     block=iota((RHS,128),1)//K
     for u in range(nc):
         cs=[ccp[pl.ds(u*64+j,8,stride=8),:] for j in range(8)]
         vs=[]
         for j in range(8):
             s=csrc[u,j]
-            place=lax.rem(s//nc,2)*(devs//2)+s//(2*nc)
-            v=jnp.concatenate([pays[place,i] for i in range(4)],axis=0)
+            here=lax.rem(s//nc,2)==mine
+            place=s//(2*nc)
+            v=jnp.concatenate([jnp.where(here,own[place,i],other[place,i]) for i in range(4)],axis=0)
             vs.append(pltpu.roll(v,lax.rem(nc+j%4-lax.rem(s,nc),nc)*K,1))
         v=jnp.concatenate([pick(block,vs[:4]),pick(block,vs[4:])],axis=1)
         out[pl.ds(u*RHS,RHS),:]=mul3(v,split(jnp.concatenate([join4(cs[:4]),join4(cs[4:])],axis=1)))
 
-def gather(csrc,pays,ccp):
+def gather(base,csrc,own,other,ccp):
     nc=ccp.shape[0]
     view=ccp.reshape(nc,8,8,128).transpose(0,2,1,3).reshape(nc*64,128)
     vm=pl.BlockSpec(memory_space=pltpu.VMEM)
     return pl.pallas_call(gather_kernel,
         out_shape=jax.ShapeDtypeStruct((nc*RHS,K),f32),
-        in_specs=[pl.BlockSpec(memory_space=pltpu.SMEM),vm,vm],
+        in_specs=[pl.BlockSpec(memory_space=pltpu.SMEM)]*2+[vm]*3,
         cost_estimate=pl.CostEstimate(flops=10**10,bytes_accessed=10**7,transcendentals=0),
-        compiler_params=pltpu.CompilerParams(vmem_limit_bytes=24<<20),name="gather")(csrc,pays,view)
+        compiler_params=pltpu.CompilerParams(vmem_limit_bytes=24<<20),name="gather")(base,csrc,own,other,view)
 
 def down_kernel(base,s0,s1,s2,s3,cfar,gcp,upt,ejh,ejl,bas,lf,near_ref,out,gs,fs):
     nc=upt.shape[0]; ng=gcp.shape[0]
@@ -284,7 +285,7 @@
         fs[pl.ds(q*nc,nc),:]=upt[:,pl.ds(q*128,128)]
         gs[pl.ds(q*ng,ng),:]=gcp[:,pl.ds(q*128,128)]
     gv=jnp.concatenate([jnp.concatenate([s[:,i*K:(i+1)*K] for i in range(4)],axis=0) for s in (s0,s1,s2,s3)],axis=1)
-    gw=join4([gs[pl.ds(lax.rem(base[1]+ng-h,ng),8,stride=ng),:] for h in range(ng)])
+    gw=join4([gs[pl.ds(jnp.bitwise_xor(base[1],h),8,stride=ng),:] for h in range(ng)])
     gf=mul3(exact(gv,natural()),split(gw))
     wh,wl=split(join4([fs[pl.ds(u,8,stride=nc),:] for u in range(nc)]))
     gh,gl=split(gf)
@@ -351,10 +352,10 @@
     nearv=near(base,near_source,near_count,eb,ext,ea,near_blocks)
     lf=far(base,leaf_source,eb,ext,ea,leaf_coupling)
     some,nearv,lf=lax.optimization_barrier((some,nearv,lf))
-    pays=lax.all_gather(some,"leaf",axis=0,tiled=True,axis_index_groups=[[2*i,2*i+1] for i in range(devs//2)])
-    total=pays[:,4].sum(axis=0)
-    sums=[total]+[lax.ppermute(total,"group",[(i,(i+k)%ng) for i in range(ng)]) for k in range(1,ng)]
-    cfar=gather(cluster_source,pays,cluster_coupling)
+    other=lax.ppermute(some,"leaf",[(i,i^1) for i in range(devs)])
+    total=some[:,4].sum(axis=0)+other[:,4].sum(axis=0)
+    sums=[total]+[lax.ppermute(total,"group",[(i,i^k) for i in range(ng)]) for k in range(1,ng)]
+    cfar=gather(base,cluster_source,some,other,cluster_coupling)
     return down(base,sums,cfar,group_coupling.reshape(-1,1024),upper,ejh,ejl,basis,lf,nearv)
 
 def solution(mesh):

time: 46.4 us -> 46.7 us (level)
  blocking collectives: 3.48 us -> 0 us
  waiting for transfers between devices: 3.05 us -> 6.16 us
  starting transfers between devices: 20.5 us -> 21.1 us
    all_gather x1 -> x0, blocking collectives: 3.48 us -> none  [per_device(): lax.all_gather(some, 'leaf', axis=0, tiled=True, axis_index_groups=[[2 *...]
    ppermute x3 -> x4, waiting for transfers between devices: 0.5 us -> 3.61 us  [the longest x3 2.39 us: per_device(): lax.ppermute(total, 'group', [(i, i ^ k) for i in range(ng)])]
    ppermute x3 -> x4, starting transfers between devices: 4.91 us -> 5.53 us  [the longest x3 3.94 us: per_device(): lax.ppermute(total, 'group', [(i, i ^ k) for i in range(ng)])]
  transfers between devices with their start and end apart: 6 -> 7, of which waited for: 2 -> 4; matrix products, arithmetic and copies ran while one was open for 0% -> 0% of each run, Pallas kernels for 30% -> 29%
where the time goes in v9:
time: 46.7 us; the launch traced here: 46.5 us
  starting transfers between devices  21.1 us (45%)
  Pallas kernels  18.9 us (40%)
  waiting for transfers between devices  6.16 us (13%)
    all_to_all x1, starting transfers between devices, per_device(): lax.all_to_all(rep, 'leaf', 0, 0, tiled=True, axis_index_groups=across(de...  10.4 us
    pallas_call x1, Pallas kernels, near(): pl.pallas_call(near_kernel, out_shape=jax.ShapeDtypeStruct((RHS, leaves *...  6.57 us
    pallas_call x1, Pallas kernels, far(): pl.pallas_call(far_kernel, out_shape=jax.ShapeDtypeStruct((n * RHS, 2 * K...  4.21 us
    ppermute x3, starting transfers between devices, per_device(): lax.ppermute(total, 'group', [(i, i ^ k) for i in range(ng)])  3.94 us
    pallas_call x1, Pallas kernels, down(): pl.pallas_call(down_kernel, out_shape=jax.ShapeDtypeStruct((RHS, n * LEAF...  3.35 us
    ppermute x1, starting transfers between devices, per_device(): eb = lax.ppermute(ext, both, [(i, i ^ 1) for i in range(every)])  3.33 us
    all_to_all x1, waiting for transfers between devices, per_device(): lax.all_to_all(rep, 'leaf', 0, 0, tiled=True, axis_index_groups=across(de...  2.54 us
    ppermute x3, waiting for transfers between devices, per_device(): lax.ppermute(total, 'group', [(i, i ^ k) for i in range(ng)])  2.39 us
  transfers between devices with their start and end apart: 7, of which 4 were waited for; matrix products, arithmetic and copies ran while one was open for 0% of the time, Pallas kernels for 29%

profile of v9, /device:TPU:1, one launch (start us, length us, event | category | flops | bytes accessed | tf_op | source)
XLA Modules:
  0.0 46.5 jit_solution(2826218452281027987)
XLA Ops:
  0.0 1.9 %up.1 = (f32[16,6144]{1,0:T(8,128)S(1)}, f32[512,128]{1,0:T(8,128)S(1)}, f32[4,1024]{1,0:T(4,128)S(1)}) custom-call(f32[16,4096]{1,0:T(8,128)} %x_h.1, f32[1024,128]{1,0:T(8,128)} %bitcast.31, f32[512,128]{1,0:T(8,128)} %bitcast.36, f32[4,1024]{1,0:T(4,128)} %upt_h.1), custom_call_target="tpu_custom_call" | custom-call | tf_op jit(solution)/shard_map/up/pallas_call | solution.py:172
  1.9 3.3 %collective-permute-start = (f32[16,6144]{1,0:T(8,128)S(1)}, f32[16,6144]{1,0:T(8,128)S(1)}, u32[]{:S(2)}, u32[]{:S(2)}) collective-permute-start(f32[16,6144]{1,0:T(8,128)S(1)} %get-tuple-element.14.ext.xo.co), channel_id=1, source_target_pairs={{0,1},{1,0},{2,3},{3,2},{4,5},{5,4},{6,7},{7,6},{8,9},{9,8},{10,11... | collective-permute-start | bytes 1179656 | tf_op jit(solution)/shard_map/ppermute | solution.py:348
  5.2 1.9 %collective-permute-start.1 = (f32[16,6144]{1,0:T(8,128)S(1)}, f32[16,6144]{1,0:T(8,128)S(1)}, u32[]{:S(2)}, u32[]{:S(2)}) collective-permute-start(f32[16,6144]{1,0:T(8,128)S(1)} %get-tuple-element.14.ext.xo.co), channel_id=1, source_target_pairs={{1,2},{2,1},{3,4},{4,3},{5,6},{6,5},{7,8},{8,7},{9,10},{10,9},{11,... | collective-permute-start | bytes 1179656 | tf_op jit(solution)/shard_map/ppermute | solution.py:349
  7.2 1.7 %lift.1 = (f32[32,5,4,128]{3,2,1,0:T(4,128)}, bf16[128,512]{1,0:T(8,128)(2,1)S(1)}, bf16[128,512]{1,0:T(8,128)(2,1)S(1)}) custom-call(f32[16,6144]{1,0:T(8,128)S(1)} %get-tuple-element.14.ext.xo.co, f32[512,128]{1,0:T(8,128)S(1)} %get-tuple-element.15.tra, f32[4,1024]{1,0:T(4,128)S(1)} %get-tuple-element.16.upt), custom_call_target="tpu_custom_call" | custom-call | tf_op jit(solution)/shard_map/lift/pallas_call | solution.py:202
  8.8 10.4 %all-to-all-start = ((f32[32,5,4,128]{3,2,1,0:T(4,128)}), f32[32,5,4,128]{3,2,1,0:T(4,128)S(1)}, u32[]{:S(2)}, u32[]{:S(2)}) async-start(f32[32,5,4,128]{3,2,1,0:T(4,128)} %get-tuple-element.17), calls=%async_computation | async-start | bytes 655360 | tf_op jit(solution)/shard_map/all_to_all | solution.py:351
  19.2 0.1 pad_add_fusion.base
  19.3 0.0 collective-permute-done.xb.cb
  19.3 0.0 collective-permute-done.1.xa.ca
  19.3 0.0 copy-start.3
  19.3 6.6 %near.1.near_ref = f32[16,4096]{1,0:T(8,128)S(1)} custom-call(s32[3]{0:T(128)S(1)} %pad_add_fusion.base, s32[8,64]{1,0:T(8,128)} %bitcast.39, s32[64]{0:T(128)} %cnt_h.1, f32[16384,128]{1,0:T(8,128)} %bitcast.38, f32[16,6144]{1,0:T(8,128)S(1)} %collective-permute-done.xb.cb, f32[16,6144]{1,0:T(8,128)S(1)} %get-tuple-element.14.ext.xo.co, ...), custom_call_target="tpu_custom_call" | custom-call | flops 99999997952 | bytes 10000000 | tf_op jit(solution)/shard_map/near/pallas_call | solution.py:85
  25.9 4.2 %far.1.lf = f32[1024,64]{1,0:T(8,128)S(1)} custom-call(s32[3]{0:T(128)S(1)} %pad_add_fusion.base, s32[8,64]{1,0:T(8,128)} %bitcast.37, f32[4096,128]{1,0:T(8,128)} %bitcast.35, f32[16,6144]{1,0:T(8,128)S(1)} %collective-permute-done.xb.cb, f32[16,6144]{1,0:T(8,128)S(1)} %get-tuple-element.14.ext.xo.co, f32[16,6144]{1,0:T(8,128)S(1)} %collective-permute-done.1.xa.ca), custom_call_target="tpu_custom_call" | custom-call | tf_op jit(solution)/shard_map/far/pallas_call | solution.py:247
  30.1 2.5 %all-to-all-done.own = f32[32,5,4,128]{3,2,1,0:T(4,128)S(1)} async-done(((f32[32,5,4,128]{3,2,1,0:T(4,128)}), f32[32,5,4,128]{3,2,1,0:T(4,128)S(1)}, u32[]{:S(2)}, u32[]{:S(2)}) %all-to-all-start) | async-done | bytes 327712 | tf_op jit(solution)/shard_map/all_to_all | solution.py:351
  32.6 1.6 %collective-permute-start.2 = (f32[32,5,4,128]{3,2,1,0:T(4,128)S(1)}, f32[32,5,4,128]{3,2,1,0:T(4,128)S(1)}, u32[]{:S(2)}, u32[]{:S(2)}) collective-permute-start(f32[32,5,4,128]{3,2,1,0:T(4,128)S(1)} %all-to-all-done.own), channel_id=1, source_target_pairs={{0,1},{1,0},{2,3},{3,2},{4,5},{5,4},{6,7},{7,6},{8,9},{9,8},{10,11... | collective-permute-start | bytes 983048 | tf_op jit(solution)/shard_map/ppermute | solution.py:355
  34.3 1.2 %collective-permute-done.2.other = f32[32,5,4,128]{3,2,1,0:T(4,128)S(1)} collective-permute-done((f32[32,5,4,128]{3,2,1,0:T(4,128)S(1)}, f32[32,5,4,128]{3,2,1,0:T(4,128)S(1)}, u32[]{:S(2)}, u32[]{:S(2)}) %collective-permute-start.2) | collective-permute-done | bytes 327712 | tf_op jit(solution)/shard_map/ppermute | solution.py:355
  35.5 1.3 %collective-permute-start.3 = (f32[4,128]{1,0:T(4,128)S(1)}, f32[4,128]{1,0:T(4,128)S(1)}, u32[]{:S(2)}, u32[]{:S(2)}) collective-permute-start(f32[4,128]{1,0:T(4,128)S(1)} %add.12.s0), channel_id=1, source_target_pairs={{0,64},{64,0},{128,192},{192,128},{1,65},{65,1},{129,193},{193,129... | collective-permute-start | bytes 6152 | tf_op jit(solution)/shard_map/ppermute | solution.py:357
  36.9 2.6 %collective-permute-start.4 = (f32[4,128]{1,0:T(4,128)S(1)}, f32[4,128]{1,0:T(4,128)S(1)}, u32[]{:S(2)}, u32[]{:S(2)}) collective-permute-start(f32[4,128]{1,0:T(4,128)S(1)} %add.12.s0), channel_id=1, source_target_pairs={{0,128},{64,192},{128,0},{192,64},{1,129},{65,193},{129,1},{193,65... | collective-permute-start | bytes 6152 | tf_op jit(solution)/shard_map/ppermute | solution.py:357
  39.5 0.0 collective-permute-start.5
  39.5 0.0 copy-done.2
  39.5 0.0 copy-start.1
  39.5 1.2 %gather.1.cfar = f32[64,32]{1,0:T(8,128)S(1)} custom-call(s32[3]{0:T(128)S(1)} %pad_add_fusion.base, s32[4,8]{1,0:T(4,128)S(1)} %copy-done.3, f32[32,5,4,128]{3,2,1,0:T(4,128)S(1)} %all-to-all-done.own, f32[32,5,4,128]{3,2,1,0:T(4,128)S(1)} %collective-permute-done.2.other, f32[256,128]{1,0:T(8,128)S(1)} %bitcast.34), custom_call_target="tpu_custom_call" | custom-call | flops 10000000000 | bytes 10000000 | tf_op jit(solution)/shard_map/gather/pallas_call | solution.py:275
  40.7 0.0 collective-permute-done.3.s1
  40.7 0.1 collective-permute-done.4.s2
  40.8 2.3 %collective-permute-done.5.s3 = f32[4,128]{1,0:T(4,128)S(1)} collective-permute-done((f32[4,128]{1,0:T(4,128)S(1)}, f32[4,128]{1,0:T(4,128)S(1)}, u32[]{:S(2)}, u32[]{:S(2)}) %collective-permute-start.5) | collective-permute-done | bytes 2080 | tf_op jit(solution)/shard_map/ppermute | solution.py:357
  43.1 3.4 %down.1 = f32[16,4096]{1,0:T(8,128)} custom-call(s32[3]{0:T(128)S(1)} %pad_add_fusion.base, f32[4,128]{1,0:T(4,128)S(1)} %add.12.s0, f32[4,128]{1,0:T(4,128)S(1)} %collective-permute-done.3.s1, f32[4,128]{1,0:T(4,128)S(1)} %collective-permute-done.4.s2, f32[4,128]{1,0:T(4,128)S(1)} %collective-permute-done.5.s3, f32[64,32]{1,0:T(8,128)S(1)} %gather.1.cfar, ...), custom_call_target="tpu_custom_call" | custom-call | tf_op jit(solution)/shard_map/down/pallas_call | solution.py:331
  (8 shorter events, 0.1 us)
Async XLA Ops:
  1.9 17.4 %collective-permute-start = (f32[16,6144]{1,0:T(8,128)S(1)}, f32[16,6144]{1,0:T(8,128)S(1)}, u32[]{:S(2)}, u32[]{:S(2)}) collective-permute-start(f32[16,6144]{1,0:T(8,128)S(1)} %get-tuple-element.14.ext.xo.co), channel_id=1, source_target_pairs={{0,1},{1,0},{2,3},{3,2},{4,5},{5,4},{6,7},{7,6},{8,9},{9,8},{10,11... | collective-permute-start | bytes 1179656 | tf_op jit(solution)/shard_map/ppermute | solution.py:348
  5.2 14.0 %collective-permute-start.1 = (f32[16,6144]{1,0:T(8,128)S(1)}, f32[16,6144]{1,0:T(8,128)S(1)}, u32[]{:S(2)}, u32[]{:S(2)}) collective-permute-start(f32[16,6144]{1,0:T(8,128)S(1)} %get-tuple-element.14.ext.xo.co), channel_id=1, source_target_pairs={{1,2},{2,1},{3,4},{4,3},{5,6},{6,5},{7,8},{8,7},{9,10},{10,9},{11,... | collective-permute-start | bytes 1179656 | tf_op jit(solution)/shard_map/ppermute | solution.py:349
  8.8 23.8 %all-to-all-start = ((f32[32,5,4,128]{3,2,1,0:T(4,128)}), f32[32,5,4,128]{3,2,1,0:T(4,128)S(1)}, u32[]{:S(2)}, u32[]{:S(2)}) async-start(f32[32,5,4,128]{3,2,1,0:T(4,128)} %get-tuple-element.17), calls=%async_computation | async-start | bytes 655360 | tf_op jit(solution)/shard_map/all_to_all | solution.py:351
  19.3 20.2 %copy-start.2 = (f32[4,8,1024]{2,1,0:T(8,128)S(1)}, f32[4,8,1024]{2,1,0:T(8,128)}, u32[]{:S(2)}) copy-start(f32[4,8,1024]{2,1,0:T(8,128)} %param.21) | copy-start | bytes 393220
  19.3 20.2 %copy-start.3 = (s32[4,8]{1,0:T(4,128)S(1)}, s32[4,8]{1,0:T(4,128)}, u32[]{:S(2)}) copy-start(s32[4,8]{1,0:T(4,128)} %csrc.1) | copy-start | bytes 388
  32.6 2.9 %collective-permute-start.2 = (f32[32,5,4,128]{3,2,1,0:T(4,128)S(1)}, f32[32,5,4,128]{3,2,1,0:T(4,128)S(1)}, u32[]{:S(2)}, u32[]{:S(2)}) collective-permute-start(f32[32,5,4,128]{3,2,1,0:T(4,128)S(1)} %all-to-all-done.own), channel_id=1, source_target_pairs={{0,1},{1,0},{2,3},{3,2},{4,5},{5,4},{6,7},{7,6},{8,9},{9,8},{10,11... | collective-permute-start | bytes 983048 | tf_op jit(solution)/shard_map/ppermute | solution.py:355
  35.5 5.2 %collective-permute-start.3 = (f32[4,128]{1,0:T(4,128)S(1)}, f32[4,128]{1,0:T(4,128)S(1)}, u32[]{:S(2)}, u32[]{:S(2)}) collective-permute-start(f32[4,128]{1,0:T(4,128)S(1)} %add.12.s0), channel_id=1, source_target_pairs={{0,64},{64,0},{128,192},{192,128},{1,65},{65,1},{129,193},{193,129... | collective-permute-start | bytes 6152 | tf_op jit(solution)/shard_map/ppermute | solution.py:357
  36.9 3.9 %collective-permute-start.4 = (f32[4,128]{1,0:T(4,128)S(1)}, f32[4,128]{1,0:T(4,128)S(1)}, u32[]{:S(2)}, u32[]{:S(2)}) collective-permute-start(f32[4,128]{1,0:T(4,128)S(1)} %add.12.s0), channel_id=1, source_target_pairs={{0,128},{64,192},{128,0},{192,64},{1,129},{65,193},{129,1},{193,65... | collective-permute-start | bytes 6152 | tf_op jit(solution)/shard_map/ppermute | solution.py:357
  39.5 3.6 %collective-permute-start.5 = (f32[4,128]{1,0:T(4,128)S(1)}, f32[4,128]{1,0:T(4,128)S(1)}, u32[]{:S(2)}, u32[]{:S(2)}) collective-permute-start(f32[4,128]{1,0:T(4,128)S(1)} %add.12.s0), channel_id=1, source_target_pairs={{0,192},{64,128},{128,64},{192,0},{1,193},{65,129},{129,65},{193,1... | collective-permute-start | bytes 6152 | tf_op jit(solution)/shard_map/ppermute | solution.py:357
  39.5 3.6 %copy-start = (f32[64,2048]{1,0:T(8,128)S(1)}, f32[64,2048]{1,0:T(8,128)}, u32[]{:S(2)}) copy-start(f32[64,2048]{1,0:T(8,128)} %param.16) | copy-start | bytes 1572868
  39.5 3.6 %copy-start.1 = (f32[1,4,1024]{2,1,0:T(4,128)S(1)}, f32[1,4,1024]{2,1,0:T(4,128)}, u32[]{:S(2)}) copy-start(f32[1,4,1024]{2,1,0:T(4,128)} %param.23) | copy-start | bytes 49156
